TPU v7x, 32 devices: a whole 2x2x4 slice. The times are simulated.
32 devices in a mesh: freq: 4 (over y, core), tcol: 8 (over z, x).
Axes of the slice: x: 2, y: 2, z: 4, core: 2. Of those that a mesh axis runs over, the one named last changes fastest.
Arguments:
- data: bfloat16 [4, 2, 4096, 128], P('freq', None, 'tcol'), may hold values from -6 to 6
- left_factor: bfloat16 [4, 2, 4096, 256], P('freq', None, 'tcol'), may hold values from -0.25 to 0.25
- right_factor: bfloat16 [4, 2, 4096, 256], P('freq', None, 'tcol'), may hold values from -0.1875 to 0.1875
- ranks: int32 [4, 8, 8], P('freq'), may hold values from 1 to 32
- freq_index: int32 [4], P('freq'), may hold values from 0 to 229
Outputs:
- wavefield: float32 [4, 2, 4096, 128], P('freq', None, 'tcol')
- residual: float32 [4, 2, 4096, 128], P('freq', None, 'tcol')
Inputs may be any that keep to these rules, and one draw needn't show every extreme that they name: `ranks`: the rank of each tile; factor columns at or beyond it are not part of the kernel.
All inputs are finite; a program needn't handle non-finite values.
Results may differ from a plain program's by a relative error of at most 0.006.
Values may be sent and summed in bfloat16 or wider, within the bound.
No kernel may reach another device: no remote copies, remote signals or barrier semaphores. Data moves between devices by JAX's collectives and lax.ppermute only.
A program may use at most 64 MiB of HBM per device.

v0:
```python
import jax
import jax.numpy as jnp
from jax import lax
from jax.sharding import PartitionSpec as P

ITERS = 3


def conj_left(factor, field):
    first = jnp.einsum(
        "ftq,fts->fqs", factor[:, 0], field[:, 0], preferred_element_type=jnp.float32
    )
    second = jnp.einsum(
        "ftq,fts->fqs", factor[:, 1], field[:, 1], preferred_element_type=jnp.float32
    )
    third = jnp.einsum(
        "ftq,fts->fqs", factor[:, 0], field[:, 1], preferred_element_type=jnp.float32
    )
    fourth = jnp.einsum(
        "ftq,fts->fqs", factor[:, 1], field[:, 0], preferred_element_type=jnp.float32
    )
    return jnp.stack([first + second, third - fourth], 1)


def plain_right(factor, coeffs):
    first = jnp.einsum(
        "ftq,fqs->fts", factor[:, 0], coeffs[:, 0], preferred_element_type=jnp.float32
    )
    second = jnp.einsum(
        "ftq,fqs->fts", factor[:, 1], coeffs[:, 1], preferred_element_type=jnp.float32
    )
    third = jnp.einsum(
        "ftq,fqs->fts", factor[:, 0], coeffs[:, 1], preferred_element_type=jnp.float32
    )
    fourth = jnp.einsum(
        "ftq,fqs->fts", factor[:, 1], coeffs[:, 0], preferred_element_type=jnp.float32
    )
    return jnp.stack([first - second, third + fourth], 1)


def body(data, left_factor, right_factor, ranks, freq_index):
    ntile = lax.axis_size("tcol")
    here = lax.axis_index("tcol")
    rank_width = left_factor.shape[3] // ntile
    levels = jnp.arange(rank_width)[None, None, :]
    column_ranks = lax.dynamic_slice_in_dim(ranks, here, 1, 2)[:, :, 0]
    row_ranks = lax.dynamic_slice_in_dim(ranks, here, 1, 1)[:, 0, :]
    colmask = (levels < column_ranks[:, :, None]).astype(jnp.float32).reshape(ranks.shape[0], -1)
    rowmask = (levels < row_ranks[:, :, None]).astype(jnp.float32).reshape(ranks.shape[0], -1)
    damping = (0.1 + 0.9 * freq_index.astype(jnp.float32) / 229.0)[:, None, None, None]
    residual = data.astype(jnp.float32)
    wavefield = jnp.zeros_like(residual)
    direction = jnp.zeros_like(residual)
    image = jnp.zeros_like(residual)
    for step in range(ITERS):
        coeffs = conj_left(left_factor, residual.astype(jnp.bfloat16))
        coeffs = (coeffs * rowmask[:, None, :, None]).astype(jnp.bfloat16)
        arrived = lax.all_to_all(coeffs, "tcol", split_axis=2, concat_axis=2, tiled=True)
        gradient = plain_right(right_factor, arrived) - damping * wavefield
        forward_coeffs = conj_left(right_factor, gradient.astype(jnp.bfloat16))
        forward_coeffs = (forward_coeffs * colmask[:, None, :, None]).astype(jnp.bfloat16)
        forward_arrived = lax.all_to_all(
            forward_coeffs, "tcol", split_axis=2, concat_axis=2, tiled=True
        )
        moved = plain_right(left_factor, forward_arrived)
        partial_sums = jnp.stack(
            [
                jnp.sum(moved * moved + damping * gradient * gradient, axis=(0, 1, 2)),
                jnp.sum(moved * image + damping * gradient * direction, axis=(0, 1, 2)),
                jnp.sum(image * image + damping * direction * direction, axis=(0, 1, 2)),
                jnp.sum(moved * residual - damping * gradient * wavefield, axis=(0, 1, 2)),
                jnp.sum(image * residual - damping * direction * wavefield, axis=(0, 1, 2)),
            ]
        )
        totals = lax.psum(partial_sums, ("freq", "tcol"))
        a11, a12, a22, b1, b2 = (totals[0], totals[1], totals[2], totals[3], totals[4])
        if step == 0:
            alpha = b1 / (1.1 * a11)
            beta = jnp.zeros_like(alpha)
        else:
            first = 1.1 * a11
            second = 1.1 * a22
            determinant = first * second - a12 * a12
            alpha = (b1 * second - a12 * b2) / determinant
            beta = (first * b2 - a12 * b1) / determinant
        direction = alpha * gradient + beta * direction
        image = alpha * moved + beta * image
        wavefield = wavefield + direction
        residual = residual - image
    return (wavefield, residual)


def solution(mesh):
    in_specs = (
        P("freq", None, "tcol", None),
        P("freq", None, "tcol", None),
        P("freq", None, "tcol", None),
        P("freq", None, None),
        P("freq"),
    )
    out_specs = (P("freq", None, "tcol", None), P("freq", None, "tcol", None))
    return jax.shard_map(body, mesh=mesh, in_specs=in_specs, out_specs=out_specs, check_vma=False)
```

profile of v0, /device:TPU:0, one launch (start us, length us, event | category | flops | bytes accessed | tf_op | source)
XLA Modules:
  0.0 213.9 jit_solution(10456277240478988102)
XLA Ops:
  0.7 0.7 copy-done
  1.5 1.2 fusion.116
  2.8 1.2 fusion.118
  5.1 0.8 copy.35
  5.9 7.3 %all-to-all-start = ((bf16[1,2,256,128]{3,1,0,2:T(2,128)(2,1)}), bf16[1,2,256,128]{3,1,0,2:T(2,128)(2,1)S(1)}, u32[]{:S(2)}, u32[]{:S(2)}) async-start(bf16[1,2,256,128]{3,1,0,2:T(2,128)(2,1)} %copy.35), calls=%async_computation | async-start | bytes 262144 | tf_op jit(solution)/shard_map/all_to_all | solution.py:58
  13.8 6.7 %all-to-all-done = bf16[1,2,256,128]{3,1,0,2:T(2,128)(2,1)S(1)} async-done(((bf16[1,2,256,128]{3,1,0,2:T(2,128)(2,1)}), bf16[1,2,256,128]{3,1,0,2:T(2,128)(2,1)S(1)}, u32[]{:S(2)}, u32[]{:S(2)}) %all-to-all-start) | async-done | bytes 131104 | tf_op jit(solution)/shard_map/all_to_all | solution.py:58
  22.5 0.8 copy.38
  23.3 3.4 %all-to-all-start.1 = ((bf16[1,2,256,128]{3,1,0,2:T(2,128)(2,1)}), bf16[1,2,256,128]{3,1,0,2:T(2,128)(2,1)S(1)}, u32[]{:S(2)}, u32[]{:S(2)}) async-start(bf16[1,2,256,128]{3,1,0,2:T(2,128)(2,1)} %copy.38), calls=%async_computation.1 | async-start | bytes 262144 | tf_op jit(solution)/shard_map/all_to_all | solution.py:62
  26.8 7.1 %all-to-all-done.1 = bf16[1,2,256,128]{3,1,0,2:T(2,128)(2,1)S(1)} async-done(((bf16[1,2,256,128]{3,1,0,2:T(2,128)(2,1)}), bf16[1,2,256,128]{3,1,0,2:T(2,128)(2,1)S(1)}, u32[]{:S(2)}, u32[]{:S(2)}) %all-to-all-start.1) | async-done | bytes 131104 | tf_op jit(solution)/shard_map/all_to_all | solution.py:62
  35.5 38.5 %psum.21 = f32[5,128]{1,0:T(8,128)S(1)} all-reduce(f32[5,128]{1,0:T(8,128)S(1)} %stack.179), channel_id=1, replica_groups=mesh['freq'=4,'tcol'=8] {'freq','tcol'}, use_global_device_ids=true, to_apply=%region_4.0 | all-reduce | flops 640 | bytes 5120 | tf_op jit(solution)/shard_map/psum | solution.py:75
  75.5 11.7 %all_to_all.30 = bf16[1,2,256,128]{3,1,0,2:T(2,128)(2,1)S(1)} all-to-all(bf16[1,2,256,128]{3,1,0,2:T(2,128)(2,1)S(1)} %copy.46), channel_id=1, replica_groups=mesh['freq'=4,'tcol'=8] {'tcol'}, dimensions={2} | all-to-all | bytes 262144 | tf_op jit(solution)/shard_map/all_to_all | solution.py:58
  89.5 9.7 %all_to_all.31 = bf16[1,2,256,128]{3,1,0,2:T(2,128)(2,1)S(1)} all-to-all(bf16[1,2,256,128]{3,1,0,2:T(2,128)(2,1)S(1)} %copy.49), channel_id=1, replica_groups=mesh['freq'=4,'tcol'=8] {'tcol'}, dimensions={2} | all-to-all | bytes 262144 | tf_op jit(solution)/shard_map/all_to_all | solution.py:62
  101.0 0.6 subtract_reduce_fusion
  101.7 38.3 %psum.22 = f32[5,128]{1,0:T(8,128)S(1)} all-reduce(f32[5,128]{1,0:T(8,128)S(1)} %stack.197), channel_id=1, replica_groups=mesh['freq'=4,'tcol'=8] {'freq','tcol'}, use_global_device_ids=true, to_apply=%region_10.0 | all-reduce | flops 640 | bytes 5120 | tf_op jit(solution)/shard_map/psum | solution.py:75
  139.9 2.1 fusion.186
  143.3 11.7 %all_to_all.32 = bf16[1,2,256,128]{3,1,0,2:T(2,128)(2,1)S(1)} all-to-all(bf16[1,2,256,128]{3,1,0,2:T(2,128)(2,1)S(1)} %copy.56), channel_id=1, replica_groups=mesh['freq'=4,'tcol'=8] {'tcol'}, dimensions={2} | all-to-all | bytes 262144 | tf_op jit(solution)/shard_map/all_to_all | solution.py:58
  156.2 1.1 fusion.185
  158.2 9.7 %all_to_all.33 = bf16[1,2,256,128]{3,1,0,2:T(2,128)(2,1)S(1)} all-to-all(bf16[1,2,256,128]{3,1,0,2:T(2,128)(2,1)S(1)} %copy.59), channel_id=1, replica_groups=mesh['freq'=4,'tcol'=8] {'tcol'}, dimensions={2} | all-to-all | bytes 262144 | tf_op jit(solution)/shard_map/all_to_all | solution.py:62
  169.1 0.5 copy-done.4
  169.9 0.7 fusion.37
  170.7 38.3 %psum.23 = f32[5,128]{1,0:T(8,128)S(1)} all-reduce(f32[5,128]{1,0:T(8,128)S(1)} %stack.215), channel_id=1, replica_groups=mesh['freq'=4,'tcol'=8] {'freq','tcol'}, use_global_device_ids=true, to_apply=%region_16.0 | all-reduce | flops 640 | bytes 5120 | tf_op jit(solution)/shard_map/psum | solution.py:75
  209.0 2.0 add_subtract_fusion
  210.9 2.0 copy.63
  213.0 1.0 copy.62
  (99 shorter events, 15.0 us)
Async XLA Ops:
  0.6 0.7 copy-start
  0.6 2.1 copy-start.2
  2.8 1.6 copy-start.8
  5.1 15.6 %copy-start.1 = (bf16[1,2,512,256]{3,2,1,0:T(8,128)(2,1)S(1)}, bf16[1,2,512,256]{3,2,1,0:T(8,128)(2,1)}, u32[]{:S(2)}) copy-start(bf16[1,2,512,256]{3,2,1,0:T(8,128)(2,1)} %param.7) | copy-start | bytes 1572868
  5.9 14.6 %all-to-all-start = ((bf16[1,2,256,128]{3,1,0,2:T(2,128)(2,1)}), bf16[1,2,256,128]{3,1,0,2:T(2,128)(2,1)S(1)}, u32[]{:S(2)}, u32[]{:S(2)}) async-start(bf16[1,2,256,128]{3,1,0,2:T(2,128)(2,1)} %copy.35), calls=%async_computation | async-start | bytes 262144 | tf_op jit(solution)/shard_map/all_to_all | solution.py:58
  23.3 10.7 %all-to-all-start.1 = ((bf16[1,2,256,128]{3,1,0,2:T(2,128)(2,1)}), bf16[1,2,256,128]{3,1,0,2:T(2,128)(2,1)S(1)}, u32[]{:S(2)}, u32[]{:S(2)}) async-start(bf16[1,2,256,128]{3,1,0,2:T(2,128)(2,1)} %copy.38), calls=%async_computation.1 | async-start | bytes 262144 | tf_op jit(solution)/shard_map/all_to_all | solution.py:62
  100.1 0.7 copy-start.5
  100.3 0.7 copy-start.6
  168.6 1.0 copy-start.4
  168.9 1.1 copy-start.3
  169.1 1.5 copy-start.7
where the time goes:
time: 215 us; the launch traced here: 214 us
  blocking collectives  158 us (73%)
  waiting for transfers between devices  13.8 us (6%)
  matrix products  13 us (6%)
  starting transfers between devices  10.7 us (5%)
  local copies, waits for them, and re-layouts  8.86 us (4%)
  other arithmetic  7.88 us (4%)
    psum x3, blocking collectives, body(): totals = lax.psum(partial_sums, ('freq', 'tcol'))  115 us
    all_to_all x2, blocking collectives, body(): lax.all_to_all(coeffs, 'tcol', split_axis=2, concat_axis=2, tiled=True)  23.4 us
    all_to_all x2, blocking collectives, body(): lax.all_to_all(forward_coeffs, 'tcol', split_axis=2, concat_axis=2, tiled...  19.5 us
    all_to_all x1, starting transfers between devices, body(): lax.all_to_all(coeffs, 'tcol', split_axis=2, concat_axis=2, tiled=True)  7.28 us
    all_to_all x1, waiting for transfers between devices, body(): lax.all_to_all(forward_coeffs, 'tcol', split_axis=2, concat_axis=2, tiled...  7.12 us
    all_to_all x1, waiting for transfers between devices, body(): lax.all_to_all(coeffs, 'tcol', split_axis=2, concat_axis=2, tiled=True)  6.69 us
    unnamed x21, local copies, waits for them, and re-layouts  5.08 us
  transfers between devices with their start and end apart: 2, of which 2 were waited for; matrix products, arithmetic and copies ran while one was open for 0% of the time, Pallas kernels for 0%

commit v1 on v0

v1 whole, which is shorter than its diff:
```python
import functools

import jax
import jax.numpy as jnp
from jax import lax
from jax.experimental import pallas as pl
from jax.experimental.pallas import tpu as pltpu
from jax.sharding import PartitionSpec as P


RIDE = 16
ROWS = 16
VMEM = pl.BlockSpec(memory_space=pltpu.VMEM)
SMEM = pl.BlockSpec(memory_space=pltpu.SMEM)
F32 = jnp.float32
BF16 = jnp.bfloat16


def dot(a, b):
    return jnp.dot(a, b, preferred_element_type=F32)


def dot_t(a, b):
    return lax.dot_general(a, b, (((0,), (0,)), ((), ())), preferred_element_type=F32)


def side(real, imag):
    return jnp.concatenate([real, imag], axis=1)


def split(value):
    high = value.astype(BF16)
    return high, (value - high.astype(F32)).astype(BF16)


def unpack(ref, rank):
    n = ref.shape[0]
    real = ref[:, 0:rank, :].reshape(n * rank, ref.shape[2])
    imag = ref[:, rank : 2 * rank, :].reshape(n * rank, ref.shape[2])
    return real, imag


def send(out_ref, value, limits, rank):
    s = out_ref.shape[2]
    level = lax.broadcasted_iota(jnp.int32, (rank, s), 0)
    for p in range(out_ref.shape[0]):
        keep = level < limits[p]
        rows = value[p * rank : (p + 1) * rank]
        out_ref[p, 0:rank, :] = jnp.where(keep, rows[:, :s], 0.0).astype(BF16)
        out_ref[p, rank : 2 * rank, :] = jnp.where(keep, rows[:, s:], 0.0).astype(BF16)


def ride(out_ref, first, second, rank):
    s = out_ref.shape[2]
    row = lax.broadcasted_iota(jnp.int32, (RIDE, s), 0)
    block = jnp.where(row == 0, first, second).astype(BF16)
    for p in range(out_ref.shape[0]):
        out_ref[p, 2 * rank : 2 * rank + RIDE, :] = block


def ridden(ref, rank):
    total = ref[0, 2 * rank : 2 * rank + RIDE, :].astype(F32)
    for p in range(1, ref.shape[0]):
        total = total + ref[p, 2 * rank : 2 * rank + RIDE, :].astype(F32)
    return total[0:1], total[1:2]


def inner(a, b):
    both = jnp.sum(a * b, axis=0, keepdims=True)
    s = both.shape[1] // 2
    return both[:, :s] + both[:, s:]


def twice(row):
    return jnp.concatenate([row, row], axis=1)


def ratio(top, bottom):
    safe = bottom > 0
    return jnp.where(safe, top / jnp.where(safe, bottom, 1.0), 0.0)


def apply_gram(hi_ref, lo_ref, real, imag):
    vector = jnp.concatenate([side(real, imag), side(-imag, real)], axis=0)
    return dot(hi_ref[...], vector) + dot(lo_ref[...], vector)


def row_limits(ranks_ref, here, n):
    return [ranks_ref[here, p] for p in range(n)]


def column_limits(ranks_ref, here, n):
    return [ranks_ref[p, here] for p in range(n)]


def start_kernel(rank, here_ref, ranks_ref, data_ref, factor_ref, back_ref, out_ref):
    n = out_ref.shape[0]
    real, imag = data_ref[0], data_ref[1]
    back = dot_t(factor_ref[0], side(real, imag)) + dot_t(factor_ref[1], side(imag, -real))
    back_ref[...] = back
    send(out_ref, back, row_limits(ranks_ref, here_ref[0], n), rank)


def gram_kernel(factor_ref, hi_ref, lo_ref):
    real, imag = factor_ref[0], factor_ref[1]
    width = real.shape[1]
    high, low = split(dot_t(real, real) + dot_t(imag, imag))
    hi_ref[:, :width] = high
    lo_ref[:, :width] = low
    high, low = split(dot_t(real, imag) - dot_t(imag, real))
    hi_ref[:, width:] = high
    lo_ref[:, width:] = low


def column0(rank, here_ref, ranks_ref, b0_ref, hi_ref, lo_ref, g0_ref, sums_ref, out_ref):
    n = out_ref.shape[0]
    real, imag = unpack(b0_ref, rank)
    g0 = apply_gram(hi_ref, lo_ref, real, imag)
    g0_ref[...] = g0
    m00 = inner(side(real, imag).astype(F32), g0)
    sums_ref[0:1, :] = m00
    send(out_ref, g0, column_limits(ranks_ref, here_ref[0], n), rank)
    ride(out_ref, m00, m00, rank)


def row0(rank, here_ref, ranks_ref, c0_ref, hi_ref, lo_ref, back_ref, sums_ref, out_ref):
    n = out_ref.shape[0]
    real, imag = unpack(c0_ref, rank)
    next0 = apply_gram(hi_ref, lo_ref, real, imag)
    c0 = side(real, imag).astype(F32)
    n00 = inner(c0, next0)
    sums_ref[0:1, :] = n00
    sums_ref[1:2, :] = inner(back_ref[...], c0)
    sums_ref[2:3, :] = ridden(c0_ref, rank)[0]
    send(out_ref, next0, row_limits(ranks_ref, here_ref[0], n), rank)
    ride(out_ref, n00, n00, rank)


def column1(
    rank, here_ref, ranks_ref, b1_ref, b0_ref, hi_ref, lo_ref, g0_ref, known_ref,
    g1_ref, b1s_ref, sums_ref, out_ref
):
    n = out_ref.shape[0]
    real, imag = unpack(b1_ref, rank)
    theta0 = ratio(ridden(b1_ref, rank)[0], known_ref[2:3, :])
    wide = twice(theta0)
    g1 = apply_gram(hi_ref, lo_ref, real, imag) - wide * g0_ref[...]
    b0 = side(*unpack(b0_ref, rank)).astype(F32)
    b1 = side(real, imag).astype(F32) - wide * b0
    g1_ref[...] = g1
    b1s_ref[...] = b1
    m11 = inner(b1, g1)
    sums_ref[0:1, :] = m11
    sums_ref[1:2, :] = inner(b0, g1)
    sums_ref[2:3, :] = theta0
    send(out_ref, g1, column_limits(ranks_ref, here_ref[0], n), rank)
    ride(out_ref, m11, m11, rank)


def row1(
    rank, here_ref, ranks_ref, c1_ref, c0_ref, hi_ref, lo_ref, back_ref, sums_ref, out_ref
):
    n = out_ref.shape[0]
    real, imag = unpack(c1_ref, rank)
    next1 = apply_gram(hi_ref, lo_ref, real, imag)
    c1 = side(real, imag).astype(F32)
    c0 = side(*unpack(c0_ref, rank)).astype(F32)
    n11 = inner(c1, next1)
    n01 = inner(c0, next1)
    sums_ref[0:1, :] = n11
    sums_ref[1:2, :] = n01
    sums_ref[2:3, :] = inner(back_ref[...], c1)
    sums_ref[3:4, :] = ridden(c1_ref, rank)[0]
    send(out_ref, next1, row_limits(ranks_ref, here_ref[0], n), rank)
    ride(out_ref, n11, n01, rank)


def column2(
    rank, here_ref, ranks_ref, b2_ref, b0_ref, b1s_ref, hi_ref, lo_ref, g0_ref, g1_ref,
    known0_ref, known1_ref, sums_ref, out_ref
):
    n = out_ref.shape[0]
    real, imag = unpack(b2_ref, rank)
    n11, n01 = ridden(b2_ref, rank)
    theta1 = ratio(n11, known1_ref[3:4, :])
    phi = ratio(n01, known0_ref[2:3, :])
    wide1, wide0 = twice(theta1), twice(phi)
    b0 = side(*unpack(b0_ref, rank)).astype(F32)
    g2 = apply_gram(hi_ref, lo_ref, real, imag) - wide1 * g1_ref[...] - wide0 * g0_ref[...]
    b2 = side(real, imag).astype(F32) - wide1 * b1s_ref[...] - wide0 * b0
    sums_ref[0:1, :] = inner(b2, g2)
    sums_ref[1:2, :] = inner(b0, g2)
    sums_ref[2:3, :] = inner(b1s_ref[...], g2)
    sums_ref[3:4, :] = theta1
    sums_ref[4:5, :] = phi
    send(out_ref, g2, column_limits(ranks_ref, here_ref[0], n), rank)


def row2(
    rank, freq_ref, c2_ref, c0_ref, c1_ref, hi_ref, lo_ref, back_ref,
    m0_ref, n0_ref, m1_ref, n1_ref, m2_ref, out_ref
):
    real, imag = unpack(c2_ref, rank)
    next2 = apply_gram(hi_ref, lo_ref, real, imag)
    c2 = side(real, imag).astype(F32)
    c0 = side(*unpack(c0_ref, rank)).astype(F32)
    c1 = side(*unpack(c1_ref, rank)).astype(F32)
    damping = 0.1 + 0.9 * freq_ref[0].astype(F32) / 229.0
    rows = [
        n0_ref[0:1, :] + damping * m0_ref[0:1, :],
        n1_ref[1:2, :] + damping * m1_ref[1:2, :],
        inner(c0, next2) + damping * m2_ref[1:2, :],
        n1_ref[0:1, :] + damping * m1_ref[0:1, :],
        inner(c1, next2) + damping * m2_ref[2:3, :],
        inner(c2, next2) + damping * m2_ref[0:1, :],
        n0_ref[1:2, :],
        n1_ref[2:3, :],
        inner(back_ref[...], c2),
        m1_ref[2:3, :],
        m2_ref[3:4, :],
        m2_ref[4:5, :],
        jnp.full_like(m0_ref[0:1, :], damping),
    ]
    rows = rows + [jnp.zeros_like(rows[0])] * (ROWS - len(rows))
    block = jnp.concatenate(rows, axis=0)
    for p in range(out_ref.shape[0]):
        out_ref[p] = block


def forms(h, u, g, p, position, size):
    def times(v):
        return [sum(h[a][b] * v[b] for b in range(size)) for a in range(size)]

    def along(a, b):
        return jnp.sum(sum(x * y for x, y in zip(a, b)), axis=0, keepdims=True)

    hg, hp, hx = times(g), times(p), times(position)
    rest = [u[a] - hx[a] for a in range(size)]
    return along(g, hg), along(p, hg), along(p, hp), along(g, rest), along(p, rest)


def finish_kernel(
    rank, nfreq, mine_ref, recv_ref, data_ref, left_ref, right_ref,
    b0_ref, b1_ref, b2_ref, c0_ref, c1_ref, c2_ref, wave_ref, res_ref, table_ref, mix_ref
):
    ntile = recv_ref.shape[0] // nfreq
    for f in range(nfreq):
        total = recv_ref[f * ntile]
        for t in range(1, ntile):
            total = total + recv_ref[f * ntile + t]
        table_ref[0, :, f, :] = total
        table_ref[1, :, f, :] = recv_ref[f * ntile]
    h = [[None] * 3 for _ in range(3)]
    for place, (a, b) in enumerate([(0, 0), (0, 1), (0, 2), (1, 1), (1, 2), (2, 2)]):
        h[a][b] = h[b][a] = table_ref[0, place]
    u = [table_ref[0, 6 + a] for a in range(3)]
    theta0, theta1, phi, damping = [table_ref[1, 9 + a] for a in range(4)]
    one = jnp.ones_like(theta0)
    a11 = jnp.sum(h[0][0], axis=0, keepdims=True)
    b1 = jnp.sum(u[0], axis=0, keepdims=True)
    alpha = b1 / (1.1 * a11)
    p = [alpha * one]
    x = [alpha * one]
    for size in (2, 3):
        zero = jnp.zeros_like(one)
        x = x + [zero]
        p = p + [zero]
        if size == 2:
            g = [one - (theta0 + damping) * x[0], -x[0]]
        else:
            g = [
                one - (theta0 + damping) * x[0] - phi * x[1],
                -x[0] - (theta1 + damping) * x[1],
                -x[1],
            ]
        a11, a12, a22, b1, b2 = forms(h, u, g, p, x, size)
        first, second = 1.1 * a11, 1.1 * a22
        determinant = first * second - a12 * a12
        alpha = (b1 * second - a12 * b2) / determinant
        beta = (first * b2 - a12 * b1) / determinant
        p = [alpha * g[a] + beta * p[a] for a in range(size)]
        x = [x[a] + p[a] for a in range(size)]
    mix_ref[0] = x[0] - theta0 * x[1] + (theta0 * theta1 - phi) * x[2]
    mix_ref[1] = x[1] - theta1 * x[2]
    mix_ref[2] = x[2]
    mix_ref[3] = x[0]
    mix_ref[4] = x[1]
    mix_ref[5] = x[2]
    row = pl.ds(mine_ref[0], 1)

    def combine(refs, offset):
        total = None
        for k, ref in enumerate(refs):
            scale = mix_ref[offset + k, row, :]
            real, imag = unpack(ref, rank)
            term = (scale * real.astype(F32), scale * imag.astype(F32))
            total = term if total is None else (total[0] + term[0], total[1] + term[1])
        return total

    def plain(factor_ref, real, imag):
        (rh, rl), (ih, il) = split(real), split(imag)
        first, second = factor_ref[0], factor_ref[1]
        return (
            dot(first, side(rh, ih)) + dot(second, side(-ih, rh))
            + dot(first, side(rl, il)) + dot(second, side(-il, rl))
        )

    s = wave_ref.shape[2]
    wave = plain(right_ref, *combine([b0_ref, b1_ref, b2_ref], 0))
    wave_ref[0] = wave[:, :s]
    wave_ref[1] = wave[:, s:]
    image = plain(left_ref, *combine([c0_ref, c1_ref, c2_ref], 3))
    res_ref[0] = data_ref[0].astype(F32) - image[:, :s]
    res_ref[1] = data_ref[1].astype(F32) - image[:, s:]


def body(data, left_factor, right_factor, ranks, freq_index):
    ntile = lax.axis_size("tcol")
    nfreq = lax.axis_size("freq")
    here = lax.axis_index("tcol").reshape(1)
    mine = lax.axis_index("freq").reshape(1)
    data, left, right, ranks = data[0], left_factor[0], right_factor[0], ranks[0]
    width = left.shape[2]
    rank = width // ntile
    s = data.shape[2]
    field = jax.ShapeDtypeStruct((width, 2 * s), F32)
    sums = jax.ShapeDtypeStruct((8, s), F32)
    bare = jax.ShapeDtypeStruct((ntile, 2 * rank, s), BF16)
    message = jax.ShapeDtypeStruct((ntile, 2 * rank + RIDE, s), BF16)
    gram = jax.ShapeDtypeStruct((width, 2 * width), BF16)

    def call(kernel, scalars, arrays, outs, scratch=(), *static):
        return pl.pallas_call(
            functools.partial(kernel, *static) if static else kernel,
            out_shape=outs,
            in_specs=[SMEM] * len(scalars) + [VMEM] * len(arrays),
            out_specs=[VMEM] * len(outs),
            scratch_shapes=scratch,
        )(*scalars, *arrays)

    def exchange(value):
        return lax.all_to_all(value, "tcol", 0, 0, tiled=True)

    where = (here, ranks)
    back, out = call(start_kernel, where, (data, left), (field, bare), (), rank)
    b0 = exchange(out)
    vhi, vlo = call(gram_kernel, (), (right,), (gram, gram))
    uhi, ulo = call(gram_kernel, (), (left,), (gram, gram))
    g0, m0, out = call(column0, where, (b0, vhi, vlo), (field, sums, message), (), rank)
    c0 = exchange(out)
    n0, out = call(row0, where, (c0, uhi, ulo, back), (sums, message), (), rank)
    b1 = exchange(out)
    g1, b1s, m1, out = call(
        column1, where, (b1, b0, vhi, vlo, g0, n0), (field, field, sums, message), (), rank
    )
    c1 = exchange(out)
    n1, out = call(row1, where, (c1, c0, uhi, ulo, back), (sums, message), (), rank)
    b2 = exchange(out)
    m2, out = call(
        column2, where, (b2, b0, b1s, vhi, vlo, g0, g1, n0, n1), (sums, bare), (), rank
    )
    c2 = exchange(out)
    (out,) = call(
        row2, (freq_index,), (c2, c0, c1, uhi, ulo, back, m0, n0, m1, n1, m2),
        (jax.ShapeDtypeStruct((nfreq * ntile, ROWS, s), F32),), (), rank
    )
    everyone = lax.all_to_all(out, ("freq", "tcol"), 0, 0, tiled=True)
    shape = jax.ShapeDtypeStruct(data.shape, F32)
    wave, res = call(
        finish_kernel, (mine,), (everyone, data, left, right, b0, b1, b2, c0, c1, c2),
        (shape, shape),
        (pltpu.VMEM((2, ROWS, nfreq, s), F32), pltpu.VMEM((6, nfreq, s), F32)), rank, nfreq
    )
    return wave[None], res[None]


def solution(mesh):
    in_specs = (
        P("freq", None, "tcol", None),
        P("freq", None, "tcol", None),
        P("freq", None, "tcol", None),
        P("freq", None, None),
        P("freq"),
    )
    out_specs = (P("freq", None, "tcol", None), P("freq", None, "tcol", None))
    return jax.shard_map(body, mesh=mesh, in_specs=in_specs, out_specs=out_specs, check_vma=False)
```

time: 215 us -> 108 us (0.50)
  blocking collectives: 158 us -> 34.7 us
  Pallas kernels: 0 us -> 24.2 us
  waiting for transfers between devices: 13.8 us -> 27.3 us
  matrix products: 13 us -> 0 us
  other arithmetic: 7.88 us -> 0 us
  local copies, waits for them, and re-layouts: 8.86 us -> 2.68 us
  starting transfers between devices: 10.7 us -> 16.6 us
    psum x3 -> x0, blocking collectives: 115 us -> none  [body(): totals = lax.psum(partial_sums, ('freq', 'tcol'))]
    pallas_call x0 -> x10, Pallas kernels: none -> 24.2 us  [call(): pl.pallas_call(functools.partial(kernel, *static) if static else kernel,...]
    all_to_all x2 -> x4, waiting for transfers between devices: 13.8 us -> 27.3 us  [the longest x3 16.9 us: exchange(): return lax.all_to_all(value, 'tcol', 0, 0, tiled=True)]
    dot_general x48 -> x0, matrix products: 13 us -> none  [the longest x6 2.36 us: conj_left(): jnp.einsum('ftq,fts->fqs', factor[:, 0], field[:, 1], preferred_element_t...]
    all_to_all x4 -> x3, blocking collectives: 42.8 us -> 34.7 us  [exchange(): return lax.all_to_all(value, 'tcol', 0, 0, tiled=True)]
    all_to_all x2 -> x4, starting transfers between devices: 10.7 us -> 16.6 us  [the longest x3 14 us: exchange(): return lax.all_to_all(value, 'tcol', 0, 0, tiled=True)]
    convert_element_type x12 -> x0, other arithmetic: 3.88 us -> none  [the longest x2 2.19 us: body(): coeffs = conj_left(left_factor, residual.astype(jnp.bfloat16))]
    unnamed x21 -> x8, local copies, waits for them, and re-layouts: 5.08 us -> 2.68 us
  transfers between devices with their start and end apart: 2 -> 4, of which waited for: 2 -> 4; matrix products, arithmetic and copies ran while one was open for 0% -> 0% of each run, Pallas kernels for 0% -> 4%
where the time goes in v1:
time: 108 us; the launch traced here: 107 us
  blocking collectives  34.7 us (32%)
  waiting for transfers between devices  27.3 us (25%)
  Pallas kernels  24.2 us (22%)
  starting transfers between devices  16.6 us (15%)
  local copies, waits for them, and re-layouts  2.68 us (2%)
  between operations  1.32 us (1%)
    all_to_all x3, blocking collectives, exchange(): return lax.all_to_all(value, 'tcol', 0, 0, tiled=True)  34.7 us
    pallas_call x10, Pallas kernels, call(): pl.pallas_call(functools.partial(kernel, *static) if static else kernel,...  24.2 us
    all_to_all x3, waiting for transfers between devices, exchange(): return lax.all_to_all(value, 'tcol', 0, 0, tiled=True)  16.9 us
    all_to_all x3, starting transfers between devices, exchange(): return lax.all_to_all(value, 'tcol', 0, 0, tiled=True)  14 us
    all_to_all x1, waiting for transfers between devices, body(): everyone = lax.all_to_all(out, ('freq', 'tcol'), 0, 0, tiled=True)  10.4 us
    unnamed x8, local copies, waits for them, and re-layouts  2.68 us
    all_to_all x1, starting transfers between devices, body(): everyone = lax.all_to_all(out, ('freq', 'tcol'), 0, 0, tiled=True)  2.59 us
  transfers between devices with their start and end apart: 4, of which 4 were waited for; matrix products, arithmetic and copies ran while one was open for 0% of the time, Pallas kernels for 4%

profile of v1, /device:TPU:0, one launch (start us, length us, event | category | flops | bytes accessed | tf_op | source)
XLA Modules:
  0.0 106.8 jit_solution(10039801878379135826)
XLA Ops:
  0.6 2.2 %shard_map.68 = (f32[256,256]{1,0:T(8,128)}, bf16[8,64,128]{2,1,0:T(8,128)(2,1)}) custom-call(s32[1]{0:T(128)} %bitcast.1.here_ref, s32[8,8]{1,0:T(8,128)} %bitcast.15, bf16[2,512,128]{2,1,0:T(8,128)(2,1)} %bitcast.13, bf16[2,512,256]{2,1,0:T(8,128)(2,1)} %bitcast.8), custom_call_target="tpu_custom_call" | custom-call | tf_op jit(solution)/shard_map/pallas_call | solution.py:333
  2.9 7.3 %all-to-all-start = ((bf16[8,64,128]{2,1,0:T(8,128)(2,1)}), bf16[8,64,128]{2,1,0:T(8,128)(2,1)S(1)}, u32[]{:S(2)}, u32[]{:S(2)}) async-start(bf16[8,64,128]{2,1,0:T(8,128)(2,1)} %get-tuple-element.23), calls=%async_computation | async-start | bytes 262144 | tf_op jit(solution)/shard_map/all_to_all | solution.py:342
  10.1 2.3 %shard_map.69 = (bf16[256,512]{1,0:T(8,128)(2,1)}, bf16[256,512]{1,0:T(8,128)(2,1)}) custom-call(bf16[2,512,256]{2,1,0:T(8,128)(2,1)} %bitcast.11), custom_call_target="tpu_custom_call" | custom-call | tf_op jit(solution)/shard_map/pallas_call | solution.py:333
  12.4 5.0 %all-to-all-done.b0_ref = bf16[8,64,128]{2,1,0:T(8,128)(2,1)S(1)} async-done(((bf16[8,64,128]{2,1,0:T(8,128)(2,1)}), bf16[8,64,128]{2,1,0:T(8,128)(2,1)S(1)}, u32[]{:S(2)}, u32[]{:S(2)}) %all-to-all-start) | async-done | bytes 131104 | tf_op jit(solution)/shard_map/all_to_all | solution.py:342
  17.5 0.7 copy-done.1
  18.1 2.2 %shard_map.70 = (f32[256,256]{1,0:T(8,128)}, f32[8,128]{1,0:T(8,128)}, bf16[8,80,128]{2,1,0:T(8,128)(2,1)}) custom-call(s32[1]{0:T(128)} %bitcast.1.here_ref, s32[8,8]{1,0:T(8,128)} %bitcast.16, bf16[8,64,128]{2,1,0:T(8,128)(2,1)} %copy-done.1, bf16[256,512]{1,0:T(8,128)(2,1)} %get-tuple-element.24.hi_ref, bf16[256,512]{1,0:T(8,128)(2,1)} %get-tuple-element.25.lo_ref), custom_call_target="tpu_custom_call" | custom-call | tf_op jit(solution)/shard_map/pallas_call | solution.py:333
  20.3 3.4 %all-to-all-start.1 = ((bf16[8,80,128]{2,1,0:T(8,128)(2,1)}), bf16[8,80,128]{2,1,0:T(8,128)(2,1)S(1)}, u32[]{:S(2)}, u32[]{:S(2)}) async-start(bf16[8,80,128]{2,1,0:T(8,128)(2,1)} %get-tuple-element.26), calls=%async_computation.1 | async-start | bytes 327680 | tf_op jit(solution)/shard_map/all_to_all | solution.py:342
  23.7 2.3 %shard_map.71 = (bf16[256,512]{1,0:T(8,128)(2,1)}, bf16[256,512]{1,0:T(8,128)(2,1)}) custom-call(bf16[2,512,256]{2,1,0:T(8,128)(2,1)} %bitcast.9), custom_call_target="tpu_custom_call" | custom-call | tf_op jit(solution)/shard_map/pallas_call | solution.py:333
  26.0 5.2 %all-to-all-done.1.c0_ref = bf16[8,80,128]{2,1,0:T(8,128)(2,1)S(1)} async-done(((bf16[8,80,128]{2,1,0:T(8,128)(2,1)}), bf16[8,80,128]{2,1,0:T(8,128)(2,1)S(1)}, u32[]{:S(2)}, u32[]{:S(2)}) %all-to-all-start.1) | async-done | bytes 163872 | tf_op jit(solution)/shard_map/all_to_all | solution.py:342
  31.2 0.7 copy-done
  31.9 2.2 %shard_map.72 = (f32[8,128]{1,0:T(8,128)}, bf16[8,80,128]{2,1,0:T(8,128)(2,1)}) custom-call(s32[1]{0:T(128)} %bitcast.1.here_ref, s32[8,8]{1,0:T(8,128)} %bitcast.17, bf16[8,80,128]{2,1,0:T(8,128)(2,1)} %copy-done, bf16[256,512]{1,0:T(8,128)(2,1)} %get-tuple-element.27.hi_ref, bf16[256,512]{1,0:T(8,128)(2,1)} %get-tuple-element.28.lo_ref, ...), custom_call_target="tpu_custom_call" | custom-call | tf_op jit(solution)/shard_map/pallas_call | solution.py:333
  34.1 11.6 %all_to_all.35.b1_ref = bf16[8,80,128]{2,1,0:T(8,128)(2,1)} all-to-all(bf16[8,80,128]{2,1,0:T(8,128)(2,1)} %get-tuple-element.30), channel_id=1, replica_groups=mesh['freq'=4,'tcol'=8] {'tcol'}, dimensions={0} | all-to-all | bytes 327680 | tf_op jit(solution)/shard_map/all_to_all | solution.py:342
  45.7 2.4 %shard_map.73 = (f32[256,256]{1,0:T(8,128)}, f32[256,256]{1,0:T(8,128)}, f32[8,128]{1,0:T(8,128)}, bf16[8,80,128]{2,1,0:T(8,128)(2,1)}) custom-call(s32[1]{0:T(128)} %bitcast.1.here_ref, s32[8,8]{1,0:T(8,128)} %bitcast.18, bf16[8,80,128]{2,1,0:T(8,128)(2,1)} %all_to_all.35.b1_ref, bf16[8,64,128]{2,1,0:T(8,128)(2,1)} %copy-done.1, ...), custom_call_target="tpu_custom_call" | custom-call | tf_op jit(solution)/shard_map/pallas_call | solution.py:333
  48.0 11.6 %all_to_all.36.c1_ref = bf16[8,80,128]{2,1,0:T(8,128)(2,1)} all-to-all(bf16[8,80,128]{2,1,0:T(8,128)(2,1)} %get-tuple-element.33), channel_id=1, replica_groups=mesh['freq'=4,'tcol'=8] {'tcol'}, dimensions={0} | all-to-all | bytes 327680 | tf_op jit(solution)/shard_map/all_to_all | solution.py:342
  59.6 2.3 %shard_map.74 = (f32[8,128]{1,0:T(8,128)}, bf16[8,80,128]{2,1,0:T(8,128)(2,1)}) custom-call(s32[1]{0:T(128)} %bitcast.1.here_ref, s32[8,8]{1,0:T(8,128)} %bitcast.19, bf16[8,80,128]{2,1,0:T(8,128)(2,1)} %all_to_all.36.c1_ref, bf16[8,80,128]{2,1,0:T(8,128)(2,1)} %copy-done, bf16[256,512]{1,0:T(8,128)(2,1)} %get-tuple-element.27.hi_ref, ...), custom_call_target="tpu_custom_call" | custom-call | tf_op jit(solution)/shard_map/pallas_call | solution.py:333
  61.9 11.6 %all_to_all.37.b2_ref = bf16[8,80,128]{2,1,0:T(8,128)(2,1)} all-to-all(bf16[8,80,128]{2,1,0:T(8,128)(2,1)} %get-tuple-element.34), channel_id=1, replica_groups=mesh['freq'=4,'tcol'=8] {'tcol'}, dimensions={0} | all-to-all | bytes 327680 | tf_op jit(solution)/shard_map/all_to_all | solution.py:342
  73.4 2.4 %shard_map.75 = (f32[8,128]{1,0:T(8,128)}, bf16[8,64,128]{2,1,0:T(8,128)(2,1)}) custom-call(s32[1]{0:T(128)} %bitcast.1.here_ref, s32[8,8]{1,0:T(8,128)} %bitcast.20, bf16[8,80,128]{2,1,0:T(8,128)(2,1)} %all_to_all.37.b2_ref, bf16[8,64,128]{2,1,0:T(8,128)(2,1)} %copy-done.1, f32[256,256]{1,0:T(8,128)} %get-tuple-element.35.b1s_ref, ...), custom_call_target="tpu_custom_call" | custom-call | tf_op jit(solution)/shard_map/pallas_call | solution.py:333
  75.9 3.4 %all-to-all-start.5 = ((bf16[8,64,128]{2,1,0:T(8,128)(2,1)}), bf16[8,64,128]{2,1,0:T(8,128)(2,1)S(1)}, u32[]{:S(2)}, u32[]{:S(2)}) async-start(bf16[8,64,128]{2,1,0:T(8,128)(2,1)} %get-tuple-element.38), calls=%async_computation.5 | async-start | bytes 262144 | tf_op jit(solution)/shard_map/all_to_all | solution.py:342
  79.9 6.6 %all-to-all-done.5.c2_ref = bf16[8,64,128]{2,1,0:T(8,128)(2,1)S(1)} async-done(((bf16[8,64,128]{2,1,0:T(8,128)(2,1)}), bf16[8,64,128]{2,1,0:T(8,128)(2,1)S(1)}, u32[]{:S(2)}, u32[]{:S(2)}) %all-to-all-start.5) | async-done | bytes 131104 | tf_op jit(solution)/shard_map/all_to_all | solution.py:342
  87.2 2.3 %shard_map.76 = f32[32,16,128]{2,1,0:T(8,128)} custom-call(s32[1]{0:T(128)S(6)} %copy.7.freq_ref, bf16[8,64,128]{2,1,0:T(8,128)(2,1)} %copy-done.2, bf16[8,80,128]{2,1,0:T(8,128)(2,1)} %copy-done, bf16[8,80,128]{2,1,0:T(8,128)(2,1)} %all_to_all.36.c1_ref, bf16[256,512]{1,0:T(8,128)(2,1)} %get-tuple-element.27.hi_ref, ...), custom_call_target="tpu_custom_call" | custom-call | tf_op jit(solution)/shard_map/pallas_call | solution.py:333
  89.5 2.6 %all-to-all-start.6 = ((f32[32,16,128]{2,1,0:T(8,128)}), f32[32,16,128]{2,1,0:T(8,128)S(1)}, u32[]{:S(2)}, u32[]{:S(2)}) async-start(f32[32,16,128]{2,1,0:T(8,128)} %shard_map.76), calls=%async_computation.6 | async-start | bytes 524288 | tf_op jit(solution)/shard_map/all_to_all | solution.py:367
  92.1 10.4 %all-to-all-done.6.recv_ref = f32[32,16,128]{2,1,0:T(8,128)S(1)} async-done(((f32[32,16,128]{2,1,0:T(8,128)}), f32[32,16,128]{2,1,0:T(8,128)S(1)}, u32[]{:S(2)}, u32[]{:S(2)}) %all-to-all-start.6) | async-done | bytes 262176 | tf_op jit(solution)/shard_map/all_to_all | solution.py:367
  102.5 0.7 copy-done.3
  103.2 3.5 %shard_map.77 = (f32[2,512,128]{2,1,0:T(8,128)}, f32[2,512,128]{2,1,0:T(8,128)}) custom-call(s32[1]{0:T(128)} %bitcast.mine_ref, f32[32,16,128]{2,1,0:T(8,128)} %copy-done.3, bf16[2,512,128]{2,1,0:T(8,128)(2,1)} %bitcast.14, bf16[2,512,256]{2,1,0:T(8,128)(2,1)} %bitcast.10, bf16[2,512,256]{2,1,0:T(8,128)(2,1)} %bitcast.12, bf16[8,64,128]{2,1,0:T(8,128)(2,1)} %copy-done.1, ...), custom_call_target="tpu_custom_call" | custom-call | tf_op jit(solution)/shard_map/pallas_call | solution.py:333
  (5 shorter events, 0.7 us)
Async XLA Ops:
  2.9 14.6 %all-to-all-start = ((bf16[8,64,128]{2,1,0:T(8,128)(2,1)}), bf16[8,64,128]{2,1,0:T(8,128)(2,1)S(1)}, u32[]{:S(2)}, u32[]{:S(2)}) async-start(bf16[8,64,128]{2,1,0:T(8,128)(2,1)} %get-tuple-element.23), calls=%async_computation | async-start | bytes 262144 | tf_op jit(solution)/shard_map/all_to_all | solution.py:342
  17.5 0.7 copy-start.1
  20.3 10.9 %all-to-all-start.1 = ((bf16[8,80,128]{2,1,0:T(8,128)(2,1)}), bf16[8,80,128]{2,1,0:T(8,128)(2,1)S(1)}, u32[]{:S(2)}, u32[]{:S(2)}) async-start(bf16[8,80,128]{2,1,0:T(8,128)(2,1)} %get-tuple-element.26), calls=%async_computation.1 | async-start | bytes 327680 | tf_op jit(solution)/shard_map/all_to_all | solution.py:342
  31.2 0.7 copy-start
  75.9 10.7 %all-to-all-start.5 = ((bf16[8,64,128]{2,1,0:T(8,128)(2,1)}), bf16[8,64,128]{2,1,0:T(8,128)(2,1)S(1)}, u32[]{:S(2)}, u32[]{:S(2)}) async-start(bf16[8,64,128]{2,1,0:T(8,128)(2,1)} %get-tuple-element.38), calls=%async_computation.5 | async-start | bytes 262144 | tf_op jit(solution)/shard_map/all_to_all | solution.py:342
  86.5 0.6 copy-start.2
  89.5 13.0 %all-to-all-start.6 = ((f32[32,16,128]{2,1,0:T(8,128)}), f32[32,16,128]{2,1,0:T(8,128)S(1)}, u32[]{:S(2)}, u32[]{:S(2)}) async-start(f32[32,16,128]{2,1,0:T(8,128)} %shard_map.76), calls=%async_computation.6 | async-start | bytes 524288 | tf_op jit(solution)/shard_map/all_to_all | solution.py:367
  102.5 0.7 copy-start.3

commit v2 on v1

--- a/solution.py
+++ b/solution.py
@@ -329,6 +329,8 @@
     message = jax.ShapeDtypeStruct((ntile, 2 * rank + RIDE, s), BF16)
     gram = jax.ShapeDtypeStruct((width, 2 * width), BF16)
 
+    room = (8 << 20) + 24 * width * width
+
     def call(kernel, scalars, arrays, outs, scratch=(), *static):
         return pl.pallas_call(
             functools.partial(kernel, *static) if static else kernel,
@@ -336,6 +338,7 @@
             in_specs=[SMEM] * len(scalars) + [VMEM] * len(arrays),
             out_specs=[VMEM] * len(outs),
             scratch_shapes=scratch,
+            compiler_params=pltpu.CompilerParams(vmem_limit_bytes=room),
         )(*scalars, *arrays)
 
     def exchange(value):

time: 108 us -> 93.8 us (0.87)
  Pallas kernels: 24.2 us -> 11.5 us
  blocking collectives: 34.7 us -> 29.9 us
  waiting for transfers between devices: 27.3 us -> 30.9 us
    pallas_call x10, Pallas kernels: 24.2 us -> 11.5 us  [call(): pl.pallas_call(functools.partial(kernel, *static) if static else kernel,...]
    all_to_all x3, blocking collectives: 34.7 us -> 29.9 us  [exchange(): return lax.all_to_all(value, 'tcol', 0, 0, tiled=True)]
    all_to_all x3, waiting for transfers between devices: 16.9 us -> 20.5 us  [exchange(): return lax.all_to_all(value, 'tcol', 0, 0, tiled=True)]
    unnamed x8 -> x12, local copies, waits for them, and re-layouts: 2.68 us -> 2.68 us
  transfers between devices with their start and end apart: 4 -> 4, of which waited for: 4 -> 4; matrix products, arithmetic and copies ran while one was open for 0% -> 0% of each run, Pallas kernels for 4% -> 1%
where the time goes in v2:
time: 93.8 us; the launch traced here: 93.1 us
  waiting for transfers between devices  30.9 us (33%)
  blocking collectives  29.9 us (32%)
  starting transfers between devices  16.8 us (18%)
  Pallas kernels  11.5 us (12%)
  local copies, waits for them, and re-layouts  2.68 us (3%)
  between operations  1.38 us (1%)
    all_to_all x3, blocking collectives, exchange(): return lax.all_to_all(value, 'tcol', 0, 0, tiled=True)  29.9 us
    all_to_all x3, waiting for transfers between devices, exchange(): return lax.all_to_all(value, 'tcol', 0, 0, tiled=True)  20.5 us
    all_to_all x3, starting transfers between devices, exchange(): return lax.all_to_all(value, 'tcol', 0, 0, tiled=True)  14 us
    pallas_call x10, Pallas kernels, call(): pl.pallas_call(functools.partial(kernel, *static) if static else kernel,...  11.5 us
    all_to_all x1, waiting for transfers between devices, body(): everyone = lax.all_to_all(out, ('freq', 'tcol'), 0, 0, tiled=True)  10.4 us
    all_to_all x1, starting transfers between devices, body(): everyone = lax.all_to_all(out, ('freq', 'tcol'), 0, 0, tiled=True)  2.72 us
    unnamed x12, local copies, waits for them, and re-layouts  2.68 us
  transfers between devices with their start and end apart: 4, of which 4 were waited for; matrix products, arithmetic and copies ran while one was open for 0% of the time, Pallas kernels for 1%

profile of v2, /device:TPU:0, one launch (start us, length us, event | category | flops | bytes accessed | tf_op | source)
XLA Modules:
  0.0 93.1 jit_solution(1481085775891962137)
XLA Ops:
  0.6 0.7 copy-done.5
  1.3 1.0 %copy-done = bf16[1,2,512,256]{3,2,1,0:T(8,128)(2,1)S(1)} copy-done((bf16[1,2,512,256]{3,2,1,0:T(8,128)(2,1)S(1)}, bf16[1,2,512,256]{3,2,1,0:T(8,128)(2,1)}, u32[]{:S(2)}) %copy-start) | copy-done | bytes 524312
  2.4 0.9 %copy-done.3 = bf16[1,2,512,128]{3,2,1,0:T(8,128)(2,1)S(1)} copy-done((bf16[1,2,512,128]{3,2,1,0:T(8,128)(2,1)S(1)}, bf16[1,2,512,128]{3,2,1,0:T(8,128)(2,1)}, u32[]{:S(2)}) %copy-start.3) | copy-done | bytes 262168
  3.3 1.6 %shard_map.68 = (f32[256,256]{1,0:T(8,128)S(1)}, bf16[8,64,128]{2,1,0:T(8,128)(2,1)}) custom-call(s32[1]{0:T(128)} %bitcast.1.here_ref, s32[8,8]{1,0:T(8,128)S(1)} %bitcast.15, bf16[2,512,128]{2,1,0:T(8,128)(2,1)S(1)} %bitcast.13, bf16[2,512,256]{2,1,0:T(8,128)(2,1)S(1)} %bitcast.8), custom_call_target="tpu_custom_call" | custom-call | tf_op jit(solution)/shard_map/pallas_call | solution.py:335
  4.9 7.3 %all-to-all-start = ((bf16[8,64,128]{2,1,0:T(8,128)(2,1)}), bf16[8,64,128]{2,1,0:T(8,128)(2,1)S(1)}, u32[]{:S(2)}, u32[]{:S(2)}) async-start(bf16[8,64,128]{2,1,0:T(8,128)(2,1)} %get-tuple-element.23), calls=%async_computation | async-start | bytes 262144 | tf_op jit(solution)/shard_map/all_to_all | solution.py:345
  12.2 0.5 shard_map.69
  12.7 6.8 %all-to-all-done.b0_ref = bf16[8,64,128]{2,1,0:T(8,128)(2,1)S(1)} async-done(((bf16[8,64,128]{2,1,0:T(8,128)(2,1)}), bf16[8,64,128]{2,1,0:T(8,128)(2,1)S(1)}, u32[]{:S(2)}, u32[]{:S(2)}) %all-to-all-start) | async-done | bytes 131104 | tf_op jit(solution)/shard_map/all_to_all | solution.py:345
  19.5 1.6 %shard_map.70 = (f32[256,256]{1,0:T(8,128)S(1)}, f32[8,128]{1,0:T(8,128)S(1)}, bf16[8,80,128]{2,1,0:T(8,128)(2,1)}) custom-call(s32[1]{0:T(128)} %bitcast.1.here_ref, s32[8,8]{1,0:T(8,128)S(1)} %bitcast.16, bf16[8,64,128]{2,1,0:T(8,128)(2,1)S(1)} %all-to-all-done.b0_ref, bf16[256,512]{1,0:T(8,128)(2,1)S(1)} %get-tuple-element.24.hi_ref, ...), custom_call_target="tpu_custom_call" | custom-call | tf_op jit(solution)/shard_map/pallas_call | solution.py:335
  21.1 3.4 %all-to-all-start.1 = ((bf16[8,80,128]{2,1,0:T(8,128)(2,1)}), bf16[8,80,128]{2,1,0:T(8,128)(2,1)S(1)}, u32[]{:S(2)}, u32[]{:S(2)}) async-start(bf16[8,80,128]{2,1,0:T(8,128)(2,1)} %get-tuple-element.26), calls=%async_computation.1 | async-start | bytes 327680 | tf_op jit(solution)/shard_map/all_to_all | solution.py:345
  24.5 0.5 shard_map.71
  25.0 7.0 %all-to-all-done.1.c0_ref = bf16[8,80,128]{2,1,0:T(8,128)(2,1)S(1)} async-done(((bf16[8,80,128]{2,1,0:T(8,128)(2,1)}), bf16[8,80,128]{2,1,0:T(8,128)(2,1)S(1)}, u32[]{:S(2)}, u32[]{:S(2)}) %all-to-all-start.1) | async-done | bytes 163872 | tf_op jit(solution)/shard_map/all_to_all | solution.py:345
  32.0 0.9 shard_map.72
  32.9 10.0 %all_to_all.35.b1_ref = bf16[8,80,128]{2,1,0:T(8,128)(2,1)S(1)} all-to-all(bf16[8,80,128]{2,1,0:T(8,128)(2,1)S(1)} %get-tuple-element.30), channel_id=1, replica_groups=mesh['freq'=4,'tcol'=8] {'tcol'}, dimensions={0} | all-to-all | bytes 327680 | tf_op jit(solution)/shard_map/all_to_all | solution.py:345
  42.9 0.9 shard_map.73
  43.8 10.0 %all_to_all.36.c1_ref = bf16[8,80,128]{2,1,0:T(8,128)(2,1)S(1)} all-to-all(bf16[8,80,128]{2,1,0:T(8,128)(2,1)S(1)} %get-tuple-element.33), channel_id=1, replica_groups=mesh['freq'=4,'tcol'=8] {'tcol'}, dimensions={0} | all-to-all | bytes 327680 | tf_op jit(solution)/shard_map/all_to_all | solution.py:345
  53.8 0.9 shard_map.74
  54.7 10.0 %all_to_all.37.b2_ref = bf16[8,80,128]{2,1,0:T(8,128)(2,1)S(1)} all-to-all(bf16[8,80,128]{2,1,0:T(8,128)(2,1)S(1)} %get-tuple-element.34), channel_id=1, replica_groups=mesh['freq'=4,'tcol'=8] {'tcol'}, dimensions={0} | all-to-all | bytes 327680 | tf_op jit(solution)/shard_map/all_to_all | solution.py:345
  64.7 1.6 %shard_map.75 = (f32[8,128]{1,0:T(8,128)S(1)}, bf16[8,64,128]{2,1,0:T(8,128)(2,1)}) custom-call(s32[1]{0:T(128)} %bitcast.1.here_ref, s32[8,8]{1,0:T(8,128)S(1)} %bitcast.20, bf16[8,80,128]{2,1,0:T(8,128)(2,1)S(1)} %all_to_all.37.b2_ref, bf16[8,64,128]{2,1,0:T(8,128)(2,1)S(1)} %all-to-all-done.b0_ref, f32[256,256]{1,0:T(8,128)S(1)} %get-tuple-element.35.b1s_ref, ...), custom_call_target="tpu_custom_call" | custom-call | tf_op jit(solution)/shard_map/pallas_call | solution.py:335
  66.3 3.4 %all-to-all-start.5 = ((bf16[8,64,128]{2,1,0:T(8,128)(2,1)}), bf16[8,64,128]{2,1,0:T(8,128)(2,1)S(1)}, u32[]{:S(2)}, u32[]{:S(2)}) async-start(bf16[8,64,128]{2,1,0:T(8,128)(2,1)} %get-tuple-element.38), calls=%async_computation.5 | async-start | bytes 262144 | tf_op jit(solution)/shard_map/all_to_all | solution.py:345
  70.3 6.6 %all-to-all-done.5.c2_ref = bf16[8,64,128]{2,1,0:T(8,128)(2,1)S(1)} async-done(((bf16[8,64,128]{2,1,0:T(8,128)(2,1)}), bf16[8,64,128]{2,1,0:T(8,128)(2,1)S(1)}, u32[]{:S(2)}, u32[]{:S(2)}) %all-to-all-start.5) | async-done | bytes 131104 | tf_op jit(solution)/shard_map/all_to_all | solution.py:345
  77.0 1.0 %shard_map.76 = f32[32,16,128]{2,1,0:T(8,128)} custom-call(s32[1]{0:T(128)S(6)} %copy.7.freq_ref, bf16[8,64,128]{2,1,0:T(8,128)(2,1)S(1)} %all-to-all-done.5.c2_ref, bf16[8,80,128]{2,1,0:T(8,128)(2,1)S(1)} %all-to-all-done.1.c0_ref, bf16[8,80,128]{2,1,0:T(8,128)(2,1)S(1)} %all_to_all.36.c1_ref, bf16[256,512]{1,0:T(8,128)(2,1)S(1)} %get-tuple-element.27.hi_ref, ...), custom_call_target="tpu_custom_call" | custom-call | tf_op jit(solution)/shard_map/pallas_call | solution.py:335
  78.0 2.7 %all-to-all-start.6 = ((f32[32,16,128]{2,1,0:T(8,128)}), f32[32,16,128]{2,1,0:T(8,128)S(1)}, u32[]{:S(2)}, u32[]{:S(2)}) async-start(f32[32,16,128]{2,1,0:T(8,128)} %shard_map.76), calls=%async_computation.6 | async-start | bytes 524288 | tf_op jit(solution)/shard_map/all_to_all | solution.py:370
  80.8 10.4 %all-to-all-done.6.recv_ref = f32[32,16,128]{2,1,0:T(8,128)S(1)} async-done(((f32[32,16,128]{2,1,0:T(8,128)}), f32[32,16,128]{2,1,0:T(8,128)S(1)}, u32[]{:S(2)}, u32[]{:S(2)}) %all-to-all-start.6) | async-done | bytes 262176 | tf_op jit(solution)/shard_map/all_to_all | solution.py:370
  91.2 1.9 %shard_map.77 = (f32[2,512,128]{2,1,0:T(8,128)}, f32[2,512,128]{2,1,0:T(8,128)}) custom-call(s32[1]{0:T(128)} %bitcast.mine_ref, f32[32,16,128]{2,1,0:T(8,128)S(1)} %all-to-all-done.6.recv_ref, bf16[2,512,128]{2,1,0:T(8,128)(2,1)S(1)} %bitcast.14, bf16[2,512,256]{2,1,0:T(8,128)(2,1)S(1)} %bitcast.10, bf16[2,512,256]{2,1,0:T(8,128)(2,1)S(1)} %bitcast.12, ...), custom_call_target="tpu_custom_call" | custom-call | tf_op jit(solution)/shard_map/pallas_call | solution.py:335
  (9 shorter events, 0.0 us)
Async XLA Ops:
  0.6 0.7 copy-start.5
  1.3 1.0 %copy-start = (bf16[1,2,512,256]{3,2,1,0:T(8,128)(2,1)S(1)}, bf16[1,2,512,256]{3,2,1,0:T(8,128)(2,1)}, u32[]{:S(2)}) copy-start(bf16[1,2,512,256]{3,2,1,0:T(8,128)(2,1)} %param.6) | copy-start | bytes 1572868
  2.4 0.9 %copy-start.3 = (bf16[1,2,512,128]{3,2,1,0:T(8,128)(2,1)S(1)}, bf16[1,2,512,128]{3,2,1,0:T(8,128)(2,1)}, u32[]{:S(2)}) copy-start(bf16[1,2,512,128]{3,2,1,0:T(8,128)(2,1)} %param.5) | copy-start | bytes 786436
  3.3 8.9 %copy-start.2 = (bf16[1,2,512,256]{3,2,1,0:T(8,128)(2,1)S(1)}, bf16[1,2,512,256]{3,2,1,0:T(8,128)(2,1)}, u32[]{:S(2)}) copy-start(bf16[1,2,512,256]{3,2,1,0:T(8,128)(2,1)} %param.7) | copy-start | bytes 1572868
  4.9 14.6 %all-to-all-start = ((bf16[8,64,128]{2,1,0:T(8,128)(2,1)}), bf16[8,64,128]{2,1,0:T(8,128)(2,1)S(1)}, u32[]{:S(2)}, u32[]{:S(2)}) async-start(bf16[8,64,128]{2,1,0:T(8,128)(2,1)} %get-tuple-element.23), calls=%async_computation | async-start | bytes 262144 | tf_op jit(solution)/shard_map/all_to_all | solution.py:345
  12.7 11.8 %copy-start.1 = (bf16[1,2,512,256]{3,2,1,0:T(8,128)(2,1)S(1)}, bf16[1,2,512,256]{3,2,1,0:T(8,128)(2,1)}, u32[]{:S(2)}) copy-start(bf16[1,2,512,256]{3,2,1,0:T(8,128)(2,1)} %param.6) | copy-start | bytes 1572868
  21.1 10.9 %all-to-all-start.1 = ((bf16[8,80,128]{2,1,0:T(8,128)(2,1)}), bf16[8,80,128]{2,1,0:T(8,128)(2,1)S(1)}, u32[]{:S(2)}, u32[]{:S(2)}) async-start(bf16[8,80,128]{2,1,0:T(8,128)(2,1)} %get-tuple-element.26), calls=%async_computation.1 | async-start | bytes 327680 | tf_op jit(solution)/shard_map/all_to_all | solution.py:345
  66.3 10.7 %all-to-all-start.5 = ((bf16[8,64,128]{2,1,0:T(8,128)(2,1)}), bf16[8,64,128]{2,1,0:T(8,128)(2,1)S(1)}, u32[]{:S(2)}, u32[]{:S(2)}) async-start(bf16[8,64,128]{2,1,0:T(8,128)(2,1)} %get-tuple-element.38), calls=%async_computation.5 | async-start | bytes 262144 | tf_op jit(solution)/shard_map/all_to_all | solution.py:345
  78.0 13.2 %copy-start.4 = (bf16[1,2,512,128]{3,2,1,0:T(8,128)(2,1)S(1)}, bf16[1,2,512,128]{3,2,1,0:T(8,128)(2,1)}, u32[]{:S(2)}) copy-start(bf16[1,2,512,128]{3,2,1,0:T(8,128)(2,1)} %param.5) | copy-start | bytes 786436
  78.0 13.2 %all-to-all-start.6 = ((f32[32,16,128]{2,1,0:T(8,128)}), f32[32,16,128]{2,1,0:T(8,128)S(1)}, u32[]{:S(2)}, u32[]{:S(2)}) async-start(f32[32,16,128]{2,1,0:T(8,128)} %shard_map.76), calls=%async_computation.6 | async-start | bytes 524288 | tf_op jit(solution)/shard_map/all_to_all | solution.py:370

commit v3 on v2

v3 whole, which is shorter than its diff:
```python
import functools

import jax
import jax.numpy as jnp
from jax import lax
from jax.experimental import pallas as pl
from jax.experimental.pallas import tpu as pltpu
from jax.sharding import PartitionSpec as P


RIDE = 16
LATE = 4
EARLY = 9
VMEM = pl.BlockSpec(memory_space=pltpu.VMEM)
SMEM = pl.BlockSpec(memory_space=pltpu.SMEM)
HBM = pl.BlockSpec(memory_space=pltpu.HBM)
F32 = jnp.float32
BF16 = jnp.bfloat16


def dot(a, b):
    return jnp.dot(a, b, preferred_element_type=F32)


def dot_t(a, b):
    return lax.dot_general(a, b, (((0,), (0,)), ((), ())), preferred_element_type=F32)


def side(real, imag):
    return jnp.concatenate([real, imag], axis=1)


def split(value):
    high = value.astype(BF16)
    return high, (value - high.astype(F32)).astype(BF16)


def unpack(ref, rank):
    n = ref.shape[0]
    real = ref[:, 0:rank, :].reshape(n * rank, ref.shape[2])
    imag = ref[:, rank : 2 * rank, :].reshape(n * rank, ref.shape[2])
    return real, imag


def fields(ref, rank):
    return side(*unpack(ref, rank)).astype(F32)


def send(out_ref, value, rank):
    s = out_ref.shape[2]
    for p in range(out_ref.shape[0]):
        rows = value[p * rank : (p + 1) * rank].astype(BF16)
        out_ref[p, 0:rank, :] = rows[:, :s]
        out_ref[p, rank : 2 * rank, :] = rows[:, s:]


def ride(out_ref, rows, rank):
    rows = rows + [jnp.zeros_like(rows[0])] * (RIDE - len(rows))
    block = jnp.concatenate(rows, axis=0).astype(BF16)
    for p in range(out_ref.shape[0]):
        out_ref[p, 2 * rank : 2 * rank + RIDE, :] = block


def ridden(ref, rank):
    total = ref[0, 2 * rank : 2 * rank + RIDE, :].astype(F32)
    for p in range(1, ref.shape[0]):
        total = total + ref[p, 2 * rank : 2 * rank + RIDE, :].astype(F32)
    return total


def inner(a, b):
    both = jnp.sum(a * b, axis=0, keepdims=True)
    s = both.shape[1] // 2
    return both[:, :s] + both[:, s:]


def twice(row):
    return jnp.concatenate([row, row], axis=1)


def ratio(top, bottom):
    safe = bottom > 0
    return jnp.where(safe, top / jnp.where(safe, bottom, 1.0), 0.0)


def apply_gram(hi_ref, lo_ref, real, imag):
    vector = jnp.concatenate([side(real, imag), side(-imag, real)], axis=0)
    return dot(hi_ref[...], vector) + dot(lo_ref[...], vector)


def make_gram(factor_ref, hi_ref, lo_ref, limits):
    real, imag = factor_ref[0], factor_ref[1]
    width = real.shape[1]
    rank = width // len(limits)
    level = lax.broadcasted_iota(jnp.int32, (rank, width), 0)

    def put(value, place):
        for p, limit in enumerate(limits):
            rows = slice(p * rank, (p + 1) * rank)
            high, low = split(jnp.where(level < limit, value[rows], 0.0))
            hi_ref[rows, place : place + width] = high
            lo_ref[rows, place : place + width] = low

    put(dot_t(real, real) + dot_t(imag, imag), 0)
    put(dot_t(real, imag) - dot_t(imag, real), width)


def start_kernel(
    rank, here_ref, mine_ref, ranks_hbm, freq_hbm, data_hbm, left_hbm, right_hbm,
    right_ref, back_ref, sums_ref, out_ref, uhi_ref, ulo_ref, vhi_ref, vlo_ref,
    ranks_ref, freq_ref, data_ref, left_ref, sem
):
    n = out_ref.shape[0]
    s = out_ref.shape[2]
    pairs = [
        (left_hbm, left_ref), (data_hbm, data_ref), (ranks_hbm, ranks_ref),
        (freq_hbm, freq_ref), (right_hbm, right_ref),
    ]
    copies = [
        pltpu.make_async_copy(source, target, sem.at[k])
        for k, (source, target) in enumerate(pairs)
    ]
    for copy in copies:
        copy.start()
    for copy in copies[:4]:
        copy.wait()
    here = here_ref[0]
    row_limits = [ranks_ref[here, p] for p in range(n)]
    column_limits = [ranks_ref[p, here] for p in range(n)]
    damping = 0.1 + 0.9 * freq_ref[0].astype(F32) / 229.0
    sums_ref[...] = jnp.full(sums_ref.shape, damping)
    real, imag = data_ref[0], data_ref[1]
    back = dot_t(left_ref[0], side(real, imag)) + dot_t(left_ref[1], side(imag, -real))
    level = lax.broadcasted_iota(jnp.int32, (rank, 2 * s), 0)
    back = jnp.concatenate(
        [
            jnp.where(level < limit, back[p * rank : (p + 1) * rank], 0.0)
            for p, limit in enumerate(row_limits)
        ],
        axis=0,
    )
    back_ref[...] = back
    send(out_ref, back, rank)
    make_gram(left_ref, uhi_ref, ulo_ref, row_limits)
    copies[4].wait()
    make_gram(right_ref, vhi_ref, vlo_ref, column_limits)


def column0(rank, b0_ref, hi_ref, lo_ref, g0_ref, sums_ref, out_ref):
    real, imag = unpack(b0_ref, rank)
    g0 = apply_gram(hi_ref, lo_ref, real, imag)
    g0_ref[...] = g0
    m00 = inner(side(real, imag).astype(F32), g0)
    sums_ref[0:1, :] = m00
    send(out_ref, g0, rank)
    ride(out_ref, [m00], rank)


def row0(rank, c0_ref, hi_ref, lo_ref, back_ref, sums_ref, out_ref):
    real, imag = unpack(c0_ref, rank)
    next0 = apply_gram(hi_ref, lo_ref, real, imag)
    c0 = side(real, imag).astype(F32)
    n00 = inner(c0, next0)
    sums_ref[0:1, :] = n00
    sums_ref[1:2, :] = inner(back_ref[...], c0)
    sums_ref[2:3, :] = ridden(c0_ref, rank)[0:1]
    send(out_ref, next0, rank)
    ride(out_ref, [n00], rank)


def column1(
    rank, b1_ref, b0_ref, hi_ref, lo_ref, g0_ref, n0_ref, g1_ref, sums_ref, out_ref
):
    real, imag = unpack(b1_ref, rank)
    theta0 = ratio(ridden(b1_ref, rank)[0:1], n0_ref[2:3, :])
    wide = twice(theta0)
    g1 = apply_gram(hi_ref, lo_ref, real, imag) - wide * g0_ref[...]
    b0 = fields(b0_ref, rank)
    b1 = side(real, imag).astype(F32) - wide * b0
    g1_ref[...] = g1
    m11 = inner(b1, g1)
    sums_ref[0:1, :] = m11
    sums_ref[1:2, :] = inner(b0, g1)
    sums_ref[2:3, :] = theta0
    send(out_ref, g1, rank)
    ride(out_ref, [m11], rank)


def row1(rank, c1_ref, c0_ref, hi_ref, lo_ref, back_ref, sums_ref, out_ref):
    real, imag = unpack(c1_ref, rank)
    next1 = apply_gram(hi_ref, lo_ref, real, imag)
    c1 = side(real, imag).astype(F32)
    n11 = inner(c1, next1)
    n01 = inner(fields(c0_ref, rank), next1)
    sums_ref[0:1, :] = n11
    sums_ref[1:2, :] = n01
    sums_ref[2:3, :] = inner(back_ref[...], c1)
    sums_ref[3:4, :] = ridden(c1_ref, rank)[0:1]
    send(out_ref, next1, rank)
    ride(out_ref, [n11, n01], rank)


def column2(
    rank, b2_ref, b0_ref, b1_ref, hi_ref, lo_ref, g0_ref, g1_ref,
    damp_ref, m0_ref, n0_ref, m1_ref, n1_ref, sums_ref, out_ref
):
    real, imag = unpack(b2_ref, rank)
    came = ridden(b2_ref, rank)
    theta1 = ratio(came[0:1], n1_ref[3:4, :])
    phi = ratio(came[1:2], n0_ref[2:3, :])
    wide1, wide0 = twice(theta1), twice(phi)
    g2 = apply_gram(hi_ref, lo_ref, real, imag) - wide1 * g1_ref[...] - wide0 * g0_ref[...]
    send(out_ref, g2, rank)
    b0 = fields(b0_ref, rank)
    b1 = fields(b1_ref, rank) - twice(m1_ref[2:3, :]) * b0
    b2 = side(real, imag).astype(F32) - wide1 * b1 - wide0 * b0
    sums_ref[0:1, :] = inner(b0, g2)
    sums_ref[1:2, :] = inner(b1, g2)
    sums_ref[2:3, :] = inner(b2, g2)
    sums_ref[3:4, :] = theta1
    sums_ref[4:5, :] = phi
    damping = damp_ref[0:1, :]
    known = [
        n0_ref[0:1, :] + damping * m0_ref[0:1, :],
        n1_ref[1:2, :] + damping * m1_ref[1:2, :],
        n1_ref[0:1, :] + damping * m1_ref[0:1, :],
        n0_ref[1:2, :],
        n1_ref[2:3, :],
    ]
    rest = [row - row.astype(BF16).astype(F32) for row in known]
    ride(out_ref, known + rest, rank)


def row2(
    rank, share, here_ref, c2_ref, c0_ref, c1_ref, hi_ref, lo_ref, back_ref,
    damp_ref, m1_ref, m2_ref, out_ref, table_ref
):
    real, imag = unpack(c2_ref, rank)
    next2 = apply_gram(hi_ref, lo_ref, real, imag)
    damping = damp_ref[0:1, :]
    came = ridden(c2_ref, rank)
    table_ref[0:5, :] = came[0:5] + came[5:10]
    table_ref[5:6, :] = m1_ref[2:3, :]
    table_ref[6:8, :] = m2_ref[3:5, :]
    table_ref[8:9, :] = damping
    rows = [
        inner(fields(c0_ref, rank), next2) + damping * m2_ref[0:1, :],
        inner(fields(c1_ref, rank), next2) + damping * m2_ref[1:2, :],
        inner(side(real, imag).astype(F32), next2) + damping * m2_ref[2:3, :],
        inner(back_ref[...], side(real, imag).astype(F32)),
        table_ref[pl.ds(here_ref[0] * share, share), :],
    ]
    more = out_ref.shape[1] - LATE - share
    if more:
        rows.append(jnp.zeros((more, real.shape[1]), F32))
    block = jnp.concatenate(rows, axis=0)
    for p in range(out_ref.shape[0]):
        out_ref[p] = block


def forms(h, u, g, p, position, size):
    def times(v):
        return [sum(h[a][b] * v[b] for b in range(size)) for a in range(size)]

    def along(a, b):
        return jnp.sum(sum(x * y for x, y in zip(a, b)), axis=0, keepdims=True)

    hg, hp, hx = times(g), times(p), times(position)
    rest = [u[a] - hx[a] for a in range(size)]
    return along(g, hg), along(p, hg), along(p, hp), along(g, rest), along(p, rest)


def finish_kernel(
    rank, nfreq, share, mine_ref, data_hbm, left_hbm, recv_ref, right_ref,
    b0_ref, b1_ref, b2_ref, c0_ref, c1_ref, c2_ref, wave_hbm, res_hbm,
    table_ref, mix_ref, wave_ref, res_ref, data_ref, left_ref, sem
):
    left_copy = pltpu.make_async_copy(left_hbm, left_ref, sem.at[2])
    data_copy = pltpu.make_async_copy(data_hbm, data_ref, sem.at[3])
    left_copy.start()
    data_copy.start()
    ntile = recv_ref.shape[0] // nfreq
    for f in range(nfreq):
        total = recv_ref[f * ntile]
        for t in range(1, ntile):
            total = total + recv_ref[f * ntile + t]
        table_ref[0:LATE, f, :] = total[0:LATE]
        for q in range(EARLY):
            place = LATE + q % share
            table_ref[LATE + q, f : f + 1, :] = recv_ref[f * ntile + q // share, place : place + 1]
    h = [[None] * 3 for _ in range(3)]
    places = [(0, 0, 2), (1, 1, 2), (2, 2, 2), (4, 0, 0), (5, 0, 1), (6, 1, 1)]
    for place, a, b in places:
        h[a][b] = h[b][a] = table_ref[place]
    u = [table_ref[7], table_ref[8], table_ref[3]]
    theta0, theta1, phi, damping = [table_ref[9 + a] for a in range(4)]
    one = jnp.ones_like(theta0)
    a11 = jnp.sum(h[0][0], axis=0, keepdims=True)
    b1 = jnp.sum(u[0], axis=0, keepdims=True)
    alpha = b1 / (1.1 * a11)
    p = [alpha * one]
    x = [alpha * one]
    for size in (2, 3):
        zero = jnp.zeros_like(one)
        x = x + [zero]
        p = p + [zero]
        if size == 2:
            g = [one - (theta0 + damping) * x[0], -x[0]]
        else:
            g = [
                one - (theta0 + damping) * x[0] - phi * x[1],
                -x[0] - (theta1 + damping) * x[1],
                -x[1],
            ]
        a11, a12, a22, b1, b2 = forms(h, u, g, p, x, size)
        first, second = 1.1 * a11, 1.1 * a22
        determinant = first * second - a12 * a12
        alpha = (b1 * second - a12 * b2) / determinant
        beta = (first * b2 - a12 * b1) / determinant
        p = [alpha * g[a] + beta * p[a] for a in range(size)]
        x = [x[a] + p[a] for a in range(size)]
    mix_ref[0] = x[0] - theta0 * x[1] + (theta0 * theta1 - phi) * x[2]
    mix_ref[1] = x[1] - theta1 * x[2]
    mix_ref[2] = x[2]
    mix_ref[3] = x[0]
    mix_ref[4] = x[1]
    mix_ref[5] = x[2]
    row = pl.ds(mine_ref[0], 1)

    def combine(refs, offset):
        total = None
        for k, ref in enumerate(refs):
            scale = mix_ref[offset + k, row, :]
            real, imag = unpack(ref, rank)
            term = (scale * real.astype(F32), scale * imag.astype(F32))
            total = term if total is None else (total[0] + term[0], total[1] + term[1])
        return total

    def plain(factor_ref, real, imag):
        (rh, rl), (ih, il) = split(real), split(imag)
        first, second = factor_ref[0], factor_ref[1]
        return (
            dot(first, side(rh, ih)) + dot(second, side(-ih, rh))
            + dot(first, side(rl, il)) + dot(second, side(-il, rl))
        )

    s = wave_ref.shape[2]
    wave = plain(right_ref, *combine([b0_ref, b1_ref, b2_ref], 0))
    wave_ref[0] = wave[:, :s]
    wave_ref[1] = wave[:, s:]
    wave_copy = pltpu.make_async_copy(wave_ref, wave_hbm, sem.at[0])
    wave_copy.start()
    mixed = combine([c0_ref, c1_ref, c2_ref], 3)
    left_copy.wait()
    data_copy.wait()
    image = plain(left_ref, *mixed)
    res_ref[0] = data_ref[0].astype(F32) - image[:, :s]
    res_ref[1] = data_ref[1].astype(F32) - image[:, s:]
    res_copy = pltpu.make_async_copy(res_ref, res_hbm, sem.at[1])
    res_copy.start()
    wave_copy.wait()
    res_copy.wait()


def body(data, left_factor, right_factor, ranks, freq_index):
    ntile = lax.axis_size("tcol")
    nfreq = lax.axis_size("freq")
    here = lax.axis_index("tcol").reshape(1)
    mine = lax.axis_index("freq").reshape(1)
    data, left, right, ranks = data[0], left_factor[0], right_factor[0], ranks[0]
    data, left, right, ranks = [
        pltpu.with_memory_space_constraint(value, pltpu.HBM)
        for value in (data, left, right, ranks)
    ]
    width = left.shape[2]
    rank = width // ntile
    s = data.shape[2]
    share = -(-EARLY // ntile)
    height = -(-(LATE + share) // 8) * 8
    field = jax.ShapeDtypeStruct((width, 2 * s), F32)
    sums = jax.ShapeDtypeStruct((8, s), F32)
    bare = jax.ShapeDtypeStruct((ntile, 2 * rank, s), BF16)
    message = jax.ShapeDtypeStruct((ntile, 2 * rank + RIDE, s), BF16)
    gram = jax.ShapeDtypeStruct((width, 2 * width), BF16)
    room = (8 << 20) + 24 * width * width

    def like(value):
        return jax.ShapeDtypeStruct(value.shape, value.dtype)

    def call(kernel, specs, args, outs, scratch=(), target=VMEM):
        return pl.pallas_call(
            functools.partial(kernel, rank),
            out_shape=outs,
            in_specs=specs,
            out_specs=[target] * len(outs),
            scratch_shapes=scratch,
            compiler_params=pltpu.CompilerParams(vmem_limit_bytes=room),
        )(*args)

    def step(kernel, args, outs):
        return call(kernel, [VMEM] * len(args), args, outs)

    def exchange(value):
        return lax.all_to_all(value, "tcol", 0, 0, tiled=True)

    vright, back, damp, out, uhi, ulo, vhi, vlo = call(
        start_kernel, [SMEM] * 2 + [HBM] * 5, (here, mine, ranks, freq_index, data, left, right),
        (like(right), field, sums, bare, gram, gram, gram, gram),
        [
            pltpu.SMEM(ranks.shape, jnp.int32),
            pltpu.SMEM(freq_index.shape, jnp.int32),
            pltpu.VMEM(data.shape, BF16),
            pltpu.VMEM(left.shape, BF16),
            pltpu.SemaphoreType.DMA((5,)),
        ],
    )
    b0 = exchange(out)
    g0, m0, out = step(column0, (b0, vhi, vlo), (field, sums, message))
    c0 = exchange(out)
    n0, out = step(row0, (c0, uhi, ulo, back), (sums, message))
    b1 = exchange(out)
    g1, m1, out = step(column1, (b1, b0, vhi, vlo, g0, n0), (field, sums, message))
    c1 = exchange(out)
    n1, out = step(row1, (c1, c0, uhi, ulo, back), (sums, message))
    b2 = exchange(out)
    m2, out = step(
        column2, (b2, b0, b1, vhi, vlo, g0, g1, damp, m0, n0, m1, n1), (sums, message)
    )
    c2 = exchange(out)
    args = (here, c2, c0, c1, uhi, ulo, back, damp, m1, m2)
    (out,) = call(
        lambda rank, *refs: row2(rank, share, *refs), [SMEM] + [VMEM] * 9, args,
        (jax.ShapeDtypeStruct((nfreq * ntile, height, s), F32),),
        [pltpu.VMEM((max(16, ntile * share), s), F32)],
    )
    everyone = lax.all_to_all(out, ("freq", "tcol"), 0, 0, tiled=True)
    shape = jax.ShapeDtypeStruct(data.shape, F32)
    wave, res = call(
        lambda rank, *refs: finish_kernel(rank, nfreq, share, *refs),
        [SMEM, HBM, HBM] + [VMEM] * 8,
        (mine, data, left, everyone, vright, b0, b1, b2, c0, c1, c2), (shape, shape),
        [
            pltpu.VMEM((LATE + EARLY, nfreq, s), F32),
            pltpu.VMEM((6, nfreq, s), F32),
            pltpu.VMEM(shape.shape, F32),
            pltpu.VMEM(shape.shape, F32),
            pltpu.VMEM(data.shape, BF16),
            pltpu.VMEM(left.shape, BF16),
            pltpu.SemaphoreType.DMA((4,)),
        ],
        HBM,
    )
    return wave[None], res[None]


def solution(mesh):
    in_specs = (
        P("freq", None, "tcol", None),
        P("freq", None, "tcol", None),
        P("freq", None, "tcol", None),
        P("freq", None, None),
        P("freq"),
    )
    out_specs = (P("freq", None, "tcol", None), P("freq", None, "tcol", None))
    return jax.shard_map(body, mesh=mesh, in_specs=in_specs, out_specs=out_specs, check_vma=False)
```

time: 93.8 us -> 83.8 us (0.89)
  blocking collectives: 29.9 us -> 74.4 us
  waiting for transfers between devices: 30.9 us -> 0 us
  starting transfers between devices: 16.8 us -> 0 us
  Pallas kernels: 11.5 us -> 7.67 us
  local copies, waits for them, and re-layouts: 2.68 us -> 0 us
    all_to_all x3 -> x6, blocking collectives: 29.9 us -> 64.2 us  [exchange(): return lax.all_to_all(value, 'tcol', 0, 0, tiled=True)]
    all_to_all x4 -> x0, waiting for transfers between devices: 30.9 us -> none  [the longest x3 20.5 us: exchange(): return lax.all_to_all(value, 'tcol', 0, 0, tiled=True)]
    all_to_all x4 -> x0, starting transfers between devices: 16.8 us -> none  [the longest x3 14 us: exchange(): return lax.all_to_all(value, 'tcol', 0, 0, tiled=True)]
    all_to_all x0 -> x1, blocking collectives: none -> 10.1 us  [body(): everyone = lax.all_to_all(out, ('freq', 'tcol'), 0, 0, tiled=True)]
    pallas_call x10 -> x8, Pallas kernels: 11.5 us -> 7.67 us  [call(): pl.pallas_call(functools.partial(kernel, rank), out_shape=outs, in_specs=...]
    unnamed x12 -> x0, local copies, waits for them, and re-layouts: 2.68 us -> none
  transfers between devices with their start and end apart: 4 -> 0, of which waited for: 4 -> 0; matrix products, arithmetic and copies ran while one was open for 0% -> 0% of each run, Pallas kernels for 1% -> 0%
where the time goes in v3:
time: 83.8 us; the launch traced here: 83.4 us
  blocking collectives  74.4 us (89%)
  Pallas kernels  7.67 us (9%)
  between operations  1.33 us (2%)
    all_to_all x6, blocking collectives, exchange(): return lax.all_to_all(value, 'tcol', 0, 0, tiled=True)  64.2 us
    all_to_all x1, blocking collectives, body(): everyone = lax.all_to_all(out, ('freq', 'tcol'), 0, 0, tiled=True)  10.1 us
    pallas_call x8, Pallas kernels, call(): pl.pallas_call(functools.partial(kernel, rank), out_shape=outs, in_specs=...  7.67 us

profile of v3, /device:TPU:0, one launch (start us, length us, event | category | flops | bytes accessed | tf_op | source)
XLA Modules:
  0.0 83.4 jit_solution(11349926115016397386)
XLA Ops:
  1.3 2.3 %shard_map.68 = (bf16[2,512,256]{2,1,0:T(8,128)(2,1)S(1)}, f32[256,256]{1,0:T(8,128)S(1)}, f32[8,128]{1,0:T(8,128)S(1)}, bf16[8,64,128]{2,1,0:T(8,128)(2,1)S(1)}...) custom-call(s32[1]{0:T(128)} %bitcast.3.here_ref.refs_0_, ...), custom_call_target="tpu_custom_call" | custom-call | tf_op jit(solution)/shard_map/pallas_call | solution.py:391
  3.6 14.4 %all_to_all.35.b0_ref.refs_5_ = bf16[8,64,128]{2,1,0:T(8,128)(2,1)S(1)} all-to-all(bf16[8,64,128]{2,1,0:T(8,128)(2,1)S(1)} %get-tuple-element.24), channel_id=1, replica_groups=mesh['freq'=4,'tcol'=8] {'tcol'}, dimensions={0} | all-to-all | bytes 262144 | tf_op jit(solution)/shard_map/all_to_all | solution.py:404
  18.0 0.3 shard_map.69
  18.3 10.0 %all_to_all.36.c0_ref.refs_2_.refs_8_ = bf16[8,80,128]{2,1,0:T(8,128)(2,1)S(1)} all-to-all(bf16[8,80,128]{2,1,0:T(8,128)(2,1)S(1)} %get-tuple-element.27), channel_id=1, replica_groups=mesh['freq'=4,'tcol'=8] {'tcol'}, dimensions={0} | all-to-all | bytes 327680 | tf_op jit(solution)/shard_map/all_to_all | solution.py:404
  28.3 0.3 shard_map.70
  28.6 10.0 %all_to_all.37.b1_ref.refs_6_ = bf16[8,80,128]{2,1,0:T(8,128)(2,1)S(1)} all-to-all(bf16[8,80,128]{2,1,0:T(8,128)(2,1)S(1)} %get-tuple-element.31), channel_id=1, replica_groups=mesh['freq'=4,'tcol'=8] {'tcol'}, dimensions={0} | all-to-all | bytes 327680 | tf_op jit(solution)/shard_map/all_to_all | solution.py:404
  38.6 0.3 shard_map.71
  38.9 10.0 %all_to_all.38.c1_ref.refs_3_.refs_9_ = bf16[8,80,128]{2,1,0:T(8,128)(2,1)S(1)} all-to-all(bf16[8,80,128]{2,1,0:T(8,128)(2,1)S(1)} %get-tuple-element.34), channel_id=1, replica_groups=mesh['freq'=4,'tcol'=8] {'tcol'}, dimensions={0} | all-to-all | bytes 327680 | tf_op jit(solution)/shard_map/all_to_all | solution.py:404
  48.9 0.3 shard_map.72
  49.2 10.0 %all_to_all.39.b2_ref.refs_7_ = bf16[8,80,128]{2,1,0:T(8,128)(2,1)S(1)} all-to-all(bf16[8,80,128]{2,1,0:T(8,128)(2,1)S(1)} %get-tuple-element.35), channel_id=1, replica_groups=mesh['freq'=4,'tcol'=8] {'tcol'}, dimensions={0} | all-to-all | bytes 327680 | tf_op jit(solution)/shard_map/all_to_all | solution.py:404
  59.2 0.4 shard_map.73
  59.5 10.0 %all_to_all.40.refs_1_.refs_10_ = bf16[8,80,128]{2,1,0:T(8,128)(2,1)S(1)} all-to-all(bf16[8,80,128]{2,1,0:T(8,128)(2,1)S(1)} %get-tuple-element.41), channel_id=1, replica_groups=mesh['freq'=4,'tcol'=8] {'tcol'}, dimensions={0} | all-to-all | bytes 327680 | tf_op jit(solution)/shard_map/all_to_all | solution.py:404
  69.5 0.3 shard_map.74
  69.8 10.1 %all_to_all.41.refs_3_ = f32[32,8,128]{2,1,0:T(8,128)S(1)} all-to-all(f32[32,8,128]{2,1,0:T(8,128)S(1)} %shard_map.74), channel_id=1, replica_groups=mesh['freq'=4,'tcol'=8] {'freq','tcol'}, dimensions={0} | all-to-all | bytes 262144 | tf_op jit(solution)/shard_map/all_to_all | solution.py:436
  80.0 3.4 %shard_map.75 = (f32[2,512,128]{2,1,0:T(8,128)}, f32[2,512,128]{2,1,0:T(8,128)}) custom-call(s32[1]{0:T(128)} %bitcast.mine_ref.refs_0_, bf16[2,512,128]{2,1,0:T(8,128)(2,1)} %bitcast.11, bf16[2,512,256]{2,1,0:T(8,128)(2,1)} %bitcast.9, f32[32,8,128]{2,1,0:T(8,128)S(1)} %all_to_all.41.refs_3_, bf16[2,512,256]{2,1,0:T(8,128)(2,1)S(1)} %get-tuple-element.43.refs_4_, ...), custom_call_target="tpu_custom_call" | custom-call | tf_op jit(solution)/shard_map/pallas_call | solution.py:391

commit v4 on v3

--- a/solution.py
+++ b/solution.py
@@ -258,16 +258,45 @@
         out_ref[p] = block
 
 
-def forms(h, u, g, p, position, size):
+def forms(h, u, g, p, position, size, axis):
     def times(v):
         return [sum(h[a][b] * v[b] for b in range(size)) for a in range(size)]
 
     def along(a, b):
-        return jnp.sum(sum(x * y for x, y in zip(a, b)), axis=0, keepdims=True)
+        return jnp.sum(sum(x * y for x, y in zip(a, b)), axis=axis, keepdims=True)
 
     hg, hp, hx = times(g), times(p), times(position)
     rest = [u[a] - hx[a] for a in range(size)]
     return along(g, hg), along(p, hg), along(p, hp), along(g, rest), along(p, rest)
+
+
+def descend(h, u, theta0, theta1, phi, damping, axis):
+    one = jnp.ones_like(theta0)
+    a11 = jnp.sum(h[0][0], axis=axis, keepdims=True)
+    b1 = jnp.sum(u[0], axis=axis, keepdims=True)
+    alpha = b1 / (1.1 * a11)
+    p = [alpha * one]
+    x = [alpha * one]
+    for size in (2, 3):
+        zero = jnp.zeros_like(one)
+        x = x + [zero]
+        p = p + [zero]
+        if size == 2:
+            g = [one - (theta0 + damping) * x[0], -x[0]]
+        else:
+            g = [
+                one - (theta0 + damping) * x[0] - phi * x[1],
+                -x[0] - (theta1 + damping) * x[1],
+                -x[1],
+            ]
+        a11, a12, a22, b1, b2 = forms(h, u, g, p, x, size, axis)
+        first, second = 1.1 * a11, 1.1 * a22
+        determinant = first * second - a12 * a12
+        alpha = (b1 * second - a12 * b2) / determinant
+        beta = (first * b2 - a12 * b1) / determinant
+        p = [alpha * g[a] + beta * p[a] for a in range(size)]
+        x = [x[a] + p[a] for a in range(size)]
+    return x
 
 
 def finish_kernel(
@@ -294,31 +323,7 @@
         h[a][b] = h[b][a] = table_ref[place]
     u = [table_ref[7], table_ref[8], table_ref[3]]
     theta0, theta1, phi, damping = [table_ref[9 + a] for a in range(4)]
-    one = jnp.ones_like(theta0)
-    a11 = jnp.sum(h[0][0], axis=0, keepdims=True)
-    b1 = jnp.sum(u[0], axis=0, keepdims=True)
-    alpha = b1 / (1.1 * a11)
-    p = [alpha * one]
-    x = [alpha * one]
-    for size in (2, 3):
-        zero = jnp.zeros_like(one)
-        x = x + [zero]
-        p = p + [zero]
-        if size == 2:
-            g = [one - (theta0 + damping) * x[0], -x[0]]
-        else:
-            g = [
-                one - (theta0 + damping) * x[0] - phi * x[1],
-                -x[0] - (theta1 + damping) * x[1],
-                -x[1],
-            ]
-        a11, a12, a22, b1, b2 = forms(h, u, g, p, x, size)
-        first, second = 1.1 * a11, 1.1 * a22
-        determinant = first * second - a12 * a12
-        alpha = (b1 * second - a12 * b2) / determinant
-        beta = (first * b2 - a12 * b1) / determinant
-        p = [alpha * g[a] + beta * p[a] for a in range(size)]
-        x = [x[a] + p[a] for a in range(size)]
+    x = descend(h, u, theta0, theta1, phi, damping, 0)
     mix_ref[0] = x[0] - theta0 * x[1] + (theta0 * theta1 - phi) * x[2]
     mix_ref[1] = x[1] - theta1 * x[2]
     mix_ref[2] = x[2]
@@ -362,6 +367,346 @@
     res_copy.wait()
 
 
+def lane_limits(limits, rank, width):
+    lane = lax.broadcasted_iota(jnp.int32, (1, width), 1)
+    limit = jnp.zeros((1, width), jnp.int32)
+    for p, value in enumerate(limits):
+        limit = jnp.where(lane >= p * rank, value, limit)
+    return (lax.rem(lane, rank) < limit).astype(F32)
+
+
+def packed_gram(real, imag):
+    width = real.shape[1]
+    both = jnp.concatenate([real, imag], axis=0)
+    upper = dot_t(both, both)
+    lower = dot_t(real, imag) - dot_t(imag, real)
+    row = lax.broadcasted_iota(jnp.int32, (width, width), 0)
+    column = lax.broadcasted_iota(jnp.int32, (width, width), 1)
+    return jnp.where(row <= column, upper, lower).astype(BF16)
+
+
+def unpacked_gram(packed):
+    width = packed.shape[1]
+    here = packed.astype(F32)
+    there = here.T
+    row = lax.broadcasted_iota(jnp.int32, (width, width), 0)
+    column = lax.broadcasted_iota(jnp.int32, (width, width), 1)
+    real = jnp.where(row <= column, here, there)
+    imag = jnp.where(row > column, here, jnp.where(row < column, -there, 0.0))
+    return real.astype(BF16), imag.astype(BF16)
+
+
+def gather_start(
+    rank, n, here_ref, mine_ref, ranks_hbm, data_hbm, left_hbm, right_hbm, *refs
+):
+    outs, (ranks_ref, data_ref, left_ref, right_ref, back_ref, sem) = refs[:-6], refs[-6:]
+    pairs = [
+        (left_hbm, left_ref), (data_hbm, data_ref), (ranks_hbm, ranks_ref),
+        (right_hbm, right_ref),
+    ]
+    copies = [
+        pltpu.make_async_copy(source, target, sem.at[k])
+        for k, (source, target) in enumerate(pairs)
+    ]
+    for copy in copies:
+        copy.start()
+    for copy in copies[:3]:
+        copy.wait()
+    width = left_ref.shape[2]
+    s = data_ref.shape[2]
+    q = s // n
+    here = here_ref[0]
+    keep = lane_limits([ranks_ref[here, p] for p in range(n)], rank, width).astype(BF16)
+    real, imag = left_ref[0] * keep, left_ref[1] * keep
+    both = side(data_ref[0], data_ref[1])
+    first, second = dot_t(both, real), dot_t(both, imag)
+    back_ref[0] = (first[:s] + second[s:]).astype(BF16)
+    back_ref[1] = (first[s:] - second[:s]).astype(BF16)
+    gram = packed_gram(real, imag)
+    for out in outs:
+        out[0:width, :] = gram
+    copies[3].wait()
+    keep = lane_limits([ranks_ref[p, here] for p in range(n)], rank, width).astype(BF16)
+    gram = packed_gram(right_ref[0] * keep, right_ref[1] * keep)
+    z, x = lax.div(here, 2), lax.rem(here, 2)
+    for k, out in enumerate(outs):
+        out[width : 2 * width, :] = gram
+        base = 2 * lax.rem(z + k, n // 2)
+        for block, target in enumerate([base + 1 - x, base + x]):
+            rows = pl.ds(pl.multiple_of(target * q, q), q)
+            place = 2 * width + 2 * q * block
+            out[place : place + q, :] = back_ref[0, rows, :]
+            out[place + q : place + 2 * q, :] = back_ref[1, rows, :]
+
+
+def swap_tiles(rank, source, target):
+    n, rows, width = source.shape
+    per = 128 // rank
+    lane = lax.div(lax.broadcasted_iota(jnp.int32, (rows, 128), 1), rank)
+    for g in range(n // per):
+        for h in range(width // 128):
+            ins = [source[per * g + a, :, 128 * h : 128 * h + 128] for a in range(per)]
+            for b in range(per):
+                out = None
+                for a in range(per):
+                    shift = (a - b) * rank % 128
+                    piece = pltpu.roll(ins[a], shift, 1) if shift else ins[a]
+                    out = piece if out is None else jnp.where(lane == a, piece, out)
+                target[per * h + b, :, 128 * g : 128 * g + 128] = out
+
+
+def apply_tiles(gram_ref, source, target):
+    n, rows, _ = source.shape
+    q = rows // 2
+    for j in range(n):
+        high, low = split(source[j])
+        vector = jnp.concatenate([high, low], axis=0)
+        real, imag = dot(vector, gram_ref[0, j]), dot(vector, gram_ref[1, j])
+        real = real[:rows] + real[rows:]
+        imag = imag[:rows] + imag[rows:]
+        target[j, 0:q, :] = real[:q] + imag[q:]
+        target[j, q:rows, :] = real[q:] - imag[:q]
+
+
+def inner_tiles(first, second):
+    n, rows, _ = first.shape
+    total = first[0] * second[0]
+    for j in range(1, n):
+        total = total + first[j] * second[j]
+    total = jnp.sum(total, axis=1, keepdims=True)
+    return total[: rows // 2] + total[rows // 2 :]
+
+
+def take_off(target, terms):
+    scales = [jnp.concatenate([scale, scale], axis=0) for scale, _ in terms]
+    for j in range(target.shape[0]):
+        value = target[j]
+        for scale, (_, other) in zip(scales, terms):
+            value = value - scale * other[j]
+        target[j] = value
+
+
+def chain_kernel(
+    rank, n, here_ref, freq_ref, *refs
+):
+    tiles = refs[:n]
+    b_ref, c_ref, stats_ref, left_ref, right_ref, one_ref, two_ref = refs[n:]
+    width = tiles[0].shape[1]
+    q = stats_ref.shape[0]
+    here = here_ref[0]
+    z, x = lax.div(here, 2), lax.rem(here, 2)
+    half = n // 2
+    for k in range(half):
+        base = 2 * lax.rem(z + half - k, half)
+        for other in range(2):
+            ref = tiles[k + half * other]
+            at = pl.ds(base + (1 - x if other else x), 1)
+            for place, gram_ref in enumerate((left_ref, right_ref)):
+                real, imag = unpacked_gram(ref[place * width : (place + 1) * width, :])
+                gram_ref[0, at] = real[None]
+                gram_ref[1, at] = imag[None]
+            start = 2 * width + (0 if other else 2 * q)
+            one_ref[at] = ref[start : start + 2 * q, :].astype(F32)[None]
+    b0, b1, b2 = b_ref.at[0], b_ref.at[1], b_ref.at[2]
+    c0, c1, c2 = c_ref.at[0], c_ref.at[1], c_ref.at[2]
+    swap_tiles(rank, one_ref, b0)
+    apply_tiles(right_ref, b0, two_ref)
+    m00 = inner_tiles(b0, two_ref)
+    swap_tiles(rank, two_ref, c0)
+    apply_tiles(left_ref, c0, one_ref)
+    n00 = inner_tiles(c0, one_ref)
+    theta0 = ratio(n00, m00)
+    swap_tiles(rank, one_ref, b1)
+    take_off(b1, [(theta0, b0)])
+    apply_tiles(right_ref, b1, two_ref)
+    m11 = inner_tiles(b1, two_ref)
+    m01 = inner_tiles(b0, two_ref)
+    swap_tiles(rank, two_ref, c1)
+    apply_tiles(left_ref, c1, one_ref)
+    n11 = inner_tiles(c1, one_ref)
+    n01 = inner_tiles(c0, one_ref)
+    theta1 = ratio(n11, m11)
+    phi = ratio(n01, m00)
+    swap_tiles(rank, one_ref, b2)
+    take_off(b2, [(theta1, b1), (phi, b0)])
+    apply_tiles(right_ref, b2, two_ref)
+    m02 = inner_tiles(b0, two_ref)
+    m12 = inner_tiles(b1, two_ref)
+    m22 = inner_tiles(b2, two_ref)
+    swap_tiles(rank, two_ref, c2)
+    apply_tiles(left_ref, c2, one_ref)
+    n02 = inner_tiles(c0, one_ref)
+    n12 = inner_tiles(c1, one_ref)
+    n22 = inner_tiles(c2, one_ref)
+    damping = 0.1 + 0.9 * freq_ref[0].astype(F32) / 229.0
+    values = [
+        n00 + damping * m00, n01 + damping * m01, n02 + damping * m02,
+        n11 + damping * m11, n12 + damping * m12, n22 + damping * m22,
+        m00, m01, m02, theta0, theta1, phi,
+    ]
+    lane = lax.broadcasted_iota(jnp.int32, stats_ref.shape, 1)
+    block = jnp.full(stats_ref.shape, damping)
+    for place, value in enumerate(values):
+        block = jnp.where(lane == place, value, block)
+    stats_ref[...] = block
+
+
+def mix_kernel(rank, stats_refs, b_ref, c_ref, out_ref):
+    blocks = [ref[...] for ref in stats_refs]
+    lane = lax.broadcasted_iota(jnp.int32, blocks[0].shape, 1)
+    where_f = [lane == f for f in range(len(blocks))]
+
+    def pick(place):
+        value = jnp.zeros_like(blocks[0])
+        for f, block in enumerate(blocks):
+            shift = (f - place) % 128
+            value = jnp.where(where_f[f], pltpu.roll(block, shift, 1) if shift else block, value)
+        return value
+
+    h = [[None] * 3 for _ in range(3)]
+    for place, (a, b) in enumerate([(0, 0), (0, 1), (0, 2), (1, 1), (1, 2), (2, 2)]):
+        h[a][b] = h[b][a] = pick(place)
+    u = [pick(6), pick(7), pick(8)]
+    theta0, theta1, phi, damping = pick(9), pick(10), pick(11), pick(12)
+    x = descend(h, u, theta0, theta1, phi, damping, 1)
+    n, rows, _ = b_ref.shape[1:]
+    scales = []
+    for value in x:
+        own = jnp.sum(jnp.where(lane == 0, value, 0.0), axis=1, keepdims=True)
+        scales.append(jnp.concatenate([own, own], axis=0))
+    for j in range(n):
+        for place, ref in enumerate((b_ref, c_ref)):
+            value = scales[0] * ref[0, j] + scales[1] * ref[1, j] + scales[2] * ref[2, j]
+            out_ref[j, place * rows : (place + 1) * rows, :] = value.astype(BF16)
+
+
+def home_mix(rank, nfreq, data_hbm, left_hbm, right_hbm, *refs):
+    stats_refs = refs[:nfreq]
+    b_ref, c_ref, out_ref, data_ref, left_ref, right_ref, sem = refs[nfreq:]
+    pairs = [(right_hbm, right_ref), (left_hbm, left_ref), (data_hbm, data_ref)]
+    copies = [
+        pltpu.make_async_copy(source, target, sem.at[k])
+        for k, (source, target) in enumerate(pairs)
+    ]
+    for copy in copies:
+        copy.start()
+    mix_kernel(rank, stats_refs, b_ref, c_ref, out_ref)
+    for copy in copies:
+        copy.wait()
+
+
+def dot_nt(a, b):
+    return lax.dot_general(a, b, (((1,), (1,)), ((), ())), preferred_element_type=F32)
+
+
+def home_kernel(
+    rank, recv_ref, data_ref, left_ref, right_ref, wave_hbm, res_hbm, wave_ref, res_ref, sem
+):
+    n, rows, width = recv_ref.shape
+    q = rows // 4
+    s = n * q
+
+    def plain(factor_ref, place):
+        real = recv_ref[:, place * q : (place + 1) * q, :].reshape(s, width)
+        imag = recv_ref[:, (place + 1) * q : (place + 2) * q, :].reshape(s, width)
+        both = jnp.concatenate([real, imag], axis=0)
+        first, second = dot_nt(factor_ref[0], both), dot_nt(factor_ref[1], both)
+        return first[:, :s] - second[:, s:], first[:, s:] + second[:, :s]
+
+    wave_ref[0], wave_ref[1] = plain(right_ref, 0)
+    wave_copy = pltpu.make_async_copy(wave_ref, wave_hbm, sem.at[0])
+    wave_copy.start()
+    real, imag = plain(left_ref, 2)
+    res_ref[0] = data_ref[0].astype(F32) - real
+    res_ref[1] = data_ref[1].astype(F32) - imag
+    res_copy = pltpu.make_async_copy(res_ref, res_hbm, sem.at[1])
+    res_copy.start()
+    wave_copy.wait()
+    res_copy.wait()
+
+
+def by_source(data, left, right, ranks, freq_index, ntile, nfreq, here, mine):
+    width = left.shape[2]
+    rank = width // ntile
+    s = data.shape[2]
+    q = s // ntile
+    half = ntile // 2
+    room = (16 << 20) + 64 * width * width
+
+    def like(value):
+        return jax.ShapeDtypeStruct(value.shape, value.dtype)
+
+    def call(kernel, specs, args, outs, scratch=(), target=VMEM):
+        return pl.pallas_call(
+            kernel,
+            out_shape=outs,
+            in_specs=specs,
+            out_specs=[target] * len(outs),
+            scratch_shapes=scratch,
+            compiler_params=pltpu.CompilerParams(vmem_limit_bytes=room),
+        )(*args)
+
+    def along(shift):
+        return [
+            (2 * z + x, 2 * ((z + shift) % half) + x) for z in range(half) for x in range(2)
+        ]
+
+    across = [(t, t ^ 1) for t in range(ntile)]
+    packet = jax.ShapeDtypeStruct((2 * width + 4 * q, width), BF16)
+    packets = call(
+        functools.partial(gather_start, rank, ntile), [SMEM] * 2 + [HBM] * 4,
+        (here, mine, ranks, data, left, right), (packet,) * half,
+        [
+            pltpu.SMEM(ranks.shape, jnp.int32),
+            pltpu.VMEM(data.shape, BF16),
+            pltpu.VMEM(left.shape, BF16),
+            pltpu.VMEM(right.shape, BF16),
+            pltpu.VMEM((2, s, width), BF16),
+            pltpu.SemaphoreType.DMA((4,)),
+        ],
+    )
+    same = [packets[0]] + [
+        lax.ppermute(packets[k], "tcol", along(k)) for k in range(1, half)
+    ]
+    other = [lax.ppermute(value, "tcol", across) for value in same]
+    vectors = jax.ShapeDtypeStruct((3, ntile, 2 * q, width), F32)
+    grams = pltpu.VMEM((2, ntile, width, width), BF16)
+    vector = pltpu.VMEM((ntile, 2 * q, width), F32)
+    b, c, stats = call(
+        functools.partial(chain_kernel, rank, ntile), [SMEM] * 2 + [VMEM] * ntile,
+        (here, freq_index, *same, *other),
+        (vectors, vectors, jax.ShapeDtypeStruct((q, 128), F32)),
+        [grams, grams, vector, vector],
+    )
+    gathered = stats[None]
+    step = 1
+    while step < nfreq:
+        pairs = [(f, f ^ step) for f in range(nfreq)]
+        gathered = jnp.concatenate([gathered, lax.ppermute(gathered, "freq", pairs)], axis=0)
+        step *= 2
+    out, data_in, left_in, right_in = call(
+        functools.partial(home_mix, rank, nfreq), [HBM] * 3 + [VMEM] * (nfreq + 2),
+        (data, left, right, *[gathered[f] for f in range(nfreq)], b, c),
+        (
+            jax.ShapeDtypeStruct((ntile, 4 * q, width), BF16),
+            like(data), like(left), like(right),
+        ),
+        [pltpu.SemaphoreType.DMA((3,))],
+    )
+    back = lax.all_to_all(out, "tcol", 0, 0, tiled=True)
+    shape = jax.ShapeDtypeStruct(data.shape, F32)
+    return call(
+        functools.partial(home_kernel, rank), [VMEM] * 4, (back, data_in, left_in, right_in),
+        (shape, shape),
+        [
+            pltpu.VMEM(shape.shape, F32),
+            pltpu.VMEM(shape.shape, F32),
+            pltpu.SemaphoreType.DMA((2,)),
+        ],
+        HBM,
+    )
+
+
 def body(data, left_factor, right_factor, ranks, freq_index):
     ntile = lax.axis_size("tcol")
     nfreq = lax.axis_size("freq")
@@ -375,6 +720,10 @@
     width = left.shape[2]
     rank = width // ntile
     s = data.shape[2]
+    fits = s % (16 * ntile) == 0 and width % 128 == 0 and 128 % rank == 0
+    if fits and nfreq & (nfreq - 1) == 0 and ntile * width * width <= 1 << 20:
+        wave, res = by_source(data, left, right, ranks, freq_index, ntile, nfreq, here, mine)
+        return wave[None], res[None]
     share = -(-EARLY // ntile)
     height = -(-(LATE + share) // 8) * 8
     field = jax.ShapeDtypeStruct((width, 2 * s), F32)

time: 83.8 us -> 72.7 us (0.87)
  blocking collectives: 74.4 us -> 17.1 us
  waiting for transfers between devices: 0 us -> 30.5 us
  starting transfers between devices: 0 us -> 13.9 us
  Pallas kernels: 7.67 us -> 9.63 us
    all_to_all x7 -> x1, blocking collectives: 74.4 us -> 17.1 us  [by_source(): back = lax.all_to_all(out, 'tcol', 0, 0, tiled=True)]
    ppermute x0 -> x9, waiting for transfers between devices: none -> 30.5 us  [the longest x3 14.7 us: by_source(): lax.ppermute(packets[k], 'tcol', along(k))]
    ppermute x0 -> x9, starting transfers between devices: none -> 13.9 us  [the longest x3 7.04 us: by_source(): lax.ppermute(packets[k], 'tcol', along(k))]
    pallas_call x8 -> x4, Pallas kernels: 7.67 us -> 9.63 us  [call(): pl.pallas_call(kernel, out_shape=outs, in_specs=specs, out_specs=[target]...]
  transfers between devices with their start and end apart: 0 -> 9, of which waited for: 0 -> 6; matrix products, arithmetic and copies ran while one was open for 0% -> 0% of each run, Pallas kernels for 0% -> 0%
where the time goes in v4:
time: 72.7 us; the launch traced here: 72.5 us
  waiting for transfers between devices  30.5 us (42%)
  blocking collectives  17.1 us (24%)
  starting transfers between devices  13.9 us (19%)
  Pallas kernels  9.63 us (13%)
  between operations  1.34 us (2%)
    all_to_all x1, blocking collectives, by_source(): back = lax.all_to_all(out, 'tcol', 0, 0, tiled=True)  17.1 us
    ppermute x3, waiting for transfers between devices, by_source(): lax.ppermute(packets[k], 'tcol', along(k))  14.7 us
    ppermute x4, waiting for transfers between devices, by_source(): other = [lax.ppermute(value, 'tcol', across) for value in same]  12.5 us
    pallas_call x4, Pallas kernels, call(): pl.pallas_call(kernel, out_shape=outs, in_specs=specs, out_specs=[target]...  9.63 us
    ppermute x3, starting transfers between devices, by_source(): lax.ppermute(packets[k], 'tcol', along(k))  7.04 us
    ppermute x4, starting transfers between devices, by_source(): other = [lax.ppermute(value, 'tcol', across) for value in same]  5.22 us
    ppermute x2, waiting for transfers between devices, by_source(): lax.ppermute(gathered, 'freq', pairs)  3.38 us
    ppermute x2, starting transfers between devices, by_source(): lax.ppermute(gathered, 'freq', pairs)  1.59 us
  transfers between devices with their start and end apart: 9, of which 6 were waited for; matrix products, arithmetic and copies ran while one was open for 0% of the time, Pallas kernels for 0%

profile of v4, /device:TPU:0, one launch (start us, length us, event | category | flops | bytes accessed | tf_op | source)
XLA Modules:
  0.0 72.5 jit_solution(16673425675233231010)
XLA Ops:
  0.6 2.3 %shard_map.68 = (bf16[576,256]{1,0:T(8,128)(2,1)S(1)}, bf16[576,256]{1,0:T(8,128)(2,1)S(1)}, bf16[576,256]{1,0:T(8,128)(2,1)S(1)}, bf16[576,256]{1,0:T(8,128)(2,1)S(1)}) custom-call(s32[1]{0:T(128)} %bitcast.3.here_ref, s32[1]{0:T(128)} %bitcast.4.mine_ref, s32[8,8]{1,0:T(8,128)} %bitcast.23, bf16[2,512,128]{2,1,0:T(8,128)(2,1)} %bitcast.21, ...), custom_call_target="tpu_custom_call" | custom-call | tf_op jit(solution)/shard_map/pallas_call | solution.py:640
  2.9 3.1 %collective-permute-start = (bf16[576,256]{1,0:T(8,128)(2,1)S(1)}, bf16[576,256]{1,0:T(8,128)(2,1)S(1)}, u32[]{:S(2)}, u32[]{:S(2)}) collective-permute-start(bf16[576,256]{1,0:T(8,128)(2,1)S(1)} %get-tuple-element.16), channel_id=1, source_target_pairs={{0,2},{1,3},{2,4},{3,5},{4,6},{5,7},{6,0},{7,1},{8,10},{9,11},{10,... | collective-permute-start | bytes 884744 | tf_op jit(solution)/shard_map/ppermute | solution.py:669
  6.0 2.6 %collective-permute-start.1 = (bf16[576,256]{1,0:T(8,128)(2,1)S(1)}, bf16[576,256]{1,0:T(8,128)(2,1)S(1)}, u32[]{:S(2)}, u32[]{:S(2)}) collective-permute-start(bf16[576,256]{1,0:T(8,128)(2,1)S(1)} %get-tuple-element.17), channel_id=1, source_target_pairs={{0,4},{1,5},{2,6},{3,7},{4,0},{5,1},{6,2},{7,3},{8,12},{9,13},{10,... | collective-permute-start | bytes 884744 | tf_op jit(solution)/shard_map/ppermute | solution.py:669
  8.6 1.4 %collective-permute-start.2 = (bf16[576,256]{1,0:T(8,128)(2,1)S(1)}, bf16[576,256]{1,0:T(8,128)(2,1)S(1)}, u32[]{:S(2)}, u32[]{:S(2)}) collective-permute-start(bf16[576,256]{1,0:T(8,128)(2,1)S(1)} %get-tuple-element.18), channel_id=1, source_target_pairs={{0,6},{1,7},{2,0},{3,1},{4,2},{5,3},{6,4},{7,5},{8,14},{9,15},{10,... | collective-permute-start | bytes 884744 | tf_op jit(solution)/shard_map/ppermute | solution.py:669
  10.0 1.5 %collective-permute-start.3 = (bf16[576,256]{1,0:T(8,128)(2,1)S(1)}, bf16[576,256]{1,0:T(8,128)(2,1)S(1)}, u32[]{:S(2)}, u32[]{:S(2)}) collective-permute-start(bf16[576,256]{1,0:T(8,128)(2,1)S(1)} %get-tuple-element.15.refs_0_), channel_id=1, source_target_pairs={{0,1},{1,0},{2,3},{3,2},{4,5},{5,4},{6,7},{7,6},{8,9},{9,8},{10,11... | collective-permute-start | bytes 884744 | tf_op jit(solution)/shard_map/ppermute | solution.py:671
  11.5 4.6 %collective-permute-done.refs_1_ = bf16[576,256]{1,0:T(8,128)(2,1)S(1)} collective-permute-done((bf16[576,256]{1,0:T(8,128)(2,1)S(1)}, bf16[576,256]{1,0:T(8,128)(2,1)S(1)}, u32[]{:S(2)}, u32[]{:S(2)}) %collective-permute-start) | collective-permute-done | bytes 294944 | tf_op jit(solution)/shard_map/ppermute | solution.py:669
  16.0 1.7 %collective-permute-start.4 = (bf16[576,256]{1,0:T(8,128)(2,1)S(1)}, bf16[576,256]{1,0:T(8,128)(2,1)S(1)}, u32[]{:S(2)}, u32[]{:S(2)}) collective-permute-start(bf16[576,256]{1,0:T(8,128)(2,1)S(1)} %collective-permute-done.refs_1_), channel_id=1, source_target_pairs={{0,1},{1,0},{2,3},{3,2},{4,5},{5,4},{6,7},{7,6},{8,9},{9,8},{10,11... | collective-permute-start | bytes 884744 | tf_op jit(solution)/shard_map/ppermute | solution.py:671
  17.8 10.1 %collective-permute-done.1.refs_2_ = bf16[576,256]{1,0:T(8,128)(2,1)S(1)} collective-permute-done((bf16[576,256]{1,0:T(8,128)(2,1)S(1)}, bf16[576,256]{1,0:T(8,128)(2,1)S(1)}, u32[]{:S(2)}, u32[]{:S(2)}) %collective-permute-start.1) | collective-permute-done | bytes 294944 | tf_op jit(solution)/shard_map/ppermute | solution.py:669
  27.8 1.5 %collective-permute-start.5 = (bf16[576,256]{1,0:T(8,128)(2,1)S(1)}, bf16[576,256]{1,0:T(8,128)(2,1)S(1)}, u32[]{:S(2)}, u32[]{:S(2)}) collective-permute-start(bf16[576,256]{1,0:T(8,128)(2,1)S(1)} %collective-permute-done.1.refs_2_), channel_id=1, source_target_pairs={{0,1},{1,0},{2,3},{3,2},{4,5},{5,4},{6,7},{7,6},{8,9},{9,8},{10,11... | collective-permute-start | bytes 884744 | tf_op jit(solution)/shard_map/ppermute | solution.py:671
  29.3 0.0 collective-permute-done.2.refs_3_
  29.3 0.5 collective-permute-start.6
  30.5 0.0 collective-permute-done.3.refs_4_
  30.5 0.0 collective-permute-done.4.refs_5_
  30.5 7.2 %collective-permute-done.5.refs_6_ = bf16[576,256]{1,0:T(8,128)(2,1)S(1)} collective-permute-done((bf16[576,256]{1,0:T(8,128)(2,1)S(1)}, bf16[576,256]{1,0:T(8,128)(2,1)S(1)}, u32[]{:S(2)}, u32[]{:S(2)}) %collective-permute-start.5) | collective-permute-done | bytes 294944 | tf_op jit(solution)/shard_map/ppermute | solution.py:671
  37.7 5.3 %collective-permute-done.6.refs_7_ = bf16[576,256]{1,0:T(8,128)(2,1)S(1)} collective-permute-done((bf16[576,256]{1,0:T(8,128)(2,1)S(1)}, bf16[576,256]{1,0:T(8,128)(2,1)S(1)}, u32[]{:S(2)}, u32[]{:S(2)}) %collective-permute-start.6) | collective-permute-done | bytes 294944 | tf_op jit(solution)/shard_map/ppermute | solution.py:671
  43.0 4.7 %shard_map.69 = (f32[3,8,32,256]{3,2,1,0:T(8,128)S(1)}, f32[3,8,32,256]{3,2,1,0:T(8,128)S(1)}, f32[16,128]{1,0:T(8,128)S(1)}) custom-call(s32[1]{0:T(128)} %bitcast.3.here_ref, s32[1]{0:T(128)S(6)} %copy.7.freq_ref, bf16[576,256]{1,0:T(8,128)(2,1)S(1)} %get-tuple-element.15.refs_0_, bf16[576,256]{1,0:T(8,128)(2,1)S(1)} %collective-permute-done.refs_1_, ...), custom_call_target="tpu_custom_call" | custom-call | tf_op jit(solution)/shard_map/pallas_call | solution.py:640
  47.7 0.1 collective-permute-start.7
  47.8 1.2 %collective-permute-done.7 = f32[1,16,128]{2,1,0:T(8,128)S(1)} collective-permute-done((f32[1,16,128]{2,1,0:T(8,128)S(1)}, f32[1,16,128]{2,1,0:T(8,128)S(1)}, u32[]{:S(2)}, u32[]{:S(2)}) %collective-permute-start.7) | collective-permute-done | bytes 8224 | tf_op jit(solution)/shard_map/ppermute | solution.py:685
  49.0 1.5 %collective-permute-start.8 = (f32[2,16,128]{2,1,0:T(8,128)S(1)}, f32[2,16,128]{2,1,0:T(8,128)S(1)}, u32[]{:S(2)}, u32[]{:S(2)}) collective-permute-start(f32[2,16,128]{2,1,0:T(8,128)S(1)} %pad_maximum_fusion), channel_id=1, source_target_pairs={{0,16},{8,24},{16,0},{24,8},{1,17},{9,25},{17,1},{25,9},{2,18},{10... | collective-permute-start | bytes 49160 | tf_op jit(solution)/shard_map/ppermute | solution.py:685
  50.5 2.2 %collective-permute-done.8 = f32[2,16,128]{2,1,0:T(8,128)S(1)} collective-permute-done((f32[2,16,128]{2,1,0:T(8,128)S(1)}, f32[2,16,128]{2,1,0:T(8,128)S(1)}, u32[]{:S(2)}, u32[]{:S(2)}) %collective-permute-start.8) | collective-permute-done | bytes 16416 | tf_op jit(solution)/shard_map/ppermute | solution.py:685
  52.7 1.3 %shard_map.70 = (bf16[8,64,256]{2,1,0:T(8,128)(2,1)S(1)}, bf16[2,512,128]{2,1,0:T(8,128)(2,1)S(1)}, bf16[2,512,256]{2,1,0:T(8,128)(2,1)S(1)}, bf16[2,512,256]{2,1,0:T(8,128)(2,1)S(1)}) custom-call(bf16[2,512,128]{2,1,0:T(8,128)(2,1)} %bitcast.22, bf16[2,512,256]{2,1,0:T(8,128)(2,1)} %bitcast.18, bf16[2,512,256]{2,1,0:T(8,128)(2,1)} %bitcast.20, ...), custom_call_target="tpu_custom_call" | custom-call | tf_op jit(solution)/shard_map/pallas_call | solution.py:640
  54.0 17.1 %all_to_all.5.recv_ref = bf16[8,64,256]{2,1,0:T(8,128)(2,1)S(1)} all-to-all(bf16[8,64,256]{2,1,0:T(8,128)(2,1)S(1)} %get-tuple-element.22), channel_id=1, replica_groups=mesh['freq'=4,'tcol'=8] {'tcol'}, dimensions={0} | all-to-all | bytes 524288 | tf_op jit(solution)/shard_map/all_to_all | solution.py:696
  71.1 1.3 %shard_map.71 = (f32[2,512,128]{2,1,0:T(8,128)}, f32[2,512,128]{2,1,0:T(8,128)}) custom-call(bf16[8,64,256]{2,1,0:T(8,128)(2,1)S(1)} %all_to_all.5.recv_ref, bf16[2,512,128]{2,1,0:T(8,128)(2,1)S(1)} %get-tuple-element.23.data_ref, bf16[2,512,256]{2,1,0:T(8,128)(2,1)S(1)} %get-tuple-element.24.left_ref, bf16[2,512,256]{2,1,0:T(8,128)(2,1)S(1)} %get-tuple-element.25.right_ref), custom_call_target="tpu_custom_call" | custom-call | tf_op jit(solution)/shard_map/pallas_call | solution.py:640
  (2 shorter events, 0.0 us)
Async XLA Ops:
  2.9 13.1 %collective-permute-start = (bf16[576,256]{1,0:T(8,128)(2,1)S(1)}, bf16[576,256]{1,0:T(8,128)(2,1)S(1)}, u32[]{:S(2)}, u32[]{:S(2)}) collective-permute-start(bf16[576,256]{1,0:T(8,128)(2,1)S(1)} %get-tuple-element.16), channel_id=1, source_target_pairs={{0,2},{1,3},{2,4},{3,5},{4,6},{5,7},{6,0},{7,1},{8,10},{9,11},{10,... | collective-permute-start | bytes 884744 | tf_op jit(solution)/shard_map/ppermute | solution.py:669
  6.0 21.8 %collective-permute-start.1 = (bf16[576,256]{1,0:T(8,128)(2,1)S(1)}, bf16[576,256]{1,0:T(8,128)(2,1)S(1)}, u32[]{:S(2)}, u32[]{:S(2)}) collective-permute-start(bf16[576,256]{1,0:T(8,128)(2,1)S(1)} %get-tuple-element.17), channel_id=1, source_target_pairs={{0,4},{1,5},{2,6},{3,7},{4,0},{5,1},{6,2},{7,3},{8,12},{9,13},{10,... | collective-permute-start | bytes 884744 | tf_op jit(solution)/shard_map/ppermute | solution.py:669
  8.6 20.7 %collective-permute-start.2 = (bf16[576,256]{1,0:T(8,128)(2,1)S(1)}, bf16[576,256]{1,0:T(8,128)(2,1)S(1)}, u32[]{:S(2)}, u32[]{:S(2)}) collective-permute-start(bf16[576,256]{1,0:T(8,128)(2,1)S(1)} %get-tuple-element.18), channel_id=1, source_target_pairs={{0,6},{1,7},{2,0},{3,1},{4,2},{5,3},{6,4},{7,5},{8,14},{9,15},{10,... | collective-permute-start | bytes 884744 | tf_op jit(solution)/shard_map/ppermute | solution.py:669
  10.0 20.6 %collective-permute-start.3 = (bf16[576,256]{1,0:T(8,128)(2,1)S(1)}, bf16[576,256]{1,0:T(8,128)(2,1)S(1)}, u32[]{:S(2)}, u32[]{:S(2)}) collective-permute-start(bf16[576,256]{1,0:T(8,128)(2,1)S(1)} %get-tuple-element.15.refs_0_), channel_id=1, source_target_pairs={{0,1},{1,0},{2,3},{3,2},{4,5},{5,4},{6,7},{7,6},{8,9},{9,8},{10,11... | collective-permute-start | bytes 884744 | tf_op jit(solution)/shard_map/ppermute | solution.py:671
  16.0 14.5 %collective-permute-start.4 = (bf16[576,256]{1,0:T(8,128)(2,1)S(1)}, bf16[576,256]{1,0:T(8,128)(2,1)S(1)}, u32[]{:S(2)}, u32[]{:S(2)}) collective-permute-start(bf16[576,256]{1,0:T(8,128)(2,1)S(1)} %collective-permute-done.refs_1_), channel_id=1, source_target_pairs={{0,1},{1,0},{2,3},{3,2},{4,5},{5,4},{6,7},{7,6},{8,9},{9,8},{10,11... | collective-permute-start | bytes 884744 | tf_op jit(solution)/shard_map/ppermute | solution.py:671
  27.8 9.9 %collective-permute-start.5 = (bf16[576,256]{1,0:T(8,128)(2,1)S(1)}, bf16[576,256]{1,0:T(8,128)(2,1)S(1)}, u32[]{:S(2)}, u32[]{:S(2)}) collective-permute-start(bf16[576,256]{1,0:T(8,128)(2,1)S(1)} %collective-permute-done.1.refs_2_), channel_id=1, source_target_pairs={{0,1},{1,0},{2,3},{3,2},{4,5},{5,4},{6,7},{7,6},{8,9},{9,8},{10,11... | collective-permute-start | bytes 884744 | tf_op jit(solution)/shard_map/ppermute | solution.py:671
  29.3 13.7 %collective-permute-start.6 = (bf16[576,256]{1,0:T(8,128)(2,1)S(1)}, bf16[576,256]{1,0:T(8,128)(2,1)S(1)}, u32[]{:S(2)}, u32[]{:S(2)}) collective-permute-start(bf16[576,256]{1,0:T(8,128)(2,1)S(1)} %collective-permute-done.2.refs_3_), channel_id=1, source_target_pairs={{0,1},{1,0},{2,3},{3,2},{4,5},{5,4},{6,7},{7,6},{8,9},{9,8},{10,11... | collective-permute-start | bytes 884744 | tf_op jit(solution)/shard_map/ppermute | solution.py:671
  47.7 1.2 %collective-permute-start.7 = (f32[1,16,128]{2,1,0:T(8,128)S(1)}, f32[1,16,128]{2,1,0:T(8,128)S(1)}, u32[]{:S(2)}, u32[]{:S(2)}) collective-permute-start(f32[1,16,128]{2,1,0:T(8,128)S(1)} %bitcast.14), channel_id=1, source_target_pairs={{0,8},{8,0},{16,24},{24,16},{1,9},{9,1},{17,25},{25,17},{2,10},{10... | collective-permute-start | bytes 24584 | tf_op jit(solution)/shard_map/ppermute | solution.py:685
  49.0 3.7 %collective-permute-start.8 = (f32[2,16,128]{2,1,0:T(8,128)S(1)}, f32[2,16,128]{2,1,0:T(8,128)S(1)}, u32[]{:S(2)}, u32[]{:S(2)}) collective-permute-start(f32[2,16,128]{2,1,0:T(8,128)S(1)} %pad_maximum_fusion), channel_id=1, source_target_pairs={{0,16},{8,24},{16,0},{24,8},{1,17},{9,25},{17,1},{25,9},{2,18},{10... | collective-permute-start | bytes 49160 | tf_op jit(solution)/shard_map/ppermute | solution.py:685

commit v5 on v4

--- a/solution.py
+++ b/solution.py
@@ -396,10 +396,26 @@
     return real.astype(BF16), imag.astype(BF16)
 
 
+def offsets(half):
+    return sorted(range(1, half), key=lambda k: (min(k, half - k), k))
+
+
+def tile_parts(refs, half):
+    whole = refs[0].shape[0] - refs[0].shape[1]
+    parts = {0: (refs[0], refs[0], whole)}
+    order = offsets(half)
+    for place, k in enumerate(order[:-1]):
+        parts[k] = (refs[1 + place], refs[1 + place], whole)
+    parts[order[-1]] = (refs[-2], refs[-1], 0)
+    return [parts[k] for k in range(half)]
+
+
 def gather_start(
     rank, n, here_ref, mine_ref, ranks_hbm, data_hbm, left_hbm, right_hbm, *refs
 ):
-    outs, (ranks_ref, data_ref, left_ref, right_ref, back_ref, sem) = refs[:-6], refs[-6:]
+    ranks_ref, data_ref, left_ref, right_ref, back_ref, sem = refs[-6:]
+    half = n // 2
+    packets = tile_parts(refs[: half + 1], half)
     pairs = [
         (left_hbm, left_ref), (data_hbm, data_ref), (ranks_hbm, ranks_ref),
         (right_hbm, right_ref),
@@ -423,20 +439,20 @@
     back_ref[0] = (first[:s] + second[s:]).astype(BF16)
     back_ref[1] = (first[s:] - second[:s]).astype(BF16)
     gram = packed_gram(real, imag)
-    for out in outs:
-        out[0:width, :] = gram
+    for first, _, _ in packets:
+        first[0:width, :] = gram
     copies[3].wait()
     keep = lane_limits([ranks_ref[p, here] for p in range(n)], rank, width).astype(BF16)
     gram = packed_gram(right_ref[0] * keep, right_ref[1] * keep)
     z, x = lax.div(here, 2), lax.rem(here, 2)
-    for k, out in enumerate(outs):
-        out[width : 2 * width, :] = gram
-        base = 2 * lax.rem(z + k, n // 2)
+    for k, (first, second, place) in enumerate(packets):
+        second[place : place + width, :] = gram
+        base = 2 * lax.rem(z + k, half)
         for block, target in enumerate([base + 1 - x, base + x]):
             rows = pl.ds(pl.multiple_of(target * q, q), q)
-            place = 2 * width + 2 * q * block
-            out[place : place + q, :] = back_ref[0, rows, :]
-            out[place + q : place + 2 * q, :] = back_ref[1, rows, :]
+            place = width + 2 * q * block
+            first[place : place + q, :] = back_ref[0, rows, :]
+            first[place + q : place + 2 * q, :] = back_ref[1, rows, :]
 
 
 def swap_tiles(rank, source, target):
@@ -489,24 +505,25 @@
 def chain_kernel(
     rank, n, here_ref, freq_ref, *refs
 ):
-    tiles = refs[:n]
-    b_ref, c_ref, stats_ref, left_ref, right_ref, one_ref, two_ref = refs[n:]
-    width = tiles[0].shape[1]
+    half = n // 2
+    tiles = [tile_parts(refs[: half + 1], half), tile_parts(refs[half + 1 : n + 2], half)]
+    b_ref, c_ref, stats_ref, left_ref, right_ref, one_ref, two_ref = refs[n + 2 :]
+    width = refs[0].shape[1]
     q = stats_ref.shape[0]
     here = here_ref[0]
     z, x = lax.div(here, 2), lax.rem(here, 2)
-    half = n // 2
     for k in range(half):
         base = 2 * lax.rem(z + half - k, half)
         for other in range(2):
-            ref = tiles[k + half * other]
+            first, second, place = tiles[other][k]
             at = pl.ds(base + (1 - x if other else x), 1)
-            for place, gram_ref in enumerate((left_ref, right_ref)):
-                real, imag = unpacked_gram(ref[place * width : (place + 1) * width, :])
+            grams = (first[0:width, :], second[place : place + width, :])
+            for packed, gram_ref in zip(grams, (left_ref, right_ref)):
+                real, imag = unpacked_gram(packed)
                 gram_ref[0, at] = real[None]
                 gram_ref[1, at] = imag[None]
-            start = 2 * width + (0 if other else 2 * q)
-            one_ref[at] = ref[start : start + 2 * q, :].astype(F32)[None]
+            start = width + (0 if other else 2 * q)
+            one_ref[at] = first[start : start + 2 * q, :].astype(F32)[None]
     b0, b1, b2 = b_ref.at[0], b_ref.at[1], b_ref.at[2]
     c0, c1, c2 = c_ref.at[0], c_ref.at[1], c_ref.at[2]
     swap_tiles(rank, one_ref, b0)
@@ -652,10 +669,13 @@
         ]
 
     across = [(t, t ^ 1) for t in range(ntile)]
-    packet = jax.ShapeDtypeStruct((2 * width + 4 * q, width), BF16)
+    sizes = [2 * width + 4 * q] * (half - 1) + [width + 4 * q, width]
+    shifts = [0] + offsets(half)
+    shifts = shifts + shifts[-1:]
     packets = call(
         functools.partial(gather_start, rank, ntile), [SMEM] * 2 + [HBM] * 4,
-        (here, mine, ranks, data, left, right), (packet,) * half,
+        (here, mine, ranks, data, left, right),
+        [jax.ShapeDtypeStruct((size, width), BF16) for size in sizes],
         [
             pltpu.SMEM(ranks.shape, jnp.int32),
             pltpu.VMEM(data.shape, BF16),
@@ -666,14 +686,14 @@
         ],
     )
     same = [packets[0]] + [
-        lax.ppermute(packets[k], "tcol", along(k)) for k in range(1, half)
+        lax.ppermute(packet, "tcol", along(k)) for packet, k in zip(packets[1:], shifts[1:])
     ]
     other = [lax.ppermute(value, "tcol", across) for value in same]
     vectors = jax.ShapeDtypeStruct((3, ntile, 2 * q, width), F32)
     grams = pltpu.VMEM((2, ntile, width, width), BF16)
     vector = pltpu.VMEM((ntile, 2 * q, width), F32)
     b, c, stats = call(
-        functools.partial(chain_kernel, rank, ntile), [SMEM] * 2 + [VMEM] * ntile,
+        functools.partial(chain_kernel, rank, ntile), [SMEM] * 2 + [VMEM] * (ntile + 2),
         (here, freq_index, *same, *other),
         (vectors, vectors, jax.ShapeDtypeStruct((q, 128), F32)),
         [grams, grams, vector, vector],
@@ -720,7 +740,7 @@
     width = left.shape[2]
     rank = width // ntile
     s = data.shape[2]
-    fits = s % (16 * ntile) == 0 and width % 128 == 0 and 128 % rank == 0
+    fits = ntile % 4 == 0 and s % (16 * ntile) == 0 and width % 128 == 0 and 128 % rank == 0
     if fits and nfreq & (nfreq - 1) == 0 and ntile * width * width <= 1 << 20:
         wave, res = by_source(data, left, right, ranks, freq_index, ntile, nfreq, here, mine)
         return wave[None], res[None]

time: 72.7 us -> 67.2 us (0.924)
  waiting for transfers between devices: 30.5 us -> 17.6 us
  starting transfers between devices: 13.9 us -> 23.3 us
  blocking collectives: 17.1 us -> 15.1 us
    ppermute x4 -> x5, waiting for transfers between devices: 12.5 us -> 2.84 us  [by_source(): other = [lax.ppermute(value, 'tcol', across) for value in same]]
    ppermute x3 -> x4, starting transfers between devices: 7.04 us -> 14 us  [by_source(): lax.ppermute(packet, 'tcol', along(k))]
    ppermute x3 -> x4, waiting for transfers between devices: 14.7 us -> 11.4 us  [by_source(): lax.ppermute(packet, 'tcol', along(k))]
    ppermute x4 -> x5, starting transfers between devices: 5.22 us -> 7.67 us  [by_source(): other = [lax.ppermute(value, 'tcol', across) for value in same]]
    all_to_all x1, blocking collectives: 17.1 us -> 15.1 us  [by_source(): back = lax.all_to_all(out, 'tcol', 0, 0, tiled=True)]
  transfers between devices with their start and end apart: 9 -> 11, of which waited for: 6 -> 6; matrix products, arithmetic and copies ran while one was open for 0% -> 0% of each run, Pallas kernels for 0% -> 0%
where the time goes in v5:
time: 67.2 us; the launch traced here: 67 us
  starting transfers between devices  23.3 us (35%)
  waiting for transfers between devices  17.6 us (26%)
  blocking collectives  15.1 us (22%)
  Pallas kernels  9.64 us (14%)
  between operations  1.34 us (2%)
    all_to_all x1, blocking collectives, by_source(): back = lax.all_to_all(out, 'tcol', 0, 0, tiled=True)  15.1 us
    ppermute x4, starting transfers between devices, by_source(): lax.ppermute(packet, 'tcol', along(k))  14 us
    ppermute x4, waiting for transfers between devices, by_source(): lax.ppermute(packet, 'tcol', along(k))  11.4 us
    pallas_call x4, Pallas kernels, call(): pl.pallas_call(kernel, out_shape=outs, in_specs=specs, out_specs=[target]...  9.64 us
    ppermute x5, starting transfers between devices, by_source(): other = [lax.ppermute(value, 'tcol', across) for value in same]  7.67 us
    ppermute x2, waiting for transfers between devices, by_source(): lax.ppermute(gathered, 'freq', pairs)  3.39 us
    ppermute x5, waiting for transfers between devices, by_source(): other = [lax.ppermute(value, 'tcol', across) for value in same]  2.84 us
    ppermute x2, starting transfers between devices, by_source(): lax.ppermute(gathered, 'freq', pairs)  1.58 us
  transfers between devices with their start and end apart: 11, of which 6 were waited for; matrix products, arithmetic and copies ran while one was open for 0% of the time, Pallas kernels for 0%

profile of v5, /device:TPU:0, one launch (start us, length us, event | category | flops | bytes accessed | tf_op | source)
XLA Modules:
  0.0 67.0 jit_solution(4148178000928701993)
XLA Ops:
  0.6 2.3 %shard_map.68 = (bf16[576,256]{1,0:T(8,128)(2,1)S(1)}, bf16[576,256]{1,0:T(8,128)(2,1)S(1)}, bf16[576,256]{1,0:T(8,128)(2,1)S(1)}, bf16[320,256]{1,0:T(8,128)(2,1)S(1)}, bf16[256,256]{1,0:T(8,128)(2,1)S(1)}) custom-call(s32[1]{0:T(128)} %bitcast.3.here_ref, s32[1]{0:T(128)} %bitcast.4.mine_ref, s32[8,8]{1,0:T(8,128)} %bitcast.23, ...), custom_call_target="tpu_custom_call" | custom-call | tf_op jit(solution)/shard_map/pallas_call | solution.py:657
  2.9 3.1 %collective-permute-start = (bf16[576,256]{1,0:T(8,128)(2,1)S(1)}, bf16[576,256]{1,0:T(8,128)(2,1)S(1)}, u32[]{:S(2)}, u32[]{:S(2)}) collective-permute-start(bf16[576,256]{1,0:T(8,128)(2,1)S(1)} %get-tuple-element.17), channel_id=1, source_target_pairs={{0,2},{1,3},{2,4},{3,5},{4,6},{5,7},{6,0},{7,1},{8,10},{9,11},{10,... | collective-permute-start | bytes 884744 | tf_op jit(solution)/shard_map/ppermute | solution.py:689
  6.0 2.1 %collective-permute-start.1 = (bf16[576,256]{1,0:T(8,128)(2,1)S(1)}, bf16[576,256]{1,0:T(8,128)(2,1)S(1)}, u32[]{:S(2)}, u32[]{:S(2)}) collective-permute-start(bf16[576,256]{1,0:T(8,128)(2,1)S(1)} %get-tuple-element.18), channel_id=1, source_target_pairs={{0,6},{1,7},{2,0},{3,1},{4,2},{5,3},{6,4},{7,5},{8,14},{9,15},{10,... | collective-permute-start | bytes 884744 | tf_op jit(solution)/shard_map/ppermute | solution.py:689
  8.1 1.0 %collective-permute-start.2 = (bf16[320,256]{1,0:T(8,128)(2,1)S(1)}, bf16[320,256]{1,0:T(8,128)(2,1)S(1)}, u32[]{:S(2)}, u32[]{:S(2)}) collective-permute-start(bf16[320,256]{1,0:T(8,128)(2,1)S(1)} %get-tuple-element.19), channel_id=1, source_target_pairs={{0,4},{1,5},{2,6},{3,7},{4,0},{5,1},{6,2},{7,3},{8,12},{9,13},{10,... | collective-permute-start | bytes 491528 | tf_op jit(solution)/shard_map/ppermute | solution.py:689
  9.1 1.5 %collective-permute-start.4 = (bf16[576,256]{1,0:T(8,128)(2,1)S(1)}, bf16[576,256]{1,0:T(8,128)(2,1)S(1)}, u32[]{:S(2)}, u32[]{:S(2)}) collective-permute-start(bf16[576,256]{1,0:T(8,128)(2,1)S(1)} %get-tuple-element.16.refs_0_), channel_id=1, source_target_pairs={{0,1},{1,0},{2,3},{3,2},{4,5},{5,4},{6,7},{7,6},{8,9},{9,8},{10,11... | collective-permute-start | bytes 884744 | tf_op jit(solution)/shard_map/ppermute | solution.py:691
  10.6 5.4 %collective-permute-done.refs_1_ = bf16[576,256]{1,0:T(8,128)(2,1)S(1)} collective-permute-done((bf16[576,256]{1,0:T(8,128)(2,1)S(1)}, bf16[576,256]{1,0:T(8,128)(2,1)S(1)}, u32[]{:S(2)}, u32[]{:S(2)}) %collective-permute-start) | collective-permute-done | bytes 294944 | tf_op jit(solution)/shard_map/ppermute | solution.py:689
  16.0 1.7 %collective-permute-start.5 = (bf16[576,256]{1,0:T(8,128)(2,1)S(1)}, bf16[576,256]{1,0:T(8,128)(2,1)S(1)}, u32[]{:S(2)}, u32[]{:S(2)}) collective-permute-start(bf16[576,256]{1,0:T(8,128)(2,1)S(1)} %collective-permute-done.refs_1_), channel_id=1, source_target_pairs={{0,1},{1,0},{2,3},{3,2},{4,5},{5,4},{6,7},{7,6},{8,9},{9,8},{10,11... | collective-permute-start | bytes 884744 | tf_op jit(solution)/shard_map/ppermute | solution.py:691
  17.7 3.2 %collective-permute-done.1.refs_2_ = bf16[576,256]{1,0:T(8,128)(2,1)S(1)} collective-permute-done((bf16[576,256]{1,0:T(8,128)(2,1)S(1)}, bf16[576,256]{1,0:T(8,128)(2,1)S(1)}, u32[]{:S(2)}, u32[]{:S(2)}) %collective-permute-start.1) | collective-permute-done | bytes 294944 | tf_op jit(solution)/shard_map/ppermute | solution.py:689
  20.8 1.5 %collective-permute-start.6 = (bf16[576,256]{1,0:T(8,128)(2,1)S(1)}, bf16[576,256]{1,0:T(8,128)(2,1)S(1)}, u32[]{:S(2)}, u32[]{:S(2)}) collective-permute-start(bf16[576,256]{1,0:T(8,128)(2,1)S(1)} %collective-permute-done.1.refs_2_), channel_id=1, source_target_pairs={{0,1},{1,0},{2,3},{3,2},{4,5},{5,4},{6,7},{7,6},{8,9},{9,8},{10,11... | collective-permute-start | bytes 884744 | tf_op jit(solution)/shard_map/ppermute | solution.py:691
  22.3 7.9 %collective-permute-start.3 = (bf16[256,256]{1,0:T(8,128)(2,1)S(1)}, bf16[256,256]{1,0:T(8,128)(2,1)S(1)}, u32[]{:S(2)}, u32[]{:S(2)}) collective-permute-start(bf16[256,256]{1,0:T(8,128)(2,1)S(1)} %get-tuple-element.20), channel_id=1, source_target_pairs={{0,4},{1,5},{2,6},{3,7},{4,0},{5,1},{6,2},{7,3},{8,12},{9,13},{10,... | collective-permute-start | bytes 393224 | tf_op jit(solution)/shard_map/ppermute | solution.py:689
  30.2 1.5 %collective-permute-start.7 = (bf16[320,256]{1,0:T(8,128)(2,1)S(1)}, bf16[320,256]{1,0:T(8,128)(2,1)S(1)}, u32[]{:S(2)}, u32[]{:S(2)}) collective-permute-start(bf16[320,256]{1,0:T(8,128)(2,1)S(1)} %collective-permute-done.2.refs_3_), channel_id=1, source_target_pairs={{0,1},{1,0},{2,3},{3,2},{4,5},{5,4},{6,7},{7,6},{8,9},{9,8},{10,11... | collective-permute-start | bytes 491528 | tf_op jit(solution)/shard_map/ppermute | solution.py:691
  31.7 2.9 %collective-permute-done.3.refs_4_ = bf16[256,256]{1,0:T(8,128)(2,1)S(1)} collective-permute-done((bf16[256,256]{1,0:T(8,128)(2,1)S(1)}, bf16[256,256]{1,0:T(8,128)(2,1)S(1)}, u32[]{:S(2)}, u32[]{:S(2)}) %collective-permute-start.3) | collective-permute-done | bytes 131104 | tf_op jit(solution)/shard_map/ppermute | solution.py:689
  34.5 1.5 %collective-permute-start.8 = (bf16[256,256]{1,0:T(8,128)(2,1)S(1)}, bf16[256,256]{1,0:T(8,128)(2,1)S(1)}, u32[]{:S(2)}, u32[]{:S(2)}) collective-permute-start(bf16[256,256]{1,0:T(8,128)(2,1)S(1)} %collective-permute-done.3.refs_4_), channel_id=1, source_target_pairs={{0,1},{1,0},{2,3},{3,2},{4,5},{5,4},{6,7},{7,6},{8,9},{9,8},{10,11... | collective-permute-start | bytes 393224 | tf_op jit(solution)/shard_map/ppermute | solution.py:691
  36.7 2.8 %collective-permute-done.8.refs_9_ = bf16[256,256]{1,0:T(8,128)(2,1)S(1)} collective-permute-done((bf16[256,256]{1,0:T(8,128)(2,1)S(1)}, bf16[256,256]{1,0:T(8,128)(2,1)S(1)}, u32[]{:S(2)}, u32[]{:S(2)}) %collective-permute-start.8) | collective-permute-done | bytes 131104 | tf_op jit(solution)/shard_map/ppermute | solution.py:691
  39.5 0.0 collective-permute-done.4.refs_5_
  39.5 0.0 collective-permute-done.7.refs_8_
  39.5 4.8 %shard_map.69 = (f32[3,8,32,256]{3,2,1,0:T(8,128)S(1)}, f32[3,8,32,256]{3,2,1,0:T(8,128)S(1)}, f32[16,128]{1,0:T(8,128)S(1)}) custom-call(s32[1]{0:T(128)} %bitcast.3.here_ref, s32[1]{0:T(128)S(6)} %copy.7.freq_ref, bf16[576,256]{1,0:T(8,128)(2,1)S(1)} %get-tuple-element.16.refs_0_, bf16[576,256]{1,0:T(8,128)(2,1)S(1)} %collective-permute-done.refs_1_, ...), custom_call_target="tpu_custom_call" | custom-call | tf_op jit(solution)/shard_map/pallas_call | solution.py:657
  44.3 0.1 collective-permute-start.9
  44.4 1.2 %collective-permute-done.9 = f32[1,16,128]{2,1,0:T(8,128)S(1)} collective-permute-done((f32[1,16,128]{2,1,0:T(8,128)S(1)}, f32[1,16,128]{2,1,0:T(8,128)S(1)}, u32[]{:S(2)}, u32[]{:S(2)}) %collective-permute-start.9) | collective-permute-done | bytes 8224 | tf_op jit(solution)/shard_map/ppermute | solution.py:705
  45.5 1.5 %collective-permute-start.10 = (f32[2,16,128]{2,1,0:T(8,128)S(1)}, f32[2,16,128]{2,1,0:T(8,128)S(1)}, u32[]{:S(2)}, u32[]{:S(2)}) collective-permute-start(f32[2,16,128]{2,1,0:T(8,128)S(1)} %pad_maximum_fusion), channel_id=1, source_target_pairs={{0,16},{8,24},{16,0},{24,8},{1,17},{9,25},{17,1},{25,9},{2,18},{10... | collective-permute-start | bytes 49160 | tf_op jit(solution)/shard_map/ppermute | solution.py:705
  47.0 2.2 %collective-permute-done.10 = f32[2,16,128]{2,1,0:T(8,128)S(1)} collective-permute-done((f32[2,16,128]{2,1,0:T(8,128)S(1)}, f32[2,16,128]{2,1,0:T(8,128)S(1)}, u32[]{:S(2)}, u32[]{:S(2)}) %collective-permute-start.10) | collective-permute-done | bytes 16416 | tf_op jit(solution)/shard_map/ppermute | solution.py:705
  49.3 1.3 %shard_map.70 = (bf16[8,64,256]{2,1,0:T(8,128)(2,1)S(1)}, bf16[2,512,128]{2,1,0:T(8,128)(2,1)S(1)}, bf16[2,512,256]{2,1,0:T(8,128)(2,1)S(1)}, bf16[2,512,256]{2,1,0:T(8,128)(2,1)S(1)}) custom-call(bf16[2,512,128]{2,1,0:T(8,128)(2,1)} %bitcast.22, bf16[2,512,256]{2,1,0:T(8,128)(2,1)} %bitcast.18, bf16[2,512,256]{2,1,0:T(8,128)(2,1)} %bitcast.20, ...), custom_call_target="tpu_custom_call" | custom-call | tf_op jit(solution)/shard_map/pallas_call | solution.py:657
  50.6 15.1 %all_to_all.5.recv_ref = bf16[8,64,256]{2,1,0:T(8,128)(2,1)S(1)} all-to-all(bf16[8,64,256]{2,1,0:T(8,128)(2,1)S(1)} %get-tuple-element.24), channel_id=1, replica_groups=mesh['freq'=4,'tcol'=8] {'tcol'}, dimensions={0} | all-to-all | bytes 524288 | tf_op jit(solution)/shard_map/all_to_all | solution.py:716
  65.7 1.3 %shard_map.71 = (f32[2,512,128]{2,1,0:T(8,128)}, f32[2,512,128]{2,1,0:T(8,128)}) custom-call(bf16[8,64,256]{2,1,0:T(8,128)(2,1)S(1)} %all_to_all.5.recv_ref, bf16[2,512,128]{2,1,0:T(8,128)(2,1)S(1)} %get-tuple-element.25.data_ref, bf16[2,512,256]{2,1,0:T(8,128)(2,1)S(1)} %get-tuple-element.26.left_ref, bf16[2,512,256]{2,1,0:T(8,128)(2,1)S(1)} %get-tuple-element.27.right_ref), custom_call_target="tpu_custom_call" | custom-call | tf_op jit(solution)/shard_map/pallas_call | solution.py:657
  (5 shorter events, 0.0 us)
Async XLA Ops:
  2.9 13.0 %collective-permute-start = (bf16[576,256]{1,0:T(8,128)(2,1)S(1)}, bf16[576,256]{1,0:T(8,128)(2,1)S(1)}, u32[]{:S(2)}, u32[]{:S(2)}) collective-permute-start(bf16[576,256]{1,0:T(8,128)(2,1)S(1)} %get-tuple-element.17), channel_id=1, source_target_pairs={{0,2},{1,3},{2,4},{3,5},{4,6},{5,7},{6,0},{7,1},{8,10},{9,11},{10,... | collective-permute-start | bytes 884744 | tf_op jit(solution)/shard_map/ppermute | solution.py:689
  6.0 14.8 %collective-permute-start.1 = (bf16[576,256]{1,0:T(8,128)(2,1)S(1)}, bf16[576,256]{1,0:T(8,128)(2,1)S(1)}, u32[]{:S(2)}, u32[]{:S(2)}) collective-permute-start(bf16[576,256]{1,0:T(8,128)(2,1)S(1)} %get-tuple-element.18), channel_id=1, source_target_pairs={{0,6},{1,7},{2,0},{3,1},{4,2},{5,3},{6,4},{7,5},{8,14},{9,15},{10,... | collective-permute-start | bytes 884744 | tf_op jit(solution)/shard_map/ppermute | solution.py:689
  8.1 22.1 %collective-permute-start.2 = (bf16[320,256]{1,0:T(8,128)(2,1)S(1)}, bf16[320,256]{1,0:T(8,128)(2,1)S(1)}, u32[]{:S(2)}, u32[]{:S(2)}) collective-permute-start(bf16[320,256]{1,0:T(8,128)(2,1)S(1)} %get-tuple-element.19), channel_id=1, source_target_pairs={{0,4},{1,5},{2,6},{3,7},{4,0},{5,1},{6,2},{7,3},{8,12},{9,13},{10,... | collective-permute-start | bytes 491528 | tf_op jit(solution)/shard_map/ppermute | solution.py:689
  9.1 30.4 %collective-permute-start.4 = (bf16[576,256]{1,0:T(8,128)(2,1)S(1)}, bf16[576,256]{1,0:T(8,128)(2,1)S(1)}, u32[]{:S(2)}, u32[]{:S(2)}) collective-permute-start(bf16[576,256]{1,0:T(8,128)(2,1)S(1)} %get-tuple-element.16.refs_0_), channel_id=1, source_target_pairs={{0,1},{1,0},{2,3},{3,2},{4,5},{5,4},{6,7},{7,6},{8,9},{9,8},{10,11... | collective-permute-start | bytes 884744 | tf_op jit(solution)/shard_map/ppermute | solution.py:691
  16.0 23.6 %collective-permute-start.5 = (bf16[576,256]{1,0:T(8,128)(2,1)S(1)}, bf16[576,256]{1,0:T(8,128)(2,1)S(1)}, u32[]{:S(2)}, u32[]{:S(2)}) collective-permute-start(bf16[576,256]{1,0:T(8,128)(2,1)S(1)} %collective-permute-done.refs_1_), channel_id=1, source_target_pairs={{0,1},{1,0},{2,3},{3,2},{4,5},{5,4},{6,7},{7,6},{8,9},{9,8},{10,11... | collective-permute-start | bytes 884744 | tf_op jit(solution)/shard_map/ppermute | solution.py:691
  20.8 18.7 %collective-permute-start.6 = (bf16[576,256]{1,0:T(8,128)(2,1)S(1)}, bf16[576,256]{1,0:T(8,128)(2,1)S(1)}, u32[]{:S(2)}, u32[]{:S(2)}) collective-permute-start(bf16[576,256]{1,0:T(8,128)(2,1)S(1)} %collective-permute-done.1.refs_2_), channel_id=1, source_target_pairs={{0,1},{1,0},{2,3},{3,2},{4,5},{5,4},{6,7},{7,6},{8,9},{9,8},{10,11... | collective-permute-start | bytes 884744 | tf_op jit(solution)/shard_map/ppermute | solution.py:691
  22.3 12.2 %collective-permute-start.3 = (bf16[256,256]{1,0:T(8,128)(2,1)S(1)}, bf16[256,256]{1,0:T(8,128)(2,1)S(1)}, u32[]{:S(2)}, u32[]{:S(2)}) collective-permute-start(bf16[256,256]{1,0:T(8,128)(2,1)S(1)} %get-tuple-element.20), channel_id=1, source_target_pairs={{0,4},{1,5},{2,6},{3,7},{4,0},{5,1},{6,2},{7,3},{8,12},{9,13},{10,... | collective-permute-start | bytes 393224 | tf_op jit(solution)/shard_map/ppermute | solution.py:689
  30.2 9.3 %collective-permute-start.7 = (bf16[320,256]{1,0:T(8,128)(2,1)S(1)}, bf16[320,256]{1,0:T(8,128)(2,1)S(1)}, u32[]{:S(2)}, u32[]{:S(2)}) collective-permute-start(bf16[320,256]{1,0:T(8,128)(2,1)S(1)} %collective-permute-done.2.refs_3_), channel_id=1, source_target_pairs={{0,1},{1,0},{2,3},{3,2},{4,5},{5,4},{6,7},{7,6},{8,9},{9,8},{10,11... | collective-permute-start | bytes 491528 | tf_op jit(solution)/shard_map/ppermute | solution.py:691
  34.5 5.0 %collective-permute-start.8 = (bf16[256,256]{1,0:T(8,128)(2,1)S(1)}, bf16[256,256]{1,0:T(8,128)(2,1)S(1)}, u32[]{:S(2)}, u32[]{:S(2)}) collective-permute-start(bf16[256,256]{1,0:T(8,128)(2,1)S(1)} %collective-permute-done.3.refs_4_), channel_id=1, source_target_pairs={{0,1},{1,0},{2,3},{3,2},{4,5},{5,4},{6,7},{7,6},{8,9},{9,8},{10,11... | collective-permute-start | bytes 393224 | tf_op jit(solution)/shard_map/ppermute | solution.py:691
  44.3 1.2 %collective-permute-start.9 = (f32[1,16,128]{2,1,0:T(8,128)S(1)}, f32[1,16,128]{2,1,0:T(8,128)S(1)}, u32[]{:S(2)}, u32[]{:S(2)}) collective-permute-start(f32[1,16,128]{2,1,0:T(8,128)S(1)} %bitcast.14), channel_id=1, source_target_pairs={{0,8},{8,0},{16,24},{24,16},{1,9},{9,1},{17,25},{25,17},{2,10},{10... | collective-permute-start | bytes 24584 | tf_op jit(solution)/shard_map/ppermute | solution.py:705
  45.5 3.7 %collective-permute-start.10 = (f32[2,16,128]{2,1,0:T(8,128)S(1)}, f32[2,16,128]{2,1,0:T(8,128)S(1)}, u32[]{:S(2)}, u32[]{:S(2)}) collective-permute-start(f32[2,16,128]{2,1,0:T(8,128)S(1)} %pad_maximum_fusion), channel_id=1, source_target_pairs={{0,16},{8,24},{16,0},{24,8},{1,17},{9,25},{17,1},{25,9},{2,18},{10... | collective-permute-start | bytes 49160 | tf_op jit(solution)/shard_map/ppermute | solution.py:705

commit v6 on v5

--- a/solution.py
+++ b/solution.py
@@ -503,11 +503,20 @@
 
 
 def chain_kernel(
-    rank, n, here_ref, freq_ref, *refs
+    rank, n, here_ref, freq_ref, data_hbm, left_hbm, right_hbm, *refs
 ):
     half = n // 2
+    *refs, data_ref, home_left, home_right, gram_left, gram_right, one_ref, two_ref, sem = refs
+    pairs = [(right_hbm, home_right), (left_hbm, home_left), (data_hbm, data_ref)]
+    copies = [
+        pltpu.make_async_copy(source, target, sem.at[k])
+        for k, (source, target) in enumerate(pairs)
+    ]
+    for copy in copies:
+        copy.start()
     tiles = [tile_parts(refs[: half + 1], half), tile_parts(refs[half + 1 : n + 2], half)]
-    b_ref, c_ref, stats_ref, left_ref, right_ref, one_ref, two_ref = refs[n + 2 :]
+    b_ref, c_ref, stats_ref = refs[n + 2 :]
+    left_ref, right_ref = gram_left, gram_right
     width = refs[0].shape[1]
     q = stats_ref.shape[0]
     here = here_ref[0]
@@ -566,9 +575,12 @@
     for place, value in enumerate(values):
         block = jnp.where(lane == place, value, block)
     stats_ref[...] = block
-
-
-def mix_kernel(rank, stats_refs, b_ref, c_ref, out_ref):
+    for copy in copies:
+        copy.wait()
+
+
+def mix_kernel(nfreq, *refs):
+    stats_refs, (b_ref, c_ref, out_ref) = refs[:nfreq], refs[nfreq:]
     blocks = [ref[...] for ref in stats_refs]
     lane = lax.broadcasted_iota(jnp.int32, blocks[0].shape, 1)
     where_f = [lane == f for f in range(len(blocks))]
@@ -595,21 +607,6 @@
         for place, ref in enumerate((b_ref, c_ref)):
             value = scales[0] * ref[0, j] + scales[1] * ref[1, j] + scales[2] * ref[2, j]
             out_ref[j, place * rows : (place + 1) * rows, :] = value.astype(BF16)
-
-
-def home_mix(rank, nfreq, data_hbm, left_hbm, right_hbm, *refs):
-    stats_refs = refs[:nfreq]
-    b_ref, c_ref, out_ref, data_ref, left_ref, right_ref, sem = refs[nfreq:]
-    pairs = [(right_hbm, right_ref), (left_hbm, left_ref), (data_hbm, data_ref)]
-    copies = [
-        pltpu.make_async_copy(source, target, sem.at[k])
-        for k, (source, target) in enumerate(pairs)
-    ]
-    for copy in copies:
-        copy.start()
-    mix_kernel(rank, stats_refs, b_ref, c_ref, out_ref)
-    for copy in copies:
-        copy.wait()
 
 
 def dot_nt(a, b):
@@ -685,18 +682,27 @@
             pltpu.SemaphoreType.DMA((4,)),
         ],
     )
-    same = [packets[0]] + [
-        lax.ppermute(packet, "tcol", along(k)) for packet, k in zip(packets[1:], shifts[1:])
-    ]
-    other = [lax.ppermute(value, "tcol", across) for value in same]
+    same = [packets[0], lax.ppermute(packets[1], "tcol", along(shifts[1]))]
+    other = [lax.ppermute(packets[0], "tcol", across)]
+    for packet, k in zip(packets[2:], shifts[2:]):
+        if k == shifts[-1]:
+            packet, same[1] = lax.optimization_barrier((packet, same[1]))
+        else:
+            packet, other[0] = lax.optimization_barrier((packet, other[0]))
+        same.append(lax.ppermute(packet, "tcol", along(k)))
+    other = other + [lax.ppermute(value, "tcol", across) for value in same[1:]]
     vectors = jax.ShapeDtypeStruct((3, ntile, 2 * q, width), F32)
     grams = pltpu.VMEM((2, ntile, width, width), BF16)
     vector = pltpu.VMEM((ntile, 2 * q, width), F32)
-    b, c, stats = call(
-        functools.partial(chain_kernel, rank, ntile), [SMEM] * 2 + [VMEM] * (ntile + 2),
-        (here, freq_index, *same, *other),
-        (vectors, vectors, jax.ShapeDtypeStruct((q, 128), F32)),
-        [grams, grams, vector, vector],
+    b, c, stats, data_in, left_in, right_in = call(
+        functools.partial(chain_kernel, rank, ntile),
+        [SMEM] * 2 + [HBM] * 3 + [VMEM] * (ntile + 2),
+        (here, freq_index, data, left, right, *same, *other),
+        (
+            vectors, vectors, jax.ShapeDtypeStruct((q, 128), F32),
+            like(data), like(left), like(right),
+        ),
+        [grams, grams, vector, vector, pltpu.SemaphoreType.DMA((3,))],
     )
     gathered = stats[None]
     step = 1
@@ -704,14 +710,10 @@
         pairs = [(f, f ^ step) for f in range(nfreq)]
         gathered = jnp.concatenate([gathered, lax.ppermute(gathered, "freq", pairs)], axis=0)
         step *= 2
-    out, data_in, left_in, right_in = call(
-        functools.partial(home_mix, rank, nfreq), [HBM] * 3 + [VMEM] * (nfreq + 2),
-        (data, left, right, *[gathered[f] for f in range(nfreq)], b, c),
-        (
-            jax.ShapeDtypeStruct((ntile, 4 * q, width), BF16),
-            like(data), like(left), like(right),
-        ),
-        [pltpu.SemaphoreType.DMA((3,))],
+    (out,) = call(
+        functools.partial(mix_kernel, nfreq), [VMEM] * (nfreq + 2),
+        (*[gathered[f] for f in range(nfreq)], b, c),
+        (jax.ShapeDtypeStruct((ntile, 4 * q, width), BF16),),
     )
     back = lax.all_to_all(out, "tcol", 0, 0, tiled=True)
     shape = jax.ShapeDtypeStruct(data.shape, F32)

time: 67.2 us -> 67.7 us (level)
  waiting for transfers between devices: 17.6 us -> 21.6 us
  starting transfers between devices: 23.3 us -> 19.4 us
    ppermute x9, waiting for transfers between devices: 14.2 us -> 18.2 us  [the longest x3 8.67 us: by_source(): same.append(lax.ppermute(packet, 'tcol', along(k)))]
    ppermute x9, starting transfers between devices: 21.7 us -> 17.8 us  [the longest x3 8.39 us: by_source(): same.append(lax.ppermute(packet, 'tcol', along(k)))]
  transfers between devices with their start and end apart: 11 -> 11, of which waited for: 6 -> 7; matrix products, arithmetic and copies ran while one was open for 0% -> 0% of each run, Pallas kernels for 0% -> 0%
where the time goes in v6:
time: 67.7 us; the launch traced here: 67.5 us
  waiting for transfers between devices  21.6 us (32%)
  starting transfers between devices  19.4 us (29%)
  blocking collectives  15.2 us (22%)
  Pallas kernels  9.93 us (15%)
  between operations  1.33 us (2%)
    all_to_all x1, blocking collectives, by_source(): back = lax.all_to_all(out, 'tcol', 0, 0, tiled=True)  15.2 us
    pallas_call x4, Pallas kernels, call(): pl.pallas_call(kernel, out_shape=outs, in_specs=specs, out_specs=[target]...  9.93 us
    ppermute x3, waiting for transfers between devices, by_source(): same.append(lax.ppermute(packet, 'tcol', along(k)))  8.67 us
    ppermute x3, starting transfers between devices, by_source(): same.append(lax.ppermute(packet, 'tcol', along(k)))  8.39 us
    ppermute x1, waiting for transfers between devices, by_source(): other = [lax.ppermute(packets[0], 'tcol', across)]  5.44 us
    ppermute x4, starting transfers between devices, by_source(): other = other + [lax.ppermute(value, 'tcol', across) for value in same[1:]]  4.81 us
    ppermute x4, waiting for transfers between devices, by_source(): other = other + [lax.ppermute(value, 'tcol', across) for value in same[1:]]  4.11 us
    ppermute x2, waiting for transfers between devices, by_source(): lax.ppermute(gathered, 'freq', pairs)  3.38 us
  transfers between devices with their start and end apart: 11, of which 7 were waited for; matrix products, arithmetic and copies ran while one was open for 0% of the time, Pallas kernels for 0%

profile of v6, /device:TPU:0, one launch (start us, length us, event | category | flops | bytes accessed | tf_op | source)
XLA Modules:
  0.0 67.5 jit_solution(10883427501898821738)
XLA Ops:
  0.6 2.3 %shard_map.68 = (bf16[576,256]{1,0:T(8,128)(2,1)S(1)}, bf16[576,256]{1,0:T(8,128)(2,1)S(1)}, bf16[576,256]{1,0:T(8,128)(2,1)S(1)}, bf16[320,256]{1,0:T(8,128)(2,1)S(1)}, bf16[256,256]{1,0:T(8,128)(2,1)S(1)}) custom-call(s32[1]{0:T(128)} %bitcast.here_ref, s32[1]{0:T(128)} %bitcast.4.mine_ref, s32[8,8]{1,0:T(8,128)} %bitcast.23, ...), custom_call_target="tpu_custom_call" | custom-call | tf_op jit(solution)/shard_map/pallas_call | solution.py:654
  2.9 3.0 %collective-permute-start.1 = (bf16[576,256]{1,0:T(8,128)(2,1)S(1)}, bf16[576,256]{1,0:T(8,128)(2,1)S(1)}, u32[]{:S(2)}, u32[]{:S(2)}) collective-permute-start(bf16[576,256]{1,0:T(8,128)(2,1)S(1)} %get-tuple-element.21.refs_0_), channel_id=1, source_target_pairs={{0,1},{1,0},{2,3},{3,2},{4,5},{5,4},{6,7},{7,6},{8,9},{9,8},{10,11... | collective-permute-start | bytes 884744 | tf_op jit(solution)/shard_map/ppermute | solution.py:686
  6.0 1.6 %collective-permute-start = (bf16[576,256]{1,0:T(8,128)(2,1)S(1)}, bf16[576,256]{1,0:T(8,128)(2,1)S(1)}, u32[]{:S(2)}, u32[]{:S(2)}) collective-permute-start(bf16[576,256]{1,0:T(8,128)(2,1)S(1)} %get-tuple-element.24), channel_id=1, source_target_pairs={{0,2},{1,3},{2,4},{3,5},{4,6},{5,7},{6,0},{7,1},{8,10},{9,11},{10,... | collective-permute-start | bytes 884744 | tf_op jit(solution)/shard_map/ppermute | solution.py:685
  7.5 5.4 %collective-permute-done.1.refs_5_ = bf16[576,256]{1,0:T(8,128)(2,1)S(1)} collective-permute-done((bf16[576,256]{1,0:T(8,128)(2,1)S(1)}, bf16[576,256]{1,0:T(8,128)(2,1)S(1)}, u32[]{:S(2)}, u32[]{:S(2)}) %collective-permute-start.1) | collective-permute-done | bytes 294944 | tf_op jit(solution)/shard_map/ppermute | solution.py:686
  13.0 3.8 %collective-permute-start.2 = (bf16[576,256]{1,0:T(8,128)(2,1)S(1)}, bf16[576,256]{1,0:T(8,128)(2,1)S(1)}, u32[]{:S(2)}, u32[]{:S(2)}) collective-permute-start(bf16[576,256]{1,0:T(8,128)(2,1)S(1)} %get-tuple-element.28), channel_id=1, source_target_pairs={{0,6},{1,7},{2,0},{3,1},{4,2},{5,3},{6,4},{7,5},{8,14},{9,15},{10,... | collective-permute-start | bytes 884744 | tf_op jit(solution)/shard_map/ppermute | solution.py:692
  16.8 0.0 collective-permute-done.refs_1_
  16.8 0.2 collective-permute-start.3
  17.0 1.3 %collective-permute-start.5 = (bf16[576,256]{1,0:T(8,128)(2,1)S(1)}, bf16[576,256]{1,0:T(8,128)(2,1)S(1)}, u32[]{:S(2)}, u32[]{:S(2)}) collective-permute-start(bf16[576,256]{1,0:T(8,128)(2,1)S(1)} %collective-permute-done.refs_1_), channel_id=1, source_target_pairs={{0,1},{1,0},{2,3},{3,2},{4,5},{5,4},{6,7},{7,6},{8,9},{9,8},{10,11... | collective-permute-start | bytes 884744 | tf_op jit(solution)/shard_map/ppermute | solution.py:693
  18.3 5.9 %collective-permute-done.2.refs_2_ = bf16[576,256]{1,0:T(8,128)(2,1)S(1)} collective-permute-done((bf16[576,256]{1,0:T(8,128)(2,1)S(1)}, bf16[576,256]{1,0:T(8,128)(2,1)S(1)}, u32[]{:S(2)}, u32[]{:S(2)}) %collective-permute-start.2) | collective-permute-done | bytes 294944 | tf_op jit(solution)/shard_map/ppermute | solution.py:692
  24.2 1.5 %collective-permute-start.6 = (bf16[576,256]{1,0:T(8,128)(2,1)S(1)}, bf16[576,256]{1,0:T(8,128)(2,1)S(1)}, u32[]{:S(2)}, u32[]{:S(2)}) collective-permute-start(bf16[576,256]{1,0:T(8,128)(2,1)S(1)} %collective-permute-done.2.refs_2_), channel_id=1, source_target_pairs={{0,1},{1,0},{2,3},{3,2},{4,5},{5,4},{6,7},{7,6},{8,9},{9,8},{10,11... | collective-permute-start | bytes 884744 | tf_op jit(solution)/shard_map/ppermute | solution.py:693
  25.7 4.3 %collective-permute-start.4 = (bf16[256,256]{1,0:T(8,128)(2,1)S(1)}, bf16[256,256]{1,0:T(8,128)(2,1)S(1)}, u32[]{:S(2)}, u32[]{:S(2)}) collective-permute-start(bf16[256,256]{1,0:T(8,128)(2,1)S(1)} %get-tuple-element.30), channel_id=1, source_target_pairs={{0,4},{1,5},{2,6},{3,7},{4,0},{5,1},{6,2},{7,3},{8,12},{9,13},{10,... | collective-permute-start | bytes 393224 | tf_op jit(solution)/shard_map/ppermute | solution.py:692
  30.1 2.4 %collective-permute-done.3.refs_3_ = bf16[320,256]{1,0:T(8,128)(2,1)S(1)} collective-permute-done((bf16[320,256]{1,0:T(8,128)(2,1)S(1)}, bf16[320,256]{1,0:T(8,128)(2,1)S(1)}, u32[]{:S(2)}, u32[]{:S(2)}) %collective-permute-start.3) | collective-permute-done | bytes 163872 | tf_op jit(solution)/shard_map/ppermute | solution.py:692
  32.4 1.0 %collective-permute-start.7 = (bf16[320,256]{1,0:T(8,128)(2,1)S(1)}, bf16[320,256]{1,0:T(8,128)(2,1)S(1)}, u32[]{:S(2)}, u32[]{:S(2)}) collective-permute-start(bf16[320,256]{1,0:T(8,128)(2,1)S(1)} %collective-permute-done.3.refs_3_), channel_id=1, source_target_pairs={{0,1},{1,0},{2,3},{3,2},{4,5},{5,4},{6,7},{7,6},{8,9},{9,8},{10,11... | collective-permute-start | bytes 491528 | tf_op jit(solution)/shard_map/ppermute | solution.py:693
  33.4 0.4 collective-permute-done.4.refs_4_
  33.8 1.0 %collective-permute-start.8 = (bf16[256,256]{1,0:T(8,128)(2,1)S(1)}, bf16[256,256]{1,0:T(8,128)(2,1)S(1)}, u32[]{:S(2)}, u32[]{:S(2)}) collective-permute-start(bf16[256,256]{1,0:T(8,128)(2,1)S(1)} %collective-permute-done.4.refs_4_), channel_id=1, source_target_pairs={{0,1},{1,0},{2,3},{3,2},{4,5},{5,4},{6,7},{7,6},{8,9},{9,8},{10,11... | collective-permute-start | bytes 393224 | tf_op jit(solution)/shard_map/ppermute | solution.py:693
  35.5 4.1 %collective-permute-done.8.refs_9_ = bf16[256,256]{1,0:T(8,128)(2,1)S(1)} collective-permute-done((bf16[256,256]{1,0:T(8,128)(2,1)S(1)}, bf16[256,256]{1,0:T(8,128)(2,1)S(1)}, u32[]{:S(2)}, u32[]{:S(2)}) %collective-permute-start.8) | collective-permute-done | bytes 131104 | tf_op jit(solution)/shard_map/ppermute | solution.py:693
  39.6 5.6 %shard_map.69 = (f32[3,8,32,256]{3,2,1,0:T(8,128)S(1)}, f32[3,8,32,256]{3,2,1,0:T(8,128)S(1)}, f32[16,128]{1,0:T(8,128)S(1)}, bf16[2,512,128]{2,1,0:T(8,128)(2,1...) custom-call(s32[1]{0:T(128)} %bitcast.here_ref, s32[1]{0:T(128)S(6)} %copy.7.freq_ref, ...), custom_call_target="tpu_custom_call" | custom-call | tf_op jit(solution)/shard_map/pallas_call | solution.py:654
  45.3 0.1 collective-permute-start.9
  45.3 1.2 %collective-permute-done.9 = f32[1,16,128]{2,1,0:T(8,128)S(1)} collective-permute-done((f32[1,16,128]{2,1,0:T(8,128)S(1)}, f32[1,16,128]{2,1,0:T(8,128)S(1)}, u32[]{:S(2)}, u32[]{:S(2)}) %collective-permute-start.9) | collective-permute-done | bytes 8224 | tf_op jit(solution)/shard_map/ppermute | solution.py:711
  46.5 1.5 %collective-permute-start.10 = (f32[2,16,128]{2,1,0:T(8,128)S(1)}, f32[2,16,128]{2,1,0:T(8,128)S(1)}, u32[]{:S(2)}, u32[]{:S(2)}) collective-permute-start(f32[2,16,128]{2,1,0:T(8,128)S(1)} %pad_maximum_fusion), channel_id=1, source_target_pairs={{0,16},{8,24},{16,0},{24,8},{1,17},{9,25},{17,1},{25,9},{2,18},{10... | collective-permute-start | bytes 49160 | tf_op jit(solution)/shard_map/ppermute | solution.py:711
  48.0 2.2 %collective-permute-done.10 = f32[2,16,128]{2,1,0:T(8,128)S(1)} collective-permute-done((f32[2,16,128]{2,1,0:T(8,128)S(1)}, f32[2,16,128]{2,1,0:T(8,128)S(1)}, u32[]{:S(2)}, u32[]{:S(2)}) %collective-permute-start.10) | collective-permute-done | bytes 16416 | tf_op jit(solution)/shard_map/ppermute | solution.py:711
  50.2 0.7 %shard_map.70 = bf16[8,64,256]{2,1,0:T(8,128)(2,1)S(1)} custom-call(f32[16,128]{1,0:T(8,128)S(1)} %get-tuple-element.32.refs_0_, f32[16,128]{1,0:T(8,128)S(1)} %bitcast.16, f32[16,128]{1,0:T(8,128)S(1)} %get-tuple-element.41.refs_2_, f32[16,128]{1,0:T(8,128)S(1)} %get-tuple-element.40.refs_3_, f32[3,8,32,256]{3,2,1,0:T(8,128)S(1)} %get-tuple-element.33.refs_4_, ...), custom_call_target="tpu_custom_call" | custom-call | tf_op jit(solution)/shard_map/pallas_call | solution.py:654
  50.9 15.2 %all_to_all.5.recv_ref = bf16[8,64,256]{2,1,0:T(8,128)(2,1)S(1)} all-to-all(bf16[8,64,256]{2,1,0:T(8,128)(2,1)S(1)} %shard_map.70), channel_id=1, replica_groups=mesh['freq'=4,'tcol'=8] {'tcol'}, dimensions={0} | all-to-all | bytes 524288 | tf_op jit(solution)/shard_map/all_to_all | solution.py:718
  66.1 1.3 %shard_map.71 = (f32[2,512,128]{2,1,0:T(8,128)}, f32[2,512,128]{2,1,0:T(8,128)}) custom-call(bf16[8,64,256]{2,1,0:T(8,128)(2,1)S(1)} %all_to_all.5.recv_ref, bf16[2,512,128]{2,1,0:T(8,128)(2,1)S(1)} %get-tuple-element.35.data_ref, bf16[2,512,256]{2,1,0:T(8,128)(2,1)S(1)} %get-tuple-element.36.left_ref, bf16[2,512,256]{2,1,0:T(8,128)(2,1)S(1)} %get-tuple-element.37.right_ref), custom_call_target="tpu_custom_call" | custom-call | tf_op jit(solution)/shard_map/pallas_call | solution.py:654
  (5 shorter events, 0.0 us)
Async XLA Ops:
  2.9 10.0 %collective-permute-start.1 = (bf16[576,256]{1,0:T(8,128)(2,1)S(1)}, bf16[576,256]{1,0:T(8,128)(2,1)S(1)}, u32[]{:S(2)}, u32[]{:S(2)}) collective-permute-start(bf16[576,256]{1,0:T(8,128)(2,1)S(1)} %get-tuple-element.21.refs_0_), channel_id=1, source_target_pairs={{0,1},{1,0},{2,3},{3,2},{4,5},{5,4},{6,7},{7,6},{8,9},{9,8},{10,11... | collective-permute-start | bytes 884744 | tf_op jit(solution)/shard_map/ppermute | solution.py:686
  6.0 10.9 %collective-permute-start = (bf16[576,256]{1,0:T(8,128)(2,1)S(1)}, bf16[576,256]{1,0:T(8,128)(2,1)S(1)}, u32[]{:S(2)}, u32[]{:S(2)}) collective-permute-start(bf16[576,256]{1,0:T(8,128)(2,1)S(1)} %get-tuple-element.24), channel_id=1, source_target_pairs={{0,2},{1,3},{2,4},{3,5},{4,6},{5,7},{6,0},{7,1},{8,10},{9,11},{10,... | collective-permute-start | bytes 884744 | tf_op jit(solution)/shard_map/ppermute | solution.py:685
  13.0 11.2 %collective-permute-start.2 = (bf16[576,256]{1,0:T(8,128)(2,1)S(1)}, bf16[576,256]{1,0:T(8,128)(2,1)S(1)}, u32[]{:S(2)}, u32[]{:S(2)}) collective-permute-start(bf16[576,256]{1,0:T(8,128)(2,1)S(1)} %get-tuple-element.28), channel_id=1, source_target_pairs={{0,6},{1,7},{2,0},{3,1},{4,2},{5,3},{6,4},{7,5},{8,14},{9,15},{10,... | collective-permute-start | bytes 884744 | tf_op jit(solution)/shard_map/ppermute | solution.py:692
  16.8 15.6 %collective-permute-start.3 = (bf16[320,256]{1,0:T(8,128)(2,1)S(1)}, bf16[320,256]{1,0:T(8,128)(2,1)S(1)}, u32[]{:S(2)}, u32[]{:S(2)}) collective-permute-start(bf16[320,256]{1,0:T(8,128)(2,1)S(1)} %get-tuple-element.29), channel_id=1, source_target_pairs={{0,4},{1,5},{2,6},{3,7},{4,0},{5,1},{6,2},{7,3},{8,12},{9,13},{10,... | collective-permute-start | bytes 491528 | tf_op jit(solution)/shard_map/ppermute | solution.py:692
  17.0 22.6 %collective-permute-start.5 = (bf16[576,256]{1,0:T(8,128)(2,1)S(1)}, bf16[576,256]{1,0:T(8,128)(2,1)S(1)}, u32[]{:S(2)}, u32[]{:S(2)}) collective-permute-start(bf16[576,256]{1,0:T(8,128)(2,1)S(1)} %collective-permute-done.refs_1_), channel_id=1, source_target_pairs={{0,1},{1,0},{2,3},{3,2},{4,5},{5,4},{6,7},{7,6},{8,9},{9,8},{10,11... | collective-permute-start | bytes 884744 | tf_op jit(solution)/shard_map/ppermute | solution.py:693
  24.2 15.4 %collective-permute-start.6 = (bf16[576,256]{1,0:T(8,128)(2,1)S(1)}, bf16[576,256]{1,0:T(8,128)(2,1)S(1)}, u32[]{:S(2)}, u32[]{:S(2)}) collective-permute-start(bf16[576,256]{1,0:T(8,128)(2,1)S(1)} %collective-permute-done.2.refs_2_), channel_id=1, source_target_pairs={{0,1},{1,0},{2,3},{3,2},{4,5},{5,4},{6,7},{7,6},{8,9},{9,8},{10,11... | collective-permute-start | bytes 884744 | tf_op jit(solution)/shard_map/ppermute | solution.py:693
  25.7 8.1 %collective-permute-start.4 = (bf16[256,256]{1,0:T(8,128)(2,1)S(1)}, bf16[256,256]{1,0:T(8,128)(2,1)S(1)}, u32[]{:S(2)}, u32[]{:S(2)}) collective-permute-start(bf16[256,256]{1,0:T(8,128)(2,1)S(1)} %get-tuple-element.30), channel_id=1, source_target_pairs={{0,4},{1,5},{2,6},{3,7},{4,0},{5,1},{6,2},{7,3},{8,12},{9,13},{10,... | collective-permute-start | bytes 393224 | tf_op jit(solution)/shard_map/ppermute | solution.py:692
  32.4 7.2 %collective-permute-start.7 = (bf16[320,256]{1,0:T(8,128)(2,1)S(1)}, bf16[320,256]{1,0:T(8,128)(2,1)S(1)}, u32[]{:S(2)}, u32[]{:S(2)}) collective-permute-start(bf16[320,256]{1,0:T(8,128)(2,1)S(1)} %collective-permute-done.3.refs_3_), channel_id=1, source_target_pairs={{0,1},{1,0},{2,3},{3,2},{4,5},{5,4},{6,7},{7,6},{8,9},{9,8},{10,11... | collective-permute-start | bytes 491528 | tf_op jit(solution)/shard_map/ppermute | solution.py:693
  33.8 5.8 %collective-permute-start.8 = (bf16[256,256]{1,0:T(8,128)(2,1)S(1)}, bf16[256,256]{1,0:T(8,128)(2,1)S(1)}, u32[]{:S(2)}, u32[]{:S(2)}) collective-permute-start(bf16[256,256]{1,0:T(8,128)(2,1)S(1)} %collective-permute-done.4.refs_4_), channel_id=1, source_target_pairs={{0,1},{1,0},{2,3},{3,2},{4,5},{5,4},{6,7},{7,6},{8,9},{9,8},{10,11... | collective-permute-start | bytes 393224 | tf_op jit(solution)/shard_map/ppermute | solution.py:693
  45.3 1.2 %collective-permute-start.9 = (f32[1,16,128]{2,1,0:T(8,128)S(1)}, f32[1,16,128]{2,1,0:T(8,128)S(1)}, u32[]{:S(2)}, u32[]{:S(2)}) collective-permute-start(f32[1,16,128]{2,1,0:T(8,128)S(1)} %bitcast.14), channel_id=1, source_target_pairs={{0,8},{8,0},{16,24},{24,16},{1,9},{9,1},{17,25},{25,17},{2,10},{10... | collective-permute-start | bytes 24584 | tf_op jit(solution)/shard_map/ppermute | solution.py:711
  46.5 3.7 %collective-permute-start.10 = (f32[2,16,128]{2,1,0:T(8,128)S(1)}, f32[2,16,128]{2,1,0:T(8,128)S(1)}, u32[]{:S(2)}, u32[]{:S(2)}) collective-permute-start(f32[2,16,128]{2,1,0:T(8,128)S(1)} %pad_maximum_fusion), channel_id=1, source_target_pairs={{0,16},{8,24},{16,0},{24,8},{1,17},{9,25},{17,1},{25,9},{2,18},{10... | collective-permute-start | bytes 49160 | tf_op jit(solution)/shard_map/ppermute | solution.py:711

commit v7 on v5

--- a/solution.py
+++ b/solution.py
@@ -396,18 +396,9 @@
     return real.astype(BF16), imag.astype(BF16)
 
 
-def offsets(half):
-    return sorted(range(1, half), key=lambda k: (min(k, half - k), k))
-
-
-def tile_parts(refs, half):
-    whole = refs[0].shape[0] - refs[0].shape[1]
-    parts = {0: (refs[0], refs[0], whole)}
-    order = offsets(half)
-    for place, k in enumerate(order[:-1]):
-        parts[k] = (refs[1 + place], refs[1 + place], whole)
-    parts[order[-1]] = (refs[-2], refs[-1], 0)
-    return [parts[k] for k in range(half)]
+def direct_offsets(half):
+    others = [k for k in range(1, half) if k != 2]
+    return sorted(others, key=lambda k: (min(k, half - k), k))
 
 
 def gather_start(
@@ -415,7 +406,8 @@
 ):
     ranks_ref, data_ref, left_ref, right_ref, back_ref, sem = refs[-6:]
     half = n // 2
-    packets = tile_parts(refs[: half + 1], half)
+    direct = [0] + direct_offsets(half)
+    packets, small = refs[: half - 1], refs[half - 1 : half + 1]
     pairs = [
         (left_hbm, left_ref), (data_hbm, data_ref), (ranks_hbm, ranks_ref),
         (right_hbm, right_ref),
@@ -439,20 +431,24 @@
     back_ref[0] = (first[:s] + second[s:]).astype(BF16)
     back_ref[1] = (first[s:] - second[:s]).astype(BF16)
     gram = packed_gram(real, imag)
-    for first, _, _ in packets:
-        first[0:width, :] = gram
+    for packet in packets:
+        packet[0:width, :] = gram
     copies[3].wait()
     keep = lane_limits([ranks_ref[p, here] for p in range(n)], rank, width).astype(BF16)
     gram = packed_gram(right_ref[0] * keep, right_ref[1] * keep)
     z, x = lax.div(here, 2), lax.rem(here, 2)
-    for k, (first, second, place) in enumerate(packets):
-        second[place : place + width, :] = gram
+    for packet in packets:
+        packet[width + 4 * q :, :] = gram
+    for k in range(half):
         base = 2 * lax.rem(z + k, half)
         for block, target in enumerate([base + 1 - x, base + x]):
             rows = pl.ds(pl.multiple_of(target * q, q), q)
-            place = width + 2 * q * block
-            first[place : place + q, :] = back_ref[0, rows, :]
-            first[place + q : place + 2 * q, :] = back_ref[1, rows, :]
+            if k == 2:
+                out, place = small[block], 0
+            else:
+                out, place = packets[direct.index(k)], width + 2 * q * block
+            out[place : place + q, :] = back_ref[0, rows, :]
+            out[place + q : place + 2 * q, :] = back_ref[1, rows, :]
 
 
 def swap_tiles(rank, source, target):
@@ -506,7 +502,9 @@
     rank, n, here_ref, freq_ref, *refs
 ):
     half = n // 2
-    tiles = [tile_parts(refs[: half + 1], half), tile_parts(refs[half + 1 : n + 2], half)]
+    order = [0] + direct_offsets(half) + [2]
+    tiles = [refs[:half], refs[half:n]]
+    small = refs[n : n + 2]
     b_ref, c_ref, stats_ref, left_ref, right_ref, one_ref, two_ref = refs[n + 2 :]
     width = refs[0].shape[1]
     q = stats_ref.shape[0]
@@ -515,15 +513,19 @@
     for k in range(half):
         base = 2 * lax.rem(z + half - k, half)
         for other in range(2):
-            first, second, place = tiles[other][k]
+            ref = tiles[other][order.index(k)]
             at = pl.ds(base + (1 - x if other else x), 1)
-            grams = (first[0:width, :], second[place : place + width, :])
+            grams = (ref[0:width, :], ref[width + 4 * q :, :])
             for packed, gram_ref in zip(grams, (left_ref, right_ref)):
                 real, imag = unpacked_gram(packed)
                 gram_ref[0, at] = real[None]
                 gram_ref[1, at] = imag[None]
             start = width + (0 if other else 2 * q)
-            one_ref[at] = first[start : start + 2 * q, :].astype(F32)[None]
+            if k == 2:
+                block = small[1 - other][...]
+            else:
+                block = ref[start : start + 2 * q, :]
+            one_ref[at] = block.astype(F32)[None]
     b0, b1, b2 = b_ref.at[0], b_ref.at[1], b_ref.at[2]
     c0, c1, c2 = c_ref.at[0], c_ref.at[1], c_ref.at[2]
     swap_tiles(rank, one_ref, b0)
@@ -663,15 +665,15 @@
             compiler_params=pltpu.CompilerParams(vmem_limit_bytes=room),
         )(*args)
 
-    def along(shift):
+    def along(shift, flip=0):
         return [
-            (2 * z + x, 2 * ((z + shift) % half) + x) for z in range(half) for x in range(2)
+            (2 * z + x, 2 * ((z + shift) % half) + (x ^ flip))
+            for z in range(half) for x in range(2)
         ]
 
     across = [(t, t ^ 1) for t in range(ntile)]
-    sizes = [2 * width + 4 * q] * (half - 1) + [width + 4 * q, width]
-    shifts = [0] + offsets(half)
-    shifts = shifts + shifts[-1:]
+    sizes = [2 * width + 4 * q] * (half - 1) + [2 * q, 2 * q]
+    direct = direct_offsets(half)
     packets = call(
         functools.partial(gather_start, rank, ntile), [SMEM] * 2 + [HBM] * 4,
         (here, mine, ranks, data, left, right),
@@ -686,15 +688,19 @@
         ],
     )
     same = [packets[0]] + [
-        lax.ppermute(packet, "tcol", along(k)) for packet, k in zip(packets[1:], shifts[1:])
-    ]
-    other = [lax.ppermute(value, "tcol", across) for value in same]
+        lax.ppermute(packet, "tcol", along(k)) for packet, k in zip(packets[1:], direct)
+    ]
+    small = [lax.ppermute(packets[half - block], "tcol", along(2, block)) for block in (1, 0)]
+    first = lax.ppermute(packets[0], "tcol", across)
+    same[1], first, *small = lax.optimization_barrier((same[1], first, *small))
+    same.append(lax.ppermute(same[1], "tcol", along(1)))
+    other = [first] + [lax.ppermute(value, "tcol", across) for value in same[1:]]
     vectors = jax.ShapeDtypeStruct((3, ntile, 2 * q, width), F32)
     grams = pltpu.VMEM((2, ntile, width, width), BF16)
     vector = pltpu.VMEM((ntile, 2 * q, width), F32)
     b, c, stats = call(
         functools.partial(chain_kernel, rank, ntile), [SMEM] * 2 + [VMEM] * (ntile + 2),
-        (here, freq_index, *same, *other),
+        (here, freq_index, *same, *other, *small),
         (vectors, vectors, jax.ShapeDtypeStruct((q, 128), F32)),
         [grams, grams, vector, vector],
     )
@@ -740,7 +746,7 @@
     width = left.shape[2]
     rank = width // ntile
     s = data.shape[2]
-    fits = ntile % 4 == 0 and s % (16 * ntile) == 0 and width % 128 == 0 and 128 % rank == 0
+    fits = ntile % 2 == 0 and ntile >= 6 and s % (16 * ntile) == 0 and width % 128 == 0 and 128 % rank == 0
     if fits and nfreq & (nfreq - 1) == 0 and ntile * width * width <= 1 << 20:
         wave, res = by_source(data, left, right, ranks, freq_index, ntile, nfreq, here, mine)
         return wave[None], res[None]

time: 67.2 us -> 66.6 us (level)
  waiting for transfers between devices: 17.6 us -> 22.3 us
  starting transfers between devices: 23.3 us -> 20.3 us
  blocking collectives: 15.1 us -> 12.9 us
    ppermute x5 -> x7, waiting for transfers between devices: 2.84 us -> 19.1 us  [the longest x3 9.18 us: by_source(): lax.ppermute(value, 'tcol', across)]
    ppermute x4 -> x2, waiting for transfers between devices: 11.4 us -> 0.01 us  [by_source(): lax.ppermute(packet, 'tcol', along(k))]
    ppermute x4 -> x2, starting transfers between devices: 14 us -> 5.2 us  [by_source(): lax.ppermute(packet, 'tcol', along(k))]
    ppermute x5 -> x7, starting transfers between devices: 7.67 us -> 13.3 us  [the longest x1 5.65 us: by_source(): same.append(lax.ppermute(same[1], 'tcol', along(1)))]
    all_to_all x1, blocking collectives: 15.1 us -> 12.9 us  [by_source(): back = lax.all_to_all(out, 'tcol', 0, 0, tiled=True)]
where the time goes in v7:
time: 66.6 us; the launch traced here: 66.4 us
  waiting for transfers between devices  22.3 us (33%)
  starting transfers between devices  20.3 us (30%)
  blocking collectives  12.9 us (19%)
  Pallas kernels  9.64 us (14%)
  between operations  1.33 us (2%)
    all_to_all x1, blocking collectives, by_source(): back = lax.all_to_all(out, 'tcol', 0, 0, tiled=True)  12.9 us
    pallas_call x4, Pallas kernels, call(): pl.pallas_call(kernel, out_shape=outs, in_specs=specs, out_specs=[target]...  9.64 us
    ppermute x3, waiting for transfers between devices, by_source(): lax.ppermute(value, 'tcol', across)  9.18 us
    ppermute x1, waiting for transfers between devices, by_source(): same.append(lax.ppermute(same[1], 'tcol', along(1)))  5.91 us
    ppermute x1, starting transfers between devices, by_source(): same.append(lax.ppermute(same[1], 'tcol', along(1)))  5.65 us
    ppermute x2, starting transfers between devices, by_source(): lax.ppermute(packet, 'tcol', along(k))  5.2 us
    ppermute x2, waiting for transfers between devices, by_source(): lax.ppermute(packets[half - block], 'tcol', along(2, block))  4 us
    ppermute x3, starting transfers between devices, by_source(): lax.ppermute(value, 'tcol', across)  3.24 us
  transfers between devices with their start and end apart: 11, of which 6 were waited for; matrix products, arithmetic and copies ran while one was open for 0% of the time, Pallas kernels for 0%

profile of v7, /device:TPU:0, one launch (start us, length us, event | category | flops | bytes accessed | tf_op | source)
XLA Modules:
  0.0 66.4 jit_solution(2735744679847521343)
XLA Ops:
  0.6 2.3 %shard_map.68 = (bf16[576,256]{1,0:T(8,128)(2,1)S(1)}, bf16[576,256]{1,0:T(8,128)(2,1)S(1)}, bf16[576,256]{1,0:T(8,128)(2,1)S(1)}, bf16[32,256]{1,0:T(8,128)(2,1)S(1)}, bf16[32,256]{1,0:T(8,128)(2,1)S(1)}) custom-call(s32[1]{0:T(128)} %bitcast.3.here_ref, s32[1]{0:T(128)} %bitcast.4.mine_ref, s32[8,8]{1,0:T(8,128)} %bitcast.23, ...), custom_call_target="tpu_custom_call" | custom-call | tf_op jit(solution)/shard_map/pallas_call | solution.py:659
  2.9 3.1 %collective-permute-start = (bf16[576,256]{1,0:T(8,128)(2,1)S(1)}, bf16[576,256]{1,0:T(8,128)(2,1)S(1)}, u32[]{:S(2)}, u32[]{:S(2)}) collective-permute-start(bf16[576,256]{1,0:T(8,128)(2,1)S(1)} %get-tuple-element.21), channel_id=1, source_target_pairs={{0,2},{1,3},{2,4},{3,5},{4,6},{5,7},{6,0},{7,1},{8,10},{9,11},{10,... | collective-permute-start | bytes 884744 | tf_op jit(solution)/shard_map/ppermute | solution.py:691
  6.0 1.5 %collective-permute-start.1 = (bf16[576,256]{1,0:T(8,128)(2,1)S(1)}, bf16[576,256]{1,0:T(8,128)(2,1)S(1)}, u32[]{:S(2)}, u32[]{:S(2)}) collective-permute-start(bf16[576,256]{1,0:T(8,128)(2,1)S(1)} %get-tuple-element.20.refs_0_), channel_id=1, source_target_pairs={{0,1},{1,0},{2,3},{3,2},{4,5},{5,4},{6,7},{7,6},{8,9},{9,8},{10,11... | collective-permute-start | bytes 884744 | tf_op jit(solution)/shard_map/ppermute | solution.py:694
  7.5 2.6 %collective-permute-start.2 = (bf16[32,256]{1,0:T(8,128)(2,1)S(1)}, bf16[32,256]{1,0:T(8,128)(2,1)S(1)}, u32[]{:S(2)}, u32[]{:S(2)}) collective-permute-start(bf16[32,256]{1,0:T(8,128)(2,1)S(1)} %get-tuple-element.22), channel_id=1, source_target_pairs={{0,5},{1,4},{2,7},{3,6},{4,1},{5,0},{6,3},{7,2},{8,13},{9,12},{10,... | collective-permute-start | bytes 49160 | tf_op jit(solution)/shard_map/ppermute | solution.py:693
  10.1 0.3 collective-permute-start.3
  10.4 2.1 %collective-permute-start.4 = (bf16[576,256]{1,0:T(8,128)(2,1)S(1)}, bf16[576,256]{1,0:T(8,128)(2,1)S(1)}, u32[]{:S(2)}, u32[]{:S(2)}) collective-permute-start(bf16[576,256]{1,0:T(8,128)(2,1)S(1)} %get-tuple-element.25), channel_id=1, source_target_pairs={{0,6},{1,7},{2,0},{3,1},{4,2},{5,3},{6,4},{7,5},{8,14},{9,15},{10,... | collective-permute-start | bytes 884744 | tf_op jit(solution)/shard_map/ppermute | solution.py:691
  12.5 4.0 %collective-permute-done.2.refs_8_ = bf16[32,256]{1,0:T(8,128)(2,1)S(1)} collective-permute-done((bf16[32,256]{1,0:T(8,128)(2,1)S(1)}, bf16[32,256]{1,0:T(8,128)(2,1)S(1)}, u32[]{:S(2)}, u32[]{:S(2)}) %collective-permute-start.2) | collective-permute-done | bytes 16416 | tf_op jit(solution)/shard_map/ppermute | solution.py:693
  16.5 5.6 %collective-permute-start.5 = (bf16[576,256]{1,0:T(8,128)(2,1)S(1)}, bf16[576,256]{1,0:T(8,128)(2,1)S(1)}, u32[]{:S(2)}, u32[]{:S(2)}) collective-permute-start(bf16[576,256]{1,0:T(8,128)(2,1)S(1)} %collective-permute-done.refs_1_), channel_id=1, source_target_pairs={{0,2},{1,3},{2,4},{3,5},{4,6},{5,7},{6,0},{7,1},{8,10},{9,11},{10,... | collective-permute-start | bytes 884744 | tf_op jit(solution)/shard_map/ppermute | solution.py:696
  22.2 1.5 %collective-permute-start.6 = (bf16[576,256]{1,0:T(8,128)(2,1)S(1)}, bf16[576,256]{1,0:T(8,128)(2,1)S(1)}, u32[]{:S(2)}, u32[]{:S(2)}) collective-permute-start(bf16[576,256]{1,0:T(8,128)(2,1)S(1)} %collective-permute-done.refs_1_), channel_id=1, source_target_pairs={{0,1},{1,0},{2,3},{3,2},{4,5},{5,4},{6,7},{7,6},{8,9},{9,8},{10,11... | collective-permute-start | bytes 884744 | tf_op jit(solution)/shard_map/ppermute | solution.py:697
  23.7 0.0 collective-permute-done.4.refs_2_
  23.7 0.9 %collective-permute-start.7 = (bf16[576,256]{1,0:T(8,128)(2,1)S(1)}, bf16[576,256]{1,0:T(8,128)(2,1)S(1)}, u32[]{:S(2)}, u32[]{:S(2)}) collective-permute-start(bf16[576,256]{1,0:T(8,128)(2,1)S(1)} %collective-permute-done.4.refs_2_), channel_id=1, source_target_pairs={{0,1},{1,0},{2,3},{3,2},{4,5},{5,4},{6,7},{7,6},{8,9},{9,8},{10,11... | collective-permute-start | bytes 884744 | tf_op jit(solution)/shard_map/ppermute | solution.py:697
  24.6 5.9 %collective-permute-done.5.refs_3_ = bf16[576,256]{1,0:T(8,128)(2,1)S(1)} collective-permute-done((bf16[576,256]{1,0:T(8,128)(2,1)S(1)}, bf16[576,256]{1,0:T(8,128)(2,1)S(1)}, u32[]{:S(2)}, u32[]{:S(2)}) %collective-permute-start.5) | collective-permute-done | bytes 294944 | tf_op jit(solution)/shard_map/ppermute | solution.py:696
  30.5 0.9 %collective-permute-start.8 = (bf16[576,256]{1,0:T(8,128)(2,1)S(1)}, bf16[576,256]{1,0:T(8,128)(2,1)S(1)}, u32[]{:S(2)}, u32[]{:S(2)}) collective-permute-start(bf16[576,256]{1,0:T(8,128)(2,1)S(1)} %collective-permute-done.5.refs_3_), channel_id=1, source_target_pairs={{0,1},{1,0},{2,3},{3,2},{4,5},{5,4},{6,7},{7,6},{8,9},{9,8},{10,11... | collective-permute-start | bytes 884744 | tf_op jit(solution)/shard_map/ppermute | solution.py:697
  32.0 6.0 %collective-permute-done.7.refs_6_ = bf16[576,256]{1,0:T(8,128)(2,1)S(1)} collective-permute-done((bf16[576,256]{1,0:T(8,128)(2,1)S(1)}, bf16[576,256]{1,0:T(8,128)(2,1)S(1)}, u32[]{:S(2)}, u32[]{:S(2)}) %collective-permute-start.7) | collective-permute-done | bytes 294944 | tf_op jit(solution)/shard_map/ppermute | solution.py:697
  38.0 0.0 collective-permute-done.6.refs_5_
  38.0 3.2 %collective-permute-done.8.refs_7_ = bf16[576,256]{1,0:T(8,128)(2,1)S(1)} collective-permute-done((bf16[576,256]{1,0:T(8,128)(2,1)S(1)}, bf16[576,256]{1,0:T(8,128)(2,1)S(1)}, u32[]{:S(2)}, u32[]{:S(2)}) %collective-permute-start.8) | collective-permute-done | bytes 294944 | tf_op jit(solution)/shard_map/ppermute | solution.py:697
  41.2 4.7 %shard_map.69 = (f32[3,8,32,256]{3,2,1,0:T(8,128)S(1)}, f32[3,8,32,256]{3,2,1,0:T(8,128)S(1)}, f32[16,128]{1,0:T(8,128)S(1)}) custom-call(s32[1]{0:T(128)} %bitcast.3.here_ref, s32[1]{0:T(128)S(6)} %copy.7.freq_ref, bf16[576,256]{1,0:T(8,128)(2,1)S(1)} %get-tuple-element.20.refs_0_, bf16[576,256]{1,0:T(8,128)(2,1)S(1)} %collective-permute-done.refs_1_, ...), custom_call_target="tpu_custom_call" | custom-call | tf_op jit(solution)/shard_map/pallas_call | solution.py:659
  45.9 0.1 collective-permute-start.9
  46.0 1.2 %collective-permute-done.9 = f32[1,16,128]{2,1,0:T(8,128)S(1)} collective-permute-done((f32[1,16,128]{2,1,0:T(8,128)S(1)}, f32[1,16,128]{2,1,0:T(8,128)S(1)}, u32[]{:S(2)}, u32[]{:S(2)}) %collective-permute-start.9) | collective-permute-done | bytes 8224 | tf_op jit(solution)/shard_map/ppermute | solution.py:711
  47.1 1.7 %collective-permute-start.10 = (f32[2,16,128]{2,1,0:T(8,128)S(1)}, f32[2,16,128]{2,1,0:T(8,128)S(1)}, u32[]{:S(2)}, u32[]{:S(2)}) collective-permute-start(f32[2,16,128]{2,1,0:T(8,128)S(1)} %pad_maximum_fusion), channel_id=1, source_target_pairs={{0,16},{8,24},{16,0},{24,8},{1,17},{9,25},{17,1},{25,9},{2,18},{10... | collective-permute-start | bytes 49160 | tf_op jit(solution)/shard_map/ppermute | solution.py:711
  48.9 2.0 %collective-permute-done.10 = f32[2,16,128]{2,1,0:T(8,128)S(1)} collective-permute-done((f32[2,16,128]{2,1,0:T(8,128)S(1)}, f32[2,16,128]{2,1,0:T(8,128)S(1)}, u32[]{:S(2)}, u32[]{:S(2)}) %collective-permute-start.10) | collective-permute-done | bytes 16416 | tf_op jit(solution)/shard_map/ppermute | solution.py:711
  50.9 1.3 %shard_map.70 = (bf16[8,64,256]{2,1,0:T(8,128)(2,1)S(1)}, bf16[2,512,128]{2,1,0:T(8,128)(2,1)S(1)}, bf16[2,512,256]{2,1,0:T(8,128)(2,1)S(1)}, bf16[2,512,256]{2,1,0:T(8,128)(2,1)S(1)}) custom-call(bf16[2,512,128]{2,1,0:T(8,128)(2,1)} %bitcast.22, bf16[2,512,256]{2,1,0:T(8,128)(2,1)} %bitcast.18, bf16[2,512,256]{2,1,0:T(8,128)(2,1)} %bitcast.20, ...), custom_call_target="tpu_custom_call" | custom-call | tf_op jit(solution)/shard_map/pallas_call | solution.py:659
  52.2 12.9 %all_to_all.5.recv_ref = bf16[8,64,256]{2,1,0:T(8,128)(2,1)S(1)} all-to-all(bf16[8,64,256]{2,1,0:T(8,128)(2,1)S(1)} %get-tuple-element.32), channel_id=1, replica_groups=mesh['freq'=4,'tcol'=8] {'tcol'}, dimensions={0} | all-to-all | bytes 524288 | tf_op jit(solution)/shard_map/all_to_all | solution.py:722
  65.1 1.3 %shard_map.71 = (f32[2,512,128]{2,1,0:T(8,128)}, f32[2,512,128]{2,1,0:T(8,128)}) custom-call(bf16[8,64,256]{2,1,0:T(8,128)(2,1)S(1)} %all_to_all.5.recv_ref, bf16[2,512,128]{2,1,0:T(8,128)(2,1)S(1)} %get-tuple-element.33.data_ref, bf16[2,512,256]{2,1,0:T(8,128)(2,1)S(1)} %get-tuple-element.34.left_ref, bf16[2,512,256]{2,1,0:T(8,128)(2,1)S(1)} %get-tuple-element.35.right_ref), custom_call_target="tpu_custom_call" | custom-call | tf_op jit(solution)/shard_map/pallas_call | solution.py:659
  (5 shorter events, 0.0 us)
Async XLA Ops:
  2.9 13.6 %collective-permute-start = (bf16[576,256]{1,0:T(8,128)(2,1)S(1)}, bf16[576,256]{1,0:T(8,128)(2,1)S(1)}, u32[]{:S(2)}, u32[]{:S(2)}) collective-permute-start(bf16[576,256]{1,0:T(8,128)(2,1)S(1)} %get-tuple-element.21), channel_id=1, source_target_pairs={{0,2},{1,3},{2,4},{3,5},{4,6},{5,7},{6,0},{7,1},{8,10},{9,11},{10,... | collective-permute-start | bytes 884744 | tf_op jit(solution)/shard_map/ppermute | solution.py:691
  6.0 10.5 %collective-permute-start.1 = (bf16[576,256]{1,0:T(8,128)(2,1)S(1)}, bf16[576,256]{1,0:T(8,128)(2,1)S(1)}, u32[]{:S(2)}, u32[]{:S(2)}) collective-permute-start(bf16[576,256]{1,0:T(8,128)(2,1)S(1)} %get-tuple-element.20.refs_0_), channel_id=1, source_target_pairs={{0,1},{1,0},{2,3},{3,2},{4,5},{5,4},{6,7},{7,6},{8,9},{9,8},{10,11... | collective-permute-start | bytes 884744 | tf_op jit(solution)/shard_map/ppermute | solution.py:694
  7.5 9.0 %collective-permute-start.2 = (bf16[32,256]{1,0:T(8,128)(2,1)S(1)}, bf16[32,256]{1,0:T(8,128)(2,1)S(1)}, u32[]{:S(2)}, u32[]{:S(2)}) collective-permute-start(bf16[32,256]{1,0:T(8,128)(2,1)S(1)} %get-tuple-element.22), channel_id=1, source_target_pairs={{0,5},{1,4},{2,7},{3,6},{4,1},{5,0},{6,3},{7,2},{8,13},{9,12},{10,... | collective-permute-start | bytes 49160 | tf_op jit(solution)/shard_map/ppermute | solution.py:693
  10.1 6.4 %collective-permute-start.3 = (bf16[32,256]{1,0:T(8,128)(2,1)S(1)}, bf16[32,256]{1,0:T(8,128)(2,1)S(1)}, u32[]{:S(2)}, u32[]{:S(2)}) collective-permute-start(bf16[32,256]{1,0:T(8,128)(2,1)S(1)} %get-tuple-element.23), channel_id=1, source_target_pairs={{0,4},{1,5},{2,6},{3,7},{4,0},{5,1},{6,2},{7,3},{8,12},{9,13},{10,... | collective-permute-start | bytes 49160 | tf_op jit(solution)/shard_map/ppermute | solution.py:693
  10.4 13.2 %collective-permute-start.4 = (bf16[576,256]{1,0:T(8,128)(2,1)S(1)}, bf16[576,256]{1,0:T(8,128)(2,1)S(1)}, u32[]{:S(2)}, u32[]{:S(2)}) collective-permute-start(bf16[576,256]{1,0:T(8,128)(2,1)S(1)} %get-tuple-element.25), channel_id=1, source_target_pairs={{0,6},{1,7},{2,0},{3,1},{4,2},{5,3},{6,4},{7,5},{8,14},{9,15},{10,... | collective-permute-start | bytes 884744 | tf_op jit(solution)/shard_map/ppermute | solution.py:691
  16.5 13.9 %collective-permute-start.5 = (bf16[576,256]{1,0:T(8,128)(2,1)S(1)}, bf16[576,256]{1,0:T(8,128)(2,1)S(1)}, u32[]{:S(2)}, u32[]{:S(2)}) collective-permute-start(bf16[576,256]{1,0:T(8,128)(2,1)S(1)} %collective-permute-done.refs_1_), channel_id=1, source_target_pairs={{0,2},{1,3},{2,4},{3,5},{4,6},{5,7},{6,0},{7,1},{8,10},{9,11},{10,... | collective-permute-start | bytes 884744 | tf_op jit(solution)/shard_map/ppermute | solution.py:696
  22.2 15.8 %collective-permute-start.6 = (bf16[576,256]{1,0:T(8,128)(2,1)S(1)}, bf16[576,256]{1,0:T(8,128)(2,1)S(1)}, u32[]{:S(2)}, u32[]{:S(2)}) collective-permute-start(bf16[576,256]{1,0:T(8,128)(2,1)S(1)} %collective-permute-done.refs_1_), channel_id=1, source_target_pairs={{0,1},{1,0},{2,3},{3,2},{4,5},{5,4},{6,7},{7,6},{8,9},{9,8},{10,11... | collective-permute-start | bytes 884744 | tf_op jit(solution)/shard_map/ppermute | solution.py:697
  23.7 14.3 %collective-permute-start.7 = (bf16[576,256]{1,0:T(8,128)(2,1)S(1)}, bf16[576,256]{1,0:T(8,128)(2,1)S(1)}, u32[]{:S(2)}, u32[]{:S(2)}) collective-permute-start(bf16[576,256]{1,0:T(8,128)(2,1)S(1)} %collective-permute-done.4.refs_2_), channel_id=1, source_target_pairs={{0,1},{1,0},{2,3},{3,2},{4,5},{5,4},{6,7},{7,6},{8,9},{9,8},{10,11... | collective-permute-start | bytes 884744 | tf_op jit(solution)/shard_map/ppermute | solution.py:697
  30.5 10.7 %collective-permute-start.8 = (bf16[576,256]{1,0:T(8,128)(2,1)S(1)}, bf16[576,256]{1,0:T(8,128)(2,1)S(1)}, u32[]{:S(2)}, u32[]{:S(2)}) collective-permute-start(bf16[576,256]{1,0:T(8,128)(2,1)S(1)} %collective-permute-done.5.refs_3_), channel_id=1, source_target_pairs={{0,1},{1,0},{2,3},{3,2},{4,5},{5,4},{6,7},{7,6},{8,9},{9,8},{10,11... | collective-permute-start | bytes 884744 | tf_op jit(solution)/shard_map/ppermute | solution.py:697
  45.9 1.2 %collective-permute-start.9 = (f32[1,16,128]{2,1,0:T(8,128)S(1)}, f32[1,16,128]{2,1,0:T(8,128)S(1)}, u32[]{:S(2)}, u32[]{:S(2)}) collective-permute-start(f32[1,16,128]{2,1,0:T(8,128)S(1)} %bitcast.14), channel_id=1, source_target_pairs={{0,8},{8,0},{16,24},{24,16},{1,9},{9,1},{17,25},{25,17},{2,10},{10... | collective-permute-start | bytes 24584 | tf_op jit(solution)/shard_map/ppermute | solution.py:711
  47.1 3.7 %collective-permute-start.10 = (f32[2,16,128]{2,1,0:T(8,128)S(1)}, f32[2,16,128]{2,1,0:T(8,128)S(1)}, u32[]{:S(2)}, u32[]{:S(2)}) collective-permute-start(f32[2,16,128]{2,1,0:T(8,128)S(1)} %pad_maximum_fusion), channel_id=1, source_target_pairs={{0,16},{8,24},{16,0},{24,8},{1,17},{9,25},{17,1},{25,9},{2,18},{10... | collective-permute-start | bytes 49160 | tf_op jit(solution)/shard_map/ppermute | solution.py:711

commit v8 on v7

--- a/solution.py
+++ b/solution.py
@@ -401,24 +401,19 @@
     return sorted(others, key=lambda k: (min(k, half - k), k))
 
 
-def gather_start(
-    rank, n, here_ref, mine_ref, ranks_hbm, data_hbm, left_hbm, right_hbm, *refs
-):
-    ranks_ref, data_ref, left_ref, right_ref, back_ref, sem = refs[-6:]
+def start_left(rank, n, here_ref, mine_ref, ranks_hbm, data_hbm, left_hbm, *refs):
+    ranks_ref, data_ref, left_ref, back_ref, sem = refs[-5:]
     half = n // 2
     direct = [0] + direct_offsets(half)
-    packets, small = refs[: half - 1], refs[half - 1 : half + 1]
-    pairs = [
-        (left_hbm, left_ref), (data_hbm, data_ref), (ranks_hbm, ranks_ref),
-        (right_hbm, right_ref),
-    ]
+    packets, small, own = refs[: half - 1], refs[half - 1 : half + 1], refs[half + 1]
+    pairs = [(left_hbm, left_ref), (data_hbm, data_ref), (ranks_hbm, ranks_ref)]
     copies = [
         pltpu.make_async_copy(source, target, sem.at[k])
         for k, (source, target) in enumerate(pairs)
     ]
     for copy in copies:
         copy.start()
-    for copy in copies[:3]:
+    for copy in copies:
         copy.wait()
     width = left_ref.shape[2]
     s = data_ref.shape[2]
@@ -433,22 +428,34 @@
     gram = packed_gram(real, imag)
     for packet in packets:
         packet[0:width, :] = gram
-    copies[3].wait()
-    keep = lane_limits([ranks_ref[p, here] for p in range(n)], rank, width).astype(BF16)
-    gram = packed_gram(right_ref[0] * keep, right_ref[1] * keep)
     z, x = lax.div(here, 2), lax.rem(here, 2)
-    for packet in packets:
-        packet[width + 4 * q :, :] = gram
     for k in range(half):
         base = 2 * lax.rem(z + k, half)
         for block, target in enumerate([base + 1 - x, base + x]):
             rows = pl.ds(pl.multiple_of(target * q, q), q)
             if k == 2:
                 out, place = small[block], 0
+            elif k == 0 and block == 1:
+                out, place = own, 0
             else:
                 out, place = packets[direct.index(k)], width + 2 * q * block
             out[place : place + q, :] = back_ref[0, rows, :]
             out[place + q : place + 2 * q, :] = back_ref[1, rows, :]
+
+
+def start_right(rank, n, here_ref, ranks_hbm, right_hbm, out_ref, ranks_ref, right_ref, sem):
+    copies = [
+        pltpu.make_async_copy(right_hbm, right_ref, sem.at[0]),
+        pltpu.make_async_copy(ranks_hbm, ranks_ref, sem.at[1]),
+    ]
+    for copy in copies:
+        copy.start()
+    for copy in copies:
+        copy.wait()
+    here = here_ref[0]
+    width = right_ref.shape[2]
+    keep = lane_limits([ranks_ref[p, here] for p in range(n)], rank, width).astype(BF16)
+    out_ref[...] = packed_gram(right_ref[0] * keep, right_ref[1] * keep)
 
 
 def swap_tiles(rank, source, target):
@@ -503,9 +510,10 @@
 ):
     half = n // 2
     order = [0] + direct_offsets(half) + [2]
-    tiles = [refs[:half], refs[half:n]]
-    small = refs[n : n + 2]
-    b_ref, c_ref, stats_ref, left_ref, right_ref, one_ref, two_ref = refs[n + 2 :]
+    lefts = [refs[:half], refs[half:n]]
+    rights = [refs[n : n + half], refs[n + half : 2 * n]]
+    small, own = refs[2 * n : 2 * n + 2], refs[2 * n + 2]
+    b_ref, c_ref, stats_ref, left_ref, right_ref, one_ref, two_ref = refs[2 * n + 3 :]
     width = refs[0].shape[1]
     q = stats_ref.shape[0]
     here = here_ref[0]
@@ -513,9 +521,9 @@
     for k in range(half):
         base = 2 * lax.rem(z + half - k, half)
         for other in range(2):
-            ref = tiles[other][order.index(k)]
+            ref = lefts[other][order.index(k)]
             at = pl.ds(base + (1 - x if other else x), 1)
-            grams = (ref[0:width, :], ref[width + 4 * q :, :])
+            grams = (ref[0:width, :], rights[other][order.index(k)][...])
             for packed, gram_ref in zip(grams, (left_ref, right_ref)):
                 real, imag = unpacked_gram(packed)
                 gram_ref[0, at] = real[None]
@@ -523,6 +531,8 @@
             start = width + (0 if other else 2 * q)
             if k == 2:
                 block = small[1 - other][...]
+            elif k == 0 and not other:
+                block = own[...]
             else:
                 block = ref[start : start + 2 * q, :]
             one_ref[at] = block.astype(F32)[None]
@@ -570,7 +580,7 @@
     stats_ref[...] = block
 
 
-def mix_kernel(rank, stats_refs, b_ref, c_ref, out_ref):
+def mix_kernel(stats_refs, b_ref, c_ref, out_ref):
     blocks = [ref[...] for ref in stats_refs]
     lane = lax.broadcasted_iota(jnp.int32, blocks[0].shape, 1)
     where_f = [lane == f for f in range(len(blocks))]
@@ -599,7 +609,7 @@
             out_ref[j, place * rows : (place + 1) * rows, :] = value.astype(BF16)
 
 
-def home_mix(rank, nfreq, data_hbm, left_hbm, right_hbm, *refs):
+def home_mix(nfreq, data_hbm, left_hbm, right_hbm, *refs):
     stats_refs = refs[:nfreq]
     b_ref, c_ref, out_ref, data_ref, left_ref, right_ref, sem = refs[nfreq:]
     pairs = [(right_hbm, right_ref), (left_hbm, left_ref), (data_hbm, data_ref)]
@@ -609,7 +619,7 @@
     ]
     for copy in copies:
         copy.start()
-    mix_kernel(rank, stats_refs, b_ref, c_ref, out_ref)
+    mix_kernel(stats_refs, b_ref, c_ref, out_ref)
     for copy in copies:
         copy.wait()
 
@@ -619,7 +629,7 @@
 
 
 def home_kernel(
-    rank, recv_ref, data_ref, left_ref, right_ref, wave_hbm, res_hbm, wave_ref, res_ref, sem
+    recv_ref, data_ref, left_ref, right_ref, wave_hbm, res_hbm, wave_ref, res_ref, sem
 ):
     n, rows, width = recv_ref.shape
     q = rows // 4
@@ -672,47 +682,68 @@
         ]
 
     across = [(t, t ^ 1) for t in range(ntile)]
-    sizes = [2 * width + 4 * q] * (half - 1) + [2 * q, 2 * q]
+    sizes = [width + 2 * q] + [width + 4 * q] * (half - 2) + [2 * q] * 3
     direct = direct_offsets(half)
-    packets = call(
-        functools.partial(gather_start, rank, ntile), [SMEM] * 2 + [HBM] * 4,
-        (here, mine, ranks, data, left, right),
+    parts = call(
+        functools.partial(start_left, rank, ntile), [SMEM] * 2 + [HBM] * 3,
+        (here, mine, ranks, data, left),
         [jax.ShapeDtypeStruct((size, width), BF16) for size in sizes],
         [
             pltpu.SMEM(ranks.shape, jnp.int32),
             pltpu.VMEM(data.shape, BF16),
             pltpu.VMEM(left.shape, BF16),
+            pltpu.VMEM((2, s, width), BF16),
+            pltpu.SemaphoreType.DMA((3,)),
+        ],
+    )
+    (gram,) = call(
+        functools.partial(start_right, rank, ntile), [SMEM] + [HBM] * 2, (here, ranks, right),
+        [jax.ShapeDtypeStruct((width, width), BF16)],
+        [
+            pltpu.SMEM(ranks.shape, jnp.int32),
             pltpu.VMEM(right.shape, BF16),
-            pltpu.VMEM((2, s, width), BF16),
-            pltpu.SemaphoreType.DMA((4,)),
+            pltpu.SemaphoreType.DMA((2,)),
         ],
     )
-    same = [packets[0]] + [
-        lax.ppermute(packet, "tcol", along(k)) for packet, k in zip(packets[1:], direct)
-    ]
-    small = [lax.ppermute(packets[half - block], "tcol", along(2, block)) for block in (1, 0)]
-    first = lax.ppermute(packets[0], "tcol", across)
-    same[1], first, *small = lax.optimization_barrier((same[1], first, *small))
-    same.append(lax.ppermute(same[1], "tcol", along(1)))
-    other = [first] + [lax.ppermute(value, "tcol", across) for value in same[1:]]
+
+    def hop(value, pairs):
+        return lax.ppermute(value, "tcol", pairs)
+
+    lefts, rights = [parts[0]], [gram]
+    cross = [hop(parts[0], across), hop(gram, across)]
+    for place, k in enumerate(direct):
+        first, second = parts[1 + place], gram
+        if place:
+            first, _ = lax.optimization_barrier((first, lefts[-1]))
+            second, _ = lax.optimization_barrier((second, rights[-1]))
+        lefts.append(hop(first, along(k)))
+        rights.append(hop(second, along(k)))
+    small = [hop(parts[half - block], along(2, block)) for block in (1, 0)]
+    first, _ = lax.optimization_barrier((lefts[1][:width], lefts[-1]))
+    second, _ = lax.optimization_barrier((rights[1], rights[-1]))
+    lefts.append(hop(first, along(1)))
+    rights.append(hop(second, along(1)))
+    other_lefts, other_rights = cross[:1], cross[1:]
+    for place in range(1, half):
+        other_lefts.append(hop(lefts[place], across))
+        other_rights.append(hop(rights[place], across))
+    packets = (*lefts, *other_lefts, *rights, *other_rights, *small, parts[half + 1])
     vectors = jax.ShapeDtypeStruct((3, ntile, 2 * q, width), F32)
     grams = pltpu.VMEM((2, ntile, width, width), BF16)
     vector = pltpu.VMEM((ntile, 2 * q, width), F32)
     b, c, stats = call(
-        functools.partial(chain_kernel, rank, ntile), [SMEM] * 2 + [VMEM] * (ntile + 2),
-        (here, freq_index, *same, *other, *small),
+        functools.partial(chain_kernel, rank, ntile), [SMEM] * 2 + [VMEM] * len(packets),
+        (here, freq_index, *packets),
         (vectors, vectors, jax.ShapeDtypeStruct((q, 128), F32)),
         [grams, grams, vector, vector],
     )
-    gathered = stats[None]
-    step = 1
-    while step < nfreq:
-        pairs = [(f, f ^ step) for f in range(nfreq)]
-        gathered = jnp.concatenate([gathered, lax.ppermute(gathered, "freq", pairs)], axis=0)
-        step *= 2
+    gathered = [stats] + [
+        lax.ppermute(stats, "freq", [(f, f ^ step) for f in range(nfreq)])
+        for step in range(1, nfreq)
+    ]
     out, data_in, left_in, right_in = call(
-        functools.partial(home_mix, rank, nfreq), [HBM] * 3 + [VMEM] * (nfreq + 2),
-        (data, left, right, *[gathered[f] for f in range(nfreq)], b, c),
+        functools.partial(home_mix, nfreq), [HBM] * 3 + [VMEM] * (nfreq + 2),
+        (data, left, right, *gathered, b, c),
         (
             jax.ShapeDtypeStruct((ntile, 4 * q, width), BF16),
             like(data), like(left), like(right),
@@ -722,7 +753,7 @@
     back = lax.all_to_all(out, "tcol", 0, 0, tiled=True)
     shape = jax.ShapeDtypeStruct(data.shape, F32)
     return call(
-        functools.partial(home_kernel, rank), [VMEM] * 4, (back, data_in, left_in, right_in),
+        home_kernel, [VMEM] * 4, (back, data_in, left_in, right_in),
         (shape, shape),
         [
             pltpu.VMEM(shape.shape, F32),

time: 66.6 us -> 68.2 us (1.024)
  waiting for transfers between devices: 22.3 us -> 18.8 us
  starting transfers between devices: 20.3 us -> 23 us
  blocking collectives: 12.9 us -> 14.1 us
  Pallas kernels: 9.64 us -> 10.7 us
    ppermute x11 -> x19, waiting for transfers between devices: 22.3 us -> 18.8 us  [the longest x16 17 us: hop(): return lax.ppermute(value, 'tcol', pairs)]
    ppermute x11 -> x19, starting transfers between devices: 20.3 us -> 23 us  [the longest x16 21 us: hop(): return lax.ppermute(value, 'tcol', pairs)]
    all_to_all x1, blocking collectives: 12.9 us -> 14.1 us  [by_source(): back = lax.all_to_all(out, 'tcol', 0, 0, tiled=True)]
    pallas_call x4 -> x5, Pallas kernels: 9.64 us -> 10.7 us  [call(): pl.pallas_call(kernel, out_shape=outs, in_specs=specs, out_specs=[target]...]
  transfers between devices with their start and end apart: 11 -> 19, of which waited for: 6 -> 11; matrix products, arithmetic and copies ran while one was open for 0% -> 0% of each run, Pallas kernels for 0% -> 2%
where the time goes in v8:
time: 68.2 us; the launch traced here: 67.9 us
  starting transfers between devices  23 us (34%)
  waiting for transfers between devices  18.8 us (28%)
  blocking collectives  14.1 us (21%)
  Pallas kernels  10.7 us (16%)
  between operations  1.36 us (2%)
    ppermute x16, starting transfers between devices, hop(): return lax.ppermute(value, 'tcol', pairs)  21 us
    ppermute x16, waiting for transfers between devices, hop(): return lax.ppermute(value, 'tcol', pairs)  17 us
    all_to_all x1, blocking collectives, by_source(): back = lax.all_to_all(out, 'tcol', 0, 0, tiled=True)  14.1 us
    pallas_call x5, Pallas kernels, call(): pl.pallas_call(kernel, out_shape=outs, in_specs=specs, out_specs=[target]...  10.7 us
    ppermute x3, starting transfers between devices, by_source(): lax.ppermute(stats, 'freq', [(f, f ^ step) for f in range(nfreq)])  1.92 us
    ppermute x3, waiting for transfers between devices, by_source(): lax.ppermute(stats, 'freq', [(f, f ^ step) for f in range(nfreq)])  1.87 us
  transfers between devices with their start and end apart: 19, of which 11 were waited for; matrix products, arithmetic and copies ran while one was open for 0% of the time, Pallas kernels for 2%

profile of v8, /device:TPU:0, one launch (start us, length us, event | category | flops | bytes accessed | tf_op | source)
XLA Modules:
  0.0 67.9 jit_solution(17527521248181774212)
XLA Ops:
  0.6 1.8 %shard_map.68 = (bf16[288,256]{1,0:T(8,128)(2,1)S(1)}, bf16[320,256]{1,0:T(8,128)(2,1)S(1)}, bf16[320,256]{1,0:T(8,128)(2,1)S(1)}, bf16[32,256]{1,0:T(8,128)(2,1...) custom-call(s32[1]{0:T(128)} %bitcast.3.here_ref, s32[1]{0:T(128)} %bitcast.4.mine_ref, s32[8,8]{1,0:T(8,128)} %bitcast.14, ...), custom_call_target="tpu_custom_call" | custom-call | tf_op jit(solution)/shard_map/pallas_call | solution.py:669
  2.4 3.1 %collective-permute-start = (bf16[320,256]{1,0:T(8,128)(2,1)S(1)}, bf16[320,256]{1,0:T(8,128)(2,1)S(1)}, u32[]{:S(2)}, u32[]{:S(2)}) collective-permute-start(bf16[320,256]{1,0:T(8,128)(2,1)S(1)} %get-tuple-element.22), channel_id=1, source_target_pairs={{0,2},{1,3},{2,4},{3,5},{4,6},{5,7},{6,0},{7,1},{8,10},{9,11},{10,... | collective-permute-start | bytes 491528 | tf_op jit(solution)/shard_map/ppermute | solution.py:710
  5.5 1.5 %shard_map.69.refs_8_ = bf16[256,256]{1,0:T(8,128)(2,1)S(1)} custom-call(s32[1]{0:T(128)} %bitcast.3.here_ref, s32[8,8]{1,0:T(8,128)} %bitcast.15, bf16[2,512,256]{2,1,0:T(8,128)(2,1)} %bitcast.10), custom_call_target="tpu_custom_call" | custom-call | tf_op jit(solution)/shard_map/pallas_call | solution.py:669
  7.1 1.6 %collective-permute-start.7 = (bf16[256,256]{1,0:T(8,128)(2,1)S(1)}, bf16[256,256]{1,0:T(8,128)(2,1)S(1)}, u32[]{:S(2)}, u32[]{:S(2)}) collective-permute-start(bf16[256,256]{1,0:T(8,128)(2,1)S(1)} %shard_map.69.refs_8_), channel_id=1, source_target_pairs={{0,2},{1,3},{2,4},{3,5},{4,6},{5,7},{6,0},{7,1},{8,10},{9,11},{10,... | collective-permute-start | bytes 393224 | tf_op jit(solution)/shard_map/ppermute | solution.py:710
  8.7 3.7 %collective-permute-done.refs_1_ = bf16[320,256]{1,0:T(8,128)(2,1)S(1)} collective-permute-done((bf16[320,256]{1,0:T(8,128)(2,1)S(1)}, bf16[320,256]{1,0:T(8,128)(2,1)S(1)}, u32[]{:S(2)}, u32[]{:S(2)}) %collective-permute-start) | collective-permute-done | bytes 163872 | tf_op jit(solution)/shard_map/ppermute | solution.py:710
  12.4 2.2 %collective-permute-start.1 = (bf16[320,256]{1,0:T(8,128)(2,1)S(1)}, bf16[320,256]{1,0:T(8,128)(2,1)S(1)}, u32[]{:S(2)}, u32[]{:S(2)}) collective-permute-start(bf16[320,256]{1,0:T(8,128)(2,1)S(1)} %get-tuple-element.24), channel_id=1, source_target_pairs={{0,6},{1,7},{2,0},{3,1},{4,2},{5,3},{6,4},{7,5},{8,14},{9,15},{10,... | collective-permute-start | bytes 491528 | tf_op jit(solution)/shard_map/ppermute | solution.py:710
  15.3 1.0 %collective-permute-start.8 = (bf16[256,256]{1,0:T(8,128)(2,1)S(1)}, bf16[256,256]{1,0:T(8,128)(2,1)S(1)}, u32[]{:S(2)}, u32[]{:S(2)}) collective-permute-start(bf16[256,256]{1,0:T(8,128)(2,1)S(1)} %shard_map.69.refs_8_), channel_id=1, source_target_pairs={{0,6},{1,7},{2,0},{3,1},{4,2},{5,3},{6,4},{7,5},{8,14},{9,15},{10,... | collective-permute-start | bytes 393224 | tf_op jit(solution)/shard_map/ppermute | solution.py:710
  16.3 1.5 %collective-permute-start.3 = (bf16[288,256]{1,0:T(8,128)(2,1)S(1)}, bf16[288,256]{1,0:T(8,128)(2,1)S(1)}, u32[]{:S(2)}, u32[]{:S(2)}) collective-permute-start(bf16[288,256]{1,0:T(8,128)(2,1)S(1)} %get-tuple-element.21.refs_0_), channel_id=1, source_target_pairs={{0,1},{1,0},{2,3},{3,2},{4,5},{5,4},{6,7},{7,6},{8,9},{9,8},{10,11... | collective-permute-start | bytes 442376 | tf_op jit(solution)/shard_map/ppermute | solution.py:710
  18.8 2.1 %collective-permute-done.8.refs_10_ = bf16[256,256]{1,0:T(8,128)(2,1)S(1)} collective-permute-done((bf16[256,256]{1,0:T(8,128)(2,1)S(1)}, bf16[256,256]{1,0:T(8,128)(2,1)S(1)}, u32[]{:S(2)}, u32[]{:S(2)}) %collective-permute-start.8) | collective-permute-done | bytes 131104 | tf_op jit(solution)/shard_map/ppermute | solution.py:710
  21.0 1.2 %collective-permute-start.15 = (bf16[32,256]{1,0:T(8,128)(2,1)S(1)}, bf16[32,256]{1,0:T(8,128)(2,1)S(1)}, u32[]{:S(2)}, u32[]{:S(2)}) collective-permute-start(bf16[32,256]{1,0:T(8,128)(2,1)S(1)} %get-tuple-element.29), channel_id=1, source_target_pairs={{0,4},{1,5},{2,6},{3,7},{4,0},{5,1},{6,2},{7,3},{8,12},{9,13},{10,... | collective-permute-start | bytes 49160 | tf_op jit(solution)/shard_map/ppermute | solution.py:710
  24.0 2.7 %collective-permute-start.9 = (bf16[256,256]{1,0:T(8,128)(2,1)S(1)}, bf16[256,256]{1,0:T(8,128)(2,1)S(1)}, u32[]{:S(2)}, u32[]{:S(2)}) collective-permute-start(bf16[256,256]{1,0:T(8,128)(2,1)S(1)} %collective-permute-done.7.refs_9_), channel_id=1, source_target_pairs={{0,2},{1,3},{2,4},{3,5},{4,6},{5,7},{6,0},{7,1},{8,10},{9,11},{10,... | collective-permute-start | bytes 393224 | tf_op jit(solution)/shard_map/ppermute | solution.py:710
  26.8 1.7 %collective-permute-start.4 = (bf16[320,256]{1,0:T(8,128)(2,1)S(1)}, bf16[320,256]{1,0:T(8,128)(2,1)S(1)}, u32[]{:S(2)}, u32[]{:S(2)}) collective-permute-start(bf16[320,256]{1,0:T(8,128)(2,1)S(1)} %collective-permute-done.refs_1_), channel_id=1, source_target_pairs={{0,1},{1,0},{2,3},{3,2},{4,5},{5,4},{6,7},{7,6},{8,9},{9,8},{10,11... | collective-permute-start | bytes 491528 | tf_op jit(solution)/shard_map/ppermute | solution.py:710
  28.8 1.7 %collective-permute-start.12 = (bf16[256,256]{1,0:T(8,128)(2,1)S(1)}, bf16[256,256]{1,0:T(8,128)(2,1)S(1)}, u32[]{:S(2)}, u32[]{:S(2)}) collective-permute-start(bf16[256,256]{1,0:T(8,128)(2,1)S(1)} %collective-permute-done.8.refs_10_), channel_id=1, source_target_pairs={{0,1},{1,0},{2,3},{3,2},{4,5},{5,4},{6,7},{7,6},{8,9},{9,8},{10,11... | collective-permute-start | bytes 393224 | tf_op jit(solution)/shard_map/ppermute | solution.py:710
  31.1 1.3 %collective-permute-start.13 = (bf16[256,256]{1,0:T(8,128)(2,1)S(1)}, bf16[256,256]{1,0:T(8,128)(2,1)S(1)}, u32[]{:S(2)}, u32[]{:S(2)}) collective-permute-start(bf16[256,256]{1,0:T(8,128)(2,1)S(1)} %collective-permute-done.9.refs_11_), channel_id=1, source_target_pairs={{0,1},{1,0},{2,3},{3,2},{4,5},{5,4},{6,7},{7,6},{8,9},{9,8},{10,11... | collective-permute-start | bytes 393224 | tf_op jit(solution)/shard_map/ppermute | solution.py:710
  32.4 1.0 %collective-permute-done.2.refs_3_ = bf16[256,256]{1,0:T(8,128)(2,1)S(1)} collective-permute-done((bf16[256,256]{1,0:T(8,128)(2,1)S(1)}, bf16[256,256]{1,0:T(8,128)(2,1)S(1)}, u32[]{:S(2)}, u32[]{:S(2)}) %collective-permute-start.2) | collective-permute-done | bytes 131104 | tf_op jit(solution)/shard_map/ppermute | solution.py:710
  34.7 5.2 %collective-permute-done.12.refs_14_ = bf16[256,256]{1,0:T(8,128)(2,1)S(1)} collective-permute-done((bf16[256,256]{1,0:T(8,128)(2,1)S(1)}, bf16[256,256]{1,0:T(8,128)(2,1)S(1)}, u32[]{:S(2)}, u32[]{:S(2)}) %collective-permute-start.12) | collective-permute-done | bytes 131104 | tf_op jit(solution)/shard_map/ppermute | solution.py:710
  39.9 1.4 %collective-permute-done.13.refs_15_ = bf16[256,256]{1,0:T(8,128)(2,1)S(1)} collective-permute-done((bf16[256,256]{1,0:T(8,128)(2,1)S(1)}, bf16[256,256]{1,0:T(8,128)(2,1)S(1)}, u32[]{:S(2)}, u32[]{:S(2)}) %collective-permute-start.13) | collective-permute-done | bytes 131104 | tf_op jit(solution)/shard_map/ppermute | solution.py:710
  41.3 1.4 %collective-permute-done.6.refs_7_ = bf16[256,256]{1,0:T(8,128)(2,1)S(1)} collective-permute-done((bf16[256,256]{1,0:T(8,128)(2,1)S(1)}, bf16[256,256]{1,0:T(8,128)(2,1)S(1)}, u32[]{:S(2)}, u32[]{:S(2)}) %collective-permute-start.6) | collective-permute-done | bytes 131104 | tf_op jit(solution)/shard_map/ppermute | solution.py:710
  42.7 4.7 %shard_map.70 = (f32[3,8,32,256]{3,2,1,0:T(8,128)S(1)}, f32[3,8,32,256]{3,2,1,0:T(8,128)S(1)}, f32[16,128]{1,0:T(8,128)S(1)}) custom-call(s32[1]{0:T(128)} %bitcast.3.here_ref, s32[1]{0:T(128)S(6)} %copy.7.freq_ref, bf16[288,256]{1,0:T(8,128)(2,1)S(1)} %get-tuple-element.21.refs_0_, bf16[320,256]{1,0:T(8,128)(2,1)S(1)} %collective-permute-done.refs_1_, ...), custom_call_target="tpu_custom_call" | custom-call | tf_op jit(solution)/shard_map/pallas_call | solution.py:669
  47.5 1.6 %collective-permute-start.17 = (f32[16,128]{1,0:T(8,128)S(1)}, f32[16,128]{1,0:T(8,128)S(1)}, u32[]{:S(2)}, u32[]{:S(2)}) collective-permute-start(f32[16,128]{1,0:T(8,128)S(1)} %get-tuple-element.31.refs_0_), channel_id=1, source_target_pairs={{0,16},{8,24},{16,0},{24,8},{1,17},{9,25},{17,1},{25,9},{2,18},{10... | collective-permute-start | bytes 24584 | tf_op jit(solution)/shard_map/ppermute | solution.py:741
  49.4 1.2 %collective-permute-done.18.refs_3_ = f32[16,128]{1,0:T(8,128)S(1)} collective-permute-done((f32[16,128]{1,0:T(8,128)S(1)}, f32[16,128]{1,0:T(8,128)S(1)}, u32[]{:S(2)}, u32[]{:S(2)}) %collective-permute-start.18) | collective-permute-done | bytes 8224 | tf_op jit(solution)/shard_map/ppermute | solution.py:741
  51.2 1.3 %shard_map.71 = (bf16[8,64,256]{2,1,0:T(8,128)(2,1)S(1)}, bf16[2,512,128]{2,1,0:T(8,128)(2,1)S(1)}, bf16[2,512,256]{2,1,0:T(8,128)(2,1)S(1)}, bf16[2,512,256]{2,1,0:T(8,128)(2,1)S(1)}) custom-call(bf16[2,512,128]{2,1,0:T(8,128)(2,1)} %bitcast.13, bf16[2,512,256]{2,1,0:T(8,128)(2,1)} %bitcast.9, bf16[2,512,256]{2,1,0:T(8,128)(2,1)} %bitcast.11, ...), custom_call_target="tpu_custom_call" | custom-call | tf_op jit(solution)/shard_map/pallas_call | solution.py:669
  52.5 14.1 %all_to_all.5.recv_ref = bf16[8,64,256]{2,1,0:T(8,128)(2,1)S(1)} all-to-all(bf16[8,64,256]{2,1,0:T(8,128)(2,1)S(1)} %get-tuple-element.34), channel_id=1, replica_groups=mesh['freq'=4,'tcol'=8] {'tcol'}, dimensions={0} | all-to-all | bytes 524288 | tf_op jit(solution)/shard_map/all_to_all | solution.py:753
  66.6 1.3 %shard_map.72 = (f32[2,512,128]{2,1,0:T(8,128)}, f32[2,512,128]{2,1,0:T(8,128)}) custom-call(bf16[8,64,256]{2,1,0:T(8,128)(2,1)S(1)} %all_to_all.5.recv_ref, bf16[2,512,128]{2,1,0:T(8,128)(2,1)S(1)} %get-tuple-element.35.data_ref, bf16[2,512,256]{2,1,0:T(8,128)(2,1)S(1)} %get-tuple-element.36.left_ref, bf16[2,512,256]{2,1,0:T(8,128)(2,1)S(1)} %get-tuple-element.37.right_ref), custom_call_target="tpu_custom_call" | custom-call | tf_op jit(solution)/shard_map/pallas_call | solution.py:669
  (21 shorter events, 6.3 us)
Async XLA Ops:
  2.4 10.0 %collective-permute-start = (bf16[320,256]{1,0:T(8,128)(2,1)S(1)}, bf16[320,256]{1,0:T(8,128)(2,1)S(1)}, u32[]{:S(2)}, u32[]{:S(2)}) collective-permute-start(bf16[320,256]{1,0:T(8,128)(2,1)S(1)} %get-tuple-element.22), channel_id=1, source_target_pairs={{0,2},{1,3},{2,4},{3,5},{4,6},{5,7},{6,0},{7,1},{8,10},{9,11},{10,... | collective-permute-start | bytes 491528 | tf_op jit(solution)/shard_map/ppermute | solution.py:710
  7.1 8.2 %collective-permute-start.7 = (bf16[256,256]{1,0:T(8,128)(2,1)S(1)}, bf16[256,256]{1,0:T(8,128)(2,1)S(1)}, u32[]{:S(2)}, u32[]{:S(2)}) collective-permute-start(bf16[256,256]{1,0:T(8,128)(2,1)S(1)} %shard_map.69.refs_8_), channel_id=1, source_target_pairs={{0,2},{1,3},{2,4},{3,5},{4,6},{5,7},{6,0},{7,1},{8,10},{9,11},{10,... | collective-permute-start | bytes 393224 | tf_op jit(solution)/shard_map/ppermute | solution.py:710
  12.4 9.8 %collective-permute-start.1 = (bf16[320,256]{1,0:T(8,128)(2,1)S(1)}, bf16[320,256]{1,0:T(8,128)(2,1)S(1)}, u32[]{:S(2)}, u32[]{:S(2)}) collective-permute-start(bf16[320,256]{1,0:T(8,128)(2,1)S(1)} %get-tuple-element.24), channel_id=1, source_target_pairs={{0,6},{1,7},{2,0},{3,1},{4,2},{5,3},{6,4},{7,5},{8,14},{9,15},{10,... | collective-permute-start | bytes 491528 | tf_op jit(solution)/shard_map/ppermute | solution.py:710
  15.3 5.7 %collective-permute-start.8 = (bf16[256,256]{1,0:T(8,128)(2,1)S(1)}, bf16[256,256]{1,0:T(8,128)(2,1)S(1)}, u32[]{:S(2)}, u32[]{:S(2)}) collective-permute-start(bf16[256,256]{1,0:T(8,128)(2,1)S(1)} %shard_map.69.refs_8_), channel_id=1, source_target_pairs={{0,6},{1,7},{2,0},{3,1},{4,2},{5,3},{6,4},{7,5},{8,14},{9,15},{10,... | collective-permute-start | bytes 393224 | tf_op jit(solution)/shard_map/ppermute | solution.py:710
  16.3 12.1 %collective-permute-start.3 = (bf16[288,256]{1,0:T(8,128)(2,1)S(1)}, bf16[288,256]{1,0:T(8,128)(2,1)S(1)}, u32[]{:S(2)}, u32[]{:S(2)}) collective-permute-start(bf16[288,256]{1,0:T(8,128)(2,1)S(1)} %get-tuple-element.21.refs_0_), channel_id=1, source_target_pairs={{0,1},{1,0},{2,3},{3,2},{4,5},{5,4},{6,7},{7,6},{8,9},{9,8},{10,11... | collective-permute-start | bytes 442376 | tf_op jit(solution)/shard_map/ppermute | solution.py:710
  17.8 9.0 %collective-permute-start.10 = (bf16[256,256]{1,0:T(8,128)(2,1)S(1)}, bf16[256,256]{1,0:T(8,128)(2,1)S(1)}, u32[]{:S(2)}, u32[]{:S(2)}) collective-permute-start(bf16[256,256]{1,0:T(8,128)(2,1)S(1)} %shard_map.69.refs_8_), channel_id=1, source_target_pairs={{0,1},{1,0},{2,3},{3,2},{4,5},{5,4},{6,7},{7,6},{8,9},{9,8},{10,11... | collective-permute-start | bytes 393224 | tf_op jit(solution)/shard_map/ppermute | solution.py:710
  18.3 5.6 %collective-permute-start.14 = (bf16[32,256]{1,0:T(8,128)(2,1)S(1)}, bf16[32,256]{1,0:T(8,128)(2,1)S(1)}, u32[]{:S(2)}, u32[]{:S(2)}) collective-permute-start(bf16[32,256]{1,0:T(8,128)(2,1)S(1)} %get-tuple-element.28), channel_id=1, source_target_pairs={{0,5},{1,4},{2,7},{3,6},{4,1},{5,0},{6,3},{7,2},{8,13},{9,12},{10,... | collective-permute-start | bytes 49160 | tf_op jit(solution)/shard_map/ppermute | solution.py:710
  21.0 5.7 %collective-permute-start.15 = (bf16[32,256]{1,0:T(8,128)(2,1)S(1)}, bf16[32,256]{1,0:T(8,128)(2,1)S(1)}, u32[]{:S(2)}, u32[]{:S(2)}) collective-permute-start(bf16[32,256]{1,0:T(8,128)(2,1)S(1)} %get-tuple-element.29), channel_id=1, source_target_pairs={{0,4},{1,5},{2,6},{3,7},{4,0},{5,1},{6,2},{7,3},{8,12},{9,13},{10,... | collective-permute-start | bytes 49160 | tf_op jit(solution)/shard_map/ppermute | solution.py:710
  22.2 6.6 %collective-permute-start.11 = (bf16[256,256]{1,0:T(8,128)(2,1)S(1)}, bf16[256,256]{1,0:T(8,128)(2,1)S(1)}, u32[]{:S(2)}, u32[]{:S(2)}) collective-permute-start(bf16[256,256]{1,0:T(8,128)(2,1)S(1)} %collective-permute-done.7.refs_9_), channel_id=1, source_target_pairs={{0,1},{1,0},{2,3},{3,2},{4,5},{5,4},{6,7},{7,6},{8,9},{9,8},{10,11... | collective-permute-start | bytes 393224 | tf_op jit(solution)/shard_map/ppermute | solution.py:710
  24.0 7.1 %collective-permute-start.9 = (bf16[256,256]{1,0:T(8,128)(2,1)S(1)}, bf16[256,256]{1,0:T(8,128)(2,1)S(1)}, u32[]{:S(2)}, u32[]{:S(2)}) collective-permute-start(bf16[256,256]{1,0:T(8,128)(2,1)S(1)} %collective-permute-done.7.refs_9_), channel_id=1, source_target_pairs={{0,2},{1,3},{2,4},{3,5},{4,6},{5,7},{6,0},{7,1},{8,10},{9,11},{10,... | collective-permute-start | bytes 393224 | tf_op jit(solution)/shard_map/ppermute | solution.py:710
  26.6 6.8 %collective-permute-start.2 = (bf16[256,256]{1,0:T(8,128)(2,1)S(1)}, bf16[256,256]{1,0:T(8,128)(2,1)S(1)}, u32[]{:S(2)}, u32[]{:S(2)}) collective-permute-start(bf16[256,256]{1,0:T(8,128)(2,1)S(1)} %slice.4), channel_id=1, source_target_pairs={{0,2},{1,3},{2,4},{3,5},{4,6},{5,7},{6,0},{7,1},{8,10},{9,11},{10,... | collective-permute-start | bytes 393224 | tf_op jit(solution)/shard_map/ppermute | solution.py:710
  26.8 7.9 %collective-permute-start.4 = (bf16[320,256]{1,0:T(8,128)(2,1)S(1)}, bf16[320,256]{1,0:T(8,128)(2,1)S(1)}, u32[]{:S(2)}, u32[]{:S(2)}) collective-permute-start(bf16[320,256]{1,0:T(8,128)(2,1)S(1)} %collective-permute-done.refs_1_), channel_id=1, source_target_pairs={{0,1},{1,0},{2,3},{3,2},{4,5},{5,4},{6,7},{7,6},{8,9},{9,8},{10,11... | collective-permute-start | bytes 491528 | tf_op jit(solution)/shard_map/ppermute | solution.py:710
  28.4 11.4 %collective-permute-start.5 = (bf16[320,256]{1,0:T(8,128)(2,1)S(1)}, bf16[320,256]{1,0:T(8,128)(2,1)S(1)}, u32[]{:S(2)}, u32[]{:S(2)}) collective-permute-start(bf16[320,256]{1,0:T(8,128)(2,1)S(1)} %collective-permute-done.1.refs_2_), channel_id=1, source_target_pairs={{0,1},{1,0},{2,3},{3,2},{4,5},{5,4},{6,7},{7,6},{8,9},{9,8},{10,11... | collective-permute-start | bytes 491528 | tf_op jit(solution)/shard_map/ppermute | solution.py:710
  28.8 11.0 %collective-permute-start.12 = (bf16[256,256]{1,0:T(8,128)(2,1)S(1)}, bf16[256,256]{1,0:T(8,128)(2,1)S(1)}, u32[]{:S(2)}, u32[]{:S(2)}) collective-permute-start(bf16[256,256]{1,0:T(8,128)(2,1)S(1)} %collective-permute-done.8.refs_10_), channel_id=1, source_target_pairs={{0,1},{1,0},{2,3},{3,2},{4,5},{5,4},{6,7},{7,6},{8,9},{9,8},{10,11... | collective-permute-start | bytes 393224 | tf_op jit(solution)/shard_map/ppermute | solution.py:710
  31.1 10.2 %collective-permute-start.13 = (bf16[256,256]{1,0:T(8,128)(2,1)S(1)}, bf16[256,256]{1,0:T(8,128)(2,1)S(1)}, u32[]{:S(2)}, u32[]{:S(2)}) collective-permute-start(bf16[256,256]{1,0:T(8,128)(2,1)S(1)} %collective-permute-done.9.refs_11_), channel_id=1, source_target_pairs={{0,1},{1,0},{2,3},{3,2},{4,5},{5,4},{6,7},{7,6},{8,9},{9,8},{10,11... | collective-permute-start | bytes 393224 | tf_op jit(solution)/shard_map/ppermute | solution.py:710
  33.4 9.3 %collective-permute-start.6 = (bf16[256,256]{1,0:T(8,128)(2,1)S(1)}, bf16[256,256]{1,0:T(8,128)(2,1)S(1)}, u32[]{:S(2)}, u32[]{:S(2)}) collective-permute-start(bf16[256,256]{1,0:T(8,128)(2,1)S(1)} %collective-permute-done.2.refs_3_), channel_id=1, source_target_pairs={{0,1},{1,0},{2,3},{3,2},{4,5},{5,4},{6,7},{7,6},{8,9},{9,8},{10,11... | collective-permute-start | bytes 393224 | tf_op jit(solution)/shard_map/ppermute | solution.py:710
  47.4 3.1 %collective-permute-start.18 = (f32[16,128]{1,0:T(8,128)S(1)}, f32[16,128]{1,0:T(8,128)S(1)}, u32[]{:S(2)}, u32[]{:S(2)}) collective-permute-start(f32[16,128]{1,0:T(8,128)S(1)} %get-tuple-element.31.refs_0_), channel_id=1, source_target_pairs={{0,24},{8,16},{16,8},{24,0},{1,25},{9,17},{17,9},{25,1},{2,26},{10... | collective-permute-start | bytes 24584 | tf_op jit(solution)/shard_map/ppermute | solution.py:741
  47.5 3.7 %collective-permute-start.17 = (f32[16,128]{1,0:T(8,128)S(1)}, f32[16,128]{1,0:T(8,128)S(1)}, u32[]{:S(2)}, u32[]{:S(2)}) collective-permute-start(f32[16,128]{1,0:T(8,128)S(1)} %get-tuple-element.31.refs_0_), channel_id=1, source_target_pairs={{0,16},{8,24},{16,0},{24,8},{1,17},{9,25},{17,1},{25,9},{2,18},{10... | collective-permute-start | bytes 24584 | tf_op jit(solution)/shard_map/ppermute | solution.py:741
  49.1 2.1 %collective-permute-start.16 = (f32[16,128]{1,0:T(8,128)S(1)}, f32[16,128]{1,0:T(8,128)S(1)}, u32[]{:S(2)}, u32[]{:S(2)}) collective-permute-start(f32[16,128]{1,0:T(8,128)S(1)} %get-tuple-element.31.refs_0_), channel_id=1, source_target_pairs={{0,8},{8,0},{16,24},{24,16},{1,9},{9,1},{17,25},{25,17},{2,10},{10... | collective-permute-start | bytes 24584 | tf_op jit(solution)/shard_map/ppermute | solution.py:741
